TPU v7x, 32 devices: a whole 2x2x4 slice. The times are simulated.
32 devices in a mesh: pole: 2 (over y), row: 4 (over x, core), col: 4 (over z).
Axes of the slice: x: 2, y: 2, z: 4, core: 2. Of those that a mesh axis runs over, the one named last changes fastest.
Arguments:
- inverse_blocks: float32 [4096, 2048], P(('pole', 'row'), 'col'), parts along dimension 0, may hold values from -6 to 6
- lower_panel: float32 [4096, 512], P(('pole', 'row'), 'col'), parts along dimension 0, may hold values from -0.125 to 0.125
- struct_mask: int32 [16, 4], P('row', 'col'), may hold values 0 or 1
- diag_inverse: float32 [1024, 128], P(('pole', 'col')), parts along dimension 0, may hold values from -6 to 6
Outputs:
- g_panel: float32 [4096, 512], P(('pole', 'row'), 'col'), parts along dimension 0
- g_diag: float32 [1024, 128], P(('pole', 'col')), parts along dimension 0
There are 2 independent parts, one for each index of `pole`. A program takes and returns all parts, laid end to end along the dimension named above; an argument that names none is the same for every part. Nothing has to cross between parts.
All inputs are finite; a program needn't handle non-finite values. No bound on the sum of `struct_mask` on one device may be relied on, other than what follows from the above.
Results may differ from a plain program's by a relative error of at most 0.000071.
Values sent between devices are 32-bit elements; how exact they have to be, the bound alone decides.
No kernel may reach another device: no remote copies, remote signals or barrier semaphores. Data moves between devices by JAX's collectives and lax.ppermute only.
A program may use at most 64 MiB of HBM per device.

v0:
```python
import jax
import jax.numpy as jnp
from jax import lax
from jax.sharding import PartitionSpec as P


def from_root(x, axis, root):
    mine = lax.axis_index(axis) == root
    return lax.psum(jnp.where(mine, x, jnp.zeros_like(x)), axis)


def on_device(inverse_blocks, lower_panel, struct_mask, diag_inverse):
    width = diag_inverse.shape[1]
    local_rows = lower_panel.shape[0]
    local_cols = lower_panel.shape[1]
    supers = local_cols // width
    expanded = jnp.repeat(jnp.repeat(struct_mask, width, axis=0), width, axis=1).astype(jnp.float32)
    masked = lower_panel * expanded
    panel_row = lax.all_gather(masked, "col", axis=1, tiled=True)
    mirrored = from_root(panel_row, "row", lax.axis_index("col"))
    summed = lax.psum_scatter(
        lax.dot_general(
            mirrored,
            inverse_blocks,
            (((0,), (1,)), ((), ())),
            precision=lax.Precision.HIGHEST,
            preferred_element_type=jnp.float32,
        ),
        "col",
        scatter_dimension=0,
        tiled=True,
    )
    g_panel = -summed.T * expanded
    masked_three = masked.reshape(local_rows, supers, width)
    panel_three = g_panel.reshape(local_rows, supers, width)
    quad_part = -jnp.einsum(
        "jka,jkb->kab", masked_three, panel_three, precision=lax.Precision.HIGHEST
    )
    quad_total = lax.psum(quad_part, "row")
    g_diag = diag_inverse + quad_total.reshape(supers * width, width)
    return (g_panel, g_diag)


def solution(mesh):
    placed = (
        P(("pole", "row"), "col"),
        P(("pole", "row"), "col"),
        P("row", "col"),
        P(("pole", "col"), None),
    )
    return jax.shard_map(
        on_device,
        mesh=mesh,
        in_specs=placed,
        out_specs=(P(("pole", "row"), "col"), P(("pole", "col"), None)),
        check_vma=False,
    )
```

profile of v0, /device:TPU:0, one launch (start us, length us, event | category | flops | bytes accessed | tf_op | source)
XLA Modules:
  0.0 153.8 jit_solution(16746672606810595600)
XLA Ops:
  7.2 0.0 copy-start
  7.2 0.0 all-gather.2.cloned.1.call-start
  7.2 0.7 convert_bitcast_fusion
  8.0 0.1 broadcast_bitcast_fusion
  8.0 1.8 %broadcast_multiply_fusion = f32[512,128]{1,0:T(8,128)} fusion(f32[512,128]{1,0:T(8,128)} %param.5, f32[512]{0:T(512)S(1)} %broadcast_bitcast_fusion), kind=kLoop, calls=%fused_computation.5 | loop fusion | flops 65536 | bytes 526336 | tf_op jit(solution)/shard_map/mul | solution.py:18
  9.8 0.0 all-gather.2.cloned.1.call-update
  9.8 0.0 all-reduce.3.cloned.1.call-start
  9.9 33.2 %all-gather.2.cloned.1.call-done = f32[512,512]{1,0:T(8,128)} async-done(((f32[512,128]{1,0:T(8,128)}), f32[512,512]{1,0:T(8,128)}) %all-gather.2.cloned.1.call-update) | async-done | bytes 1048592 | tf_op jit(solution)/shard_map/all_gather | solution.py:19
  43.1 2.3 %broadcast_select_fusion = f32[512,512]{1,0:T(8,128)} fusion(f32[512,512]{1,0:T(8,128)} %all-gather.2.cloned.1.call-done, pred[]{:T(512)S(6)} %eq.3), kind=kLoop, calls=%fused_computation.1 | loop fusion | flops 262144 | bytes 2097153 | tf_op jit(solution)/shard_map/jit(_where)/select_n | solution.py:9
  45.4 0.0 all-reduce.3.cloned.1.call-update
  45.4 0.0 reduce-scatter.2.cloned.1.call-start
  45.5 34.4 %all-reduce.3.cloned.1.call-done = f32[512,512]{1,0:T(8,128)} async-done(((f32[512,512]{1,0:T(8,128)}), f32[512,512]{1,0:T(8,128)}) %all-reduce.3.cloned.1.call-update) | async-done | bytes 1048592 | tf_op jit(solution)/shard_map/psum | solution.py:9
  79.9 0.0 copy-done
  79.9 5.7 %fusion.2 = f32[512,512]{1,0:T(8,128)} fusion(f32[512,512]{1,0:T(8,128)} %all-reduce.3.cloned.1.call-done, f32[512,512]{1,0:T(8,128)S(1)} %copy-done), kind=kOutput, calls=%fused_computation.8 | convolution fusion | flops 1610612736 | bytes 3145728 | tf_op jit(solution)/shard_map/dot_general | solution.py:22
  85.6 0.0 copy-start.1
  85.6 0.0 reduce-scatter.2.cloned.1.call-update
  85.7 0.0 all-reduce.5.cloned.1.call-start
  85.7 27.6 %reduce-scatter.2.cloned.1.call-done = f32[128,512]{1,0:T(8,128)} async-done(((f32[512,512]{1,0:T(8,128)}), f32[128,512]{1,0:T(8,128)}) %reduce-scatter.2.cloned.1.call-update) | async-done | bytes 262160 | tf_op jit(solution)/shard_map/reduce_scatter | solution.py:21
  113.3 0.0 copy-done.1
  113.4 0.0 copy-start.2
  113.4 2.3 %convolution_negate_fusion = f32[128,128]{1,0:T(8,128)} fusion(f32[128,512]{1,0:T(8,128)} %reduce-scatter.2.cloned.1.call-done, f32[512]{0:T(512)S(1)} %broadcast_bitcast_fusion, f32[512,128]{1,0:T(8,128)S(1)} %copy-done.1), kind=kOutput, calls=%fused_computation | convolution fusion | flops 100876288 | bytes 591872 | tf_op jit(solution)/shard_map/jka,jkb->kab/dot_general | solution.py:36
  115.7 0.0 all-reduce.5.cloned.1.call-update
  115.7 0.0 copy-done.2
  115.8 0.0 copy-start.3
  115.8 0.8 copy.6
  116.6 29.2 %all-reduce.5.cloned.1.call-done = f32[128,128]{1,0:T(8,128)} async-done(((f32[128,128]{1,0:T(8,128)}), f32[128,128]{1,0:T(8,128)}) %all-reduce.5.cloned.1.call-update) | async-done | bytes 65552 | tf_op jit(solution)/shard_map/psum | solution.py:39
  145.8 0.0 copy-done.3
  145.8 1.5 add.9
  (1 shorter events, 0.0 us)
Async XLA Ops:
  7.2 72.7 %copy-start = (f32[512,512]{1,0:T(8,128)S(1)}, f32[512,512]{1,0:T(8,128)}, u32[]{:S(2)}) copy-start(f32[512,512]{1,0:T(8,128)} %param.4) | copy-start | bytes 3145732
  7.2 35.9 %all-gather.2.cloned.1.call-start = ((), (), s32[]{:S(2)}) async-start(), calls=%async_computation.1 | async-start | bytes 1310720 | tf_op jit(solution)/shard_map/all_gather | solution.py:19
  9.8 70.1 %all-reduce.3.cloned.1.call-start = ((), (), s32[]{:S(2)}) async-start(), calls=%async_computation.2 | async-start | bytes 2097152 | tf_op jit(solution)/shard_map/psum | solution.py:9
  45.4 67.9 %reduce-scatter.2.cloned.1.call-start = ((), (), s32[]{:S(2)}) async-start(), calls=%async_computation.3 | async-start | bytes 1310720 | tf_op jit(solution)/shard_map/reduce_scatter | solution.py:21
  85.6 27.7 %copy-start.1 = (f32[512,128]{1,0:T(8,128)S(1)}, f32[512,128]{1,0:T(8,128)}, u32[]{:S(2)}) copy-start(f32[512,128]{1,0:T(8,128)} %param.5) | copy-start | bytes 786436
  85.7 60.2 %all-reduce.5.cloned.1.call-start = ((), (), s32[]{:S(2)}) async-start(), calls=%async_computation.4 | async-start | bytes 131072 | tf_op jit(solution)/shard_map/psum | solution.py:39
  113.4 2.4 %copy-start.2 = (f32[128,512]{1,0:T(8,128)S(1)}, f32[128,512]{1,0:T(8,128)}, u32[]{:S(2)}) copy-start(f32[128,512]{1,0:T(8,128)} %reduce-scatter.2.cloned.1.call-done) | copy-start | bytes 786436
  115.8 30.1 %copy-start.3 = (f32[128,128]{1,0:T(8,128)S(1)}, f32[128,128]{1,0:T(8,128)}, u32[]{:S(2)}) copy-start(f32[128,128]{1,0:T(8,128)} %param.7) | copy-start | bytes 196612
Sparse Core Ops, SparseCore 0:
  10.1 32.8 all-gather.1
  45.6 34.2 all-reduce.2
  85.8 27.5 reduce-scatter.1
  116.1 29.6 all-reduce.4
where the time goes:
time: 154 us
  waiting for transfers between devices  124 us (81%)
  between operations  13.8 us (9%)
  matrix products  8.07 us (5%)
  other arithmetic  6.37 us (4%)
    psum x1, waiting for transfers between devices, from_root(): return lax.psum(jnp.where(mine, x, jnp.zeros_like(x)), axis)  34.4 us
    all_gather x1, waiting for transfers between devices, on_device(): panel_row = lax.all_gather(masked, 'col', axis=1, tiled=True)  33.2 us
    psum x1, waiting for transfers between devices, on_device(): quad_total = lax.psum(quad_part, 'row')  29.2 us
    reduce_scatter x1, waiting for transfers between devices, on_device(): lax.psum_scatter(lax.dot_general(mirrored, inverse_blocks, (((0,), (1,)),...  27.6 us
    dot_general x1, matrix products, on_device(): lax.dot_general(mirrored, inverse_blocks, (((0,), (1,)), ((), ())), preci...  5.73 us
  transfers between devices with their start and end apart: 4, of which 4 were waited for; matrix products, arithmetic and copies ran while one was open for 1% of the time, Pallas kernels for 0%

commit v1 on v0

v1 whole, which is shorter than its diff:
```python
import functools

import jax
import jax.numpy as jnp
from jax import lax
from jax.experimental import pallas as pl
from jax.experimental.pallas import tpu as pltpu
from jax.sharding import PartitionSpec as P

GRID = ("row", "col")
VMEM = pl.BlockSpec(memory_space=pltpu.VMEM)
SMEM = pl.BlockSpec(memory_space=pltpu.SMEM)
LIMIT = pltpu.CompilerParams(vmem_limit_bytes=40 * 1024 * 1024)


def split(x):
    high = x.astype(jnp.bfloat16)
    return high, (x - high.astype(jnp.float32)).astype(jnp.bfloat16)


def dot(a, b, dims):
    return lax.dot_general(a, b, (dims, ((), ())), preferred_element_type=jnp.float32)


def masking(mask_ref, panel_ref, out_ref):
    blocks, supers = mask_ref.shape
    tall, wide = panel_ref.shape[0] // blocks, panel_ref.shape[1] // supers
    for b in range(blocks):
        for s in range(supers):
            at = (slice(b * tall, (b + 1) * tall), slice(s * wide, (s + 1) * wide))
            out_ref[at] = panel_ref[at] * mask_ref[b, s].astype(jnp.float32)


def products(count, shift_ref, a_ref, *refs):
    panels, outs = refs[:count], refs[count:]
    ah, al = split(a_ref[...])
    shift = shift_ref[0]
    for i in range(count):
        m = panels[0][...]
        for j in range(1, count):
            m = jnp.where(shift == (i ^ j), panels[j][...], m)
        mh, ml = split(m)
        both = jnp.concatenate([mh, ml], axis=1)
        width = m.shape[1]
        first = dot(ah, both, ((1,), (0,)))
        outs[i][...] = first[:, :width] + (first[:, width:] + dot(al, mh, ((1,), (0,))))


def finish(count, width, mask_ref, masked_ref, *refs):
    parts, g_ref, quad_ref = refs[:count], refs[count], refs[count + 1]
    total = parts[0][...]
    for part in parts[1:]:
        total = total + part[...]
    blocks, supers = mask_ref.shape
    tall = total.shape[0] // blocks
    for b in range(blocks):
        for s in range(supers):
            at = (slice(b * tall, (b + 1) * tall), slice(s * width, (s + 1) * width))
            g_ref[at] = total[at] * -mask_ref[b, s].astype(jnp.float32)
    for s in range(supers):
        cols = slice(s * width, (s + 1) * width)
        mh, ml = split(masked_ref[:, cols])
        gh, gl = split(g_ref[:, cols])
        rows = ((0,), (0,))
        quad_ref[cols, :] = -(dot(mh, gh, rows) + (dot(mh, gl, rows) + dot(ml, gh, rows)))


def on_device(side, inverse_blocks, lower_panel, struct_mask, diag_inverse):
    width = diag_inverse.shape[1]
    rows, cols = lower_panel.shape
    f32 = jnp.float32
    row, col = lax.axis_index("row"), lax.axis_index("col")

    def swap(x, axis, bit):
        return lax.ppermute(x, axis, [(i, i ^ bit) for i in range(side)])

    masked = pl.pallas_call(
        masking,
        out_shape=jax.ShapeDtypeStruct((rows, cols), f32),
        in_specs=[SMEM, VMEM],
        out_specs=VMEM,
        name="masking",
    )(struct_mask, lower_panel)

    turned = lax.ppermute(
        masked, GRID, [(r * side + c, c * side + r) for r in range(side) for c in range(side)]
    )
    panels = {0: turned}
    bit = side // 2
    while bit:
        for j, x in list(panels.items()):
            panels[j ^ bit] = swap(x, "row", bit)
        bit //= 2

    shift = jnp.bitwise_xor(row, col).astype(jnp.int32).reshape(1)
    partials = pl.pallas_call(
        functools.partial(products, side),
        out_shape=[jax.ShapeDtypeStruct((rows, cols), f32)] * side,
        in_specs=[SMEM] + [VMEM] * (1 + side),
        out_specs=[VMEM] * side,
        compiler_params=LIMIT,
        name="products",
    )(shift, inverse_blocks, *[panels[j] for j in range(side)])

    arrived = [partials[0]] + [swap(partials[i], "col", i) for i in range(1, side)]

    g_panel, quad = pl.pallas_call(
        functools.partial(finish, side, width),
        out_shape=[
            jax.ShapeDtypeStruct((rows, cols), f32),
            jax.ShapeDtypeStruct((cols, width), f32),
        ],
        in_specs=[SMEM] + [VMEM] * (1 + side),
        out_specs=[VMEM, VMEM],
        compiler_params=LIMIT,
        name="finish",
    )(struct_mask, masked, *arrived)

    bit = 1
    while bit < side:
        quad = quad + swap(quad, "row", bit)
        bit *= 2
    return g_panel, diag_inverse + quad


def solution(mesh):
    side = mesh.shape["row"]
    assert side == mesh.shape["col"] and side & (side - 1) == 0
    placed = (
        P(("pole", "row"), "col"),
        P(("pole", "row"), "col"),
        P("row", "col"),
        P(("pole", "col"), None),
    )
    return jax.shard_map(
        functools.partial(on_device, side),
        mesh=mesh,
        in_specs=placed,
        out_specs=(P(("pole", "row"), "col"), P(("pole", "col"), None)),
        check_vma=False,
    )
```

time: 154 us -> 66.2 us (0.43)
  the two profiles are of different devices: /device:TPU:0 before, /device:TPU:20 now
where the time goes in v1:
time: 66.2 us; the launch traced here: 65.9 us
  waiting for transfers between devices  49.5 us (75%)
  starting transfers between devices  8.29 us (13%)
  Pallas kernels  4.3 us (6%)
  local copies, waits for them, and re-layouts  2.55 us (4%)
  between operations  0.68 us (1%)
    ppermute x8, waiting for transfers between devices, swap(): return lax.ppermute(x, axis, [(i, i ^ bit) for i in range(side)])  37.3 us
    ppermute x1, waiting for transfers between devices, on_device(): lax.ppermute(masked, GRID, [(r * side + c, c * side + r) for r in range(s...  12.2 us
    ppermute x8, starting transfers between devices, swap(): return lax.ppermute(x, axis, [(i, i ^ bit) for i in range(side)])  5.13 us
    ppermute x1, starting transfers between devices, on_device(): lax.ppermute(masked, GRID, [(r * side + c, c * side + r) for r in range(s...  3.16 us
    unnamed x9, local copies, waits for them, and re-layouts  2.55 us
    pallas_call x1, Pallas kernels, on_device(): pl.pallas_call(masking, out_shape=jax.ShapeDtypeStruct((rows, cols), f32)...  1.68 us
    pallas_call x1, Pallas kernels, on_device(): pl.pallas_call(functools.partial(finish, side, width), out_shape=[jax.Sha...  1.35 us
  transfers between devices with their start and end apart: 9, of which 8 were waited for; matrix products, arithmetic and copies ran while one was open for 0% of the time, Pallas kernels for 0%

profile of v1, /device:TPU:20, one launch (start us, length us, event | category | flops | bytes accessed | tf_op | source)
XLA Modules:
  0.0 65.9 jit_solution(15300934593529490204)
XLA Ops:
  0.6 1.3 %copy.7.mask_ref = s32[4,1]{1,0:T(4,128)} copy(s32[4,1]{0,1:T(1,128)} %param.6) | data formatting | bytes 32 | tf_op args[2]
  1.9 1.7 %masking.1.masked_ref = f32[512,128]{1,0:T(8,128)} custom-call(s32[4,1]{1,0:T(4,128)} %copy.7.mask_ref, f32[512,128]{1,0:T(8,128)} %panel_ref.1), custom_call_target="tpu_custom_call" | custom-call | tf_op jit(solution)/shard_map/masking/pallas_call | solution.py:77
  3.6 3.2 %collective-permute-start = (f32[512,128]{1,0:T(8,128)}, f32[512,128]{1,0:T(8,128)S(1)}, u32[]{:S(2)}, u32[]{:S(2)}) collective-permute-start(f32[512,128]{1,0:T(8,128)} %masking.1.masked_ref), channel_id=1, source_target_pairs={{0,0},{1,4},{2,8},{3,12},{4,1},{5,5},{6,9},{7,13},{8,2},{9,6},{10,... | collective-permute-start | bytes 786440 | tf_op jit(solution)/shard_map/ppermute | solution.py:85
  6.8 12.2 %collective-permute-done.refs_0_ = f32[512,128]{1,0:T(8,128)S(1)} collective-permute-done((f32[512,128]{1,0:T(8,128)}, f32[512,128]{1,0:T(8,128)S(1)}, u32[]{:S(2)}, u32[]{:S(2)}) %collective-permute-start) | collective-permute-done | bytes 262176 | tf_op jit(solution)/shard_map/ppermute | solution.py:85
  18.9 0.0 collective-permute-start.2
  18.9 1.4 %collective-permute-start.1 = (f32[512,128]{1,0:T(8,128)S(1)}, f32[512,128]{1,0:T(8,128)S(1)}, u32[]{:S(2)}, u32[]{:S(2)}) collective-permute-start(f32[512,128]{1,0:T(8,128)S(1)} %collective-permute-done.refs_0_), channel_id=1, source_target_pairs={{0,4},{4,0},{8,12},{12,8},{1,5},{5,1},{9,13},{13,9},{2,6},{6,2},{1... | collective-permute-start | bytes 786440 | tf_op jit(solution)/shard_map/ppermute | solution.py:75
  20.3 7.5 %collective-permute-done.2.refs_2_ = f32[512,128]{1,0:T(8,128)S(1)} collective-permute-done((f32[512,128]{1,0:T(8,128)S(1)}, f32[512,128]{1,0:T(8,128)S(1)}, u32[]{:S(2)}, u32[]{:S(2)}) %collective-permute-start.2) | collective-permute-done | bytes 262176 | tf_op jit(solution)/shard_map/ppermute | solution.py:75
  27.8 0.1 collective-permute-start.3
  27.9 0.0 collective-permute-done.1.refs_1_
  27.9 1.4 %collective-permute-done.3.refs_3_ = f32[512,128]{1,0:T(8,128)S(1)} collective-permute-done((f32[512,128]{1,0:T(8,128)S(1)}, f32[512,128]{1,0:T(8,128)S(1)}, u32[]{:S(2)}, u32[]{:S(2)}) %collective-permute-start.3) | collective-permute-done | bytes 262176 | tf_op jit(solution)/shard_map/ppermute | solution.py:75
  29.3 0.0 copy-start
  29.3 1.2 %copy-done = f32[512,512]{1,0:T(8,128)S(1)} copy-done((f32[512,512]{1,0:T(8,128)S(1)}, f32[512,512]{1,0:T(8,128)}, u32[]{:S(2)}) %copy-start) | copy-done | bytes 1048600
  30.6 0.0 copy-start.1
  30.6 1.3 %products.1 = (f32[512,128]{1,0:T(8,128)S(1)}, f32[512,128]{1,0:T(8,128)S(1)}, f32[512,128]{1,0:T(8,128)S(1)}, f32[512,128]{1,0:T(8,128)S(1)}) custom-call(s32[1]{0:T(128)} %bitcast.shift_ref, f32[512,512]{1,0:T(8,128)S(1)} %copy-done, f32[512,128]{1,0:T(8,128)S(1)} %collective-permute-done.refs_0_, f32[512,128]{1,0:T(8,128)S(1)} %collective-permute-done.1.refs_1_, ...), custom_call_target="tpu_custom_call" | custom-call | tf_op jit(solution)/shard_map/products/pallas_call | solution.py:96
  31.8 0.1 collective-permute-start.4
  31.9 0.0 copy-start.2
  31.9 1.3 %collective-permute-start.5 = (f32[512,128]{1,0:T(8,128)S(1)}, f32[512,128]{1,0:T(8,128)S(1)}, u32[]{:S(2)}, u32[]{:S(2)}) collective-permute-start(f32[512,128]{1,0:T(8,128)S(1)} %get-tuple-element.10), channel_id=1, source_target_pairs={{0,2},{1,3},{2,0},{3,1},{4,6},{5,7},{6,4},{7,5},{8,10},{9,11},{10,... | collective-permute-start | bytes 786440 | tf_op jit(solution)/shard_map/ppermute | solution.py:75
  33.2 2.2 %collective-permute-start.6 = (f32[512,128]{1,0:T(8,128)S(1)}, f32[512,128]{1,0:T(8,128)S(1)}, u32[]{:S(2)}, u32[]{:S(2)}) collective-permute-start(f32[512,128]{1,0:T(8,128)S(1)} %get-tuple-element.11), channel_id=1, source_target_pairs={{0,3},{1,2},{2,1},{3,0},{4,7},{5,6},{6,5},{7,4},{8,11},{9,10},{10,... | collective-permute-start | bytes 786440 | tf_op jit(solution)/shard_map/ppermute | solution.py:75
  35.4 6.4 %collective-permute-done.4.refs_1_ = f32[512,128]{1,0:T(8,128)S(1)} collective-permute-done((f32[512,128]{1,0:T(8,128)S(1)}, f32[512,128]{1,0:T(8,128)S(1)}, u32[]{:S(2)}, u32[]{:S(2)}) %collective-permute-start.4) | collective-permute-done | bytes 262176 | tf_op jit(solution)/shard_map/ppermute | solution.py:75
  41.8 9.2 %collective-permute-done.5.refs_2_ = f32[512,128]{1,0:T(8,128)S(1)} collective-permute-done((f32[512,128]{1,0:T(8,128)S(1)}, f32[512,128]{1,0:T(8,128)S(1)}, u32[]{:S(2)}, u32[]{:S(2)}) %collective-permute-start.5) | collective-permute-done | bytes 262176 | tf_op jit(solution)/shard_map/ppermute | solution.py:75
  51.0 7.3 %collective-permute-done.6.refs_3_ = f32[512,128]{1,0:T(8,128)S(1)} collective-permute-done((f32[512,128]{1,0:T(8,128)S(1)}, f32[512,128]{1,0:T(8,128)S(1)}, u32[]{:S(2)}, u32[]{:S(2)}) %collective-permute-start.6) | collective-permute-done | bytes 262176 | tf_op jit(solution)/shard_map/ppermute | solution.py:75
  58.3 0.0 copy-done.1
  58.3 0.0 copy-done.2
  58.3 1.3 %finish.1 = (f32[512,128]{1,0:T(8,128)}, f32[128,128]{1,0:T(8,128)S(1)}) custom-call(s32[4,1]{1,0:T(4,128)S(1)} %copy-done.2, f32[512,128]{1,0:T(8,128)S(1)} %copy-done.1, f32[512,128]{1,0:T(8,128)S(1)} %get-tuple-element.8.refs_0_, f32[512,128]{1,0:T(8,128)S(1)} %collective-permute-done.4.refs_1_, f32[512,128]{1,0:T(8,128)S(1)} %collective-permute-done.5.refs_2_, ...), custom_call_target="tpu_custom_call" | custom-call | tf_op jit(solution)/shard_map/finish/pallas_call | solution.py:107
  59.7 0.0 copy-start.3
  59.7 0.0 collective-permute-start.7
  59.7 1.3 %collective-permute-done.7 = f32[128,128]{1,0:T(8,128)S(1)} collective-permute-done((f32[128,128]{1,0:T(8,128)S(1)}, f32[128,128]{1,0:T(8,128)S(1)}, u32[]{:S(2)}, u32[]{:S(2)}) %collective-permute-start.7) | collective-permute-done | bytes 65568 | tf_op jit(solution)/shard_map/ppermute | solution.py:75
  61.0 0.1 collective-permute-start.8
  61.0 4.3 %collective-permute-done.8 = f32[128,128]{1,0:T(8,128)S(1)} collective-permute-done((f32[128,128]{1,0:T(8,128)S(1)}, f32[128,128]{1,0:T(8,128)S(1)}, u32[]{:S(2)}, u32[]{:S(2)}) %collective-permute-start.8) | collective-permute-done | bytes 65568 | tf_op jit(solution)/shard_map/ppermute | solution.py:75
  65.3 0.0 copy-done.3
  65.3 0.6 add_add_fusion
  (1 shorter events, 0.0 us)
Async XLA Ops:
  3.6 15.3 %collective-permute-start = (f32[512,128]{1,0:T(8,128)}, f32[512,128]{1,0:T(8,128)S(1)}, u32[]{:S(2)}, u32[]{:S(2)}) collective-permute-start(f32[512,128]{1,0:T(8,128)} %masking.1.masked_ref), channel_id=1, source_target_pairs={{0,0},{1,4},{2,8},{3,12},{4,1},{5,5},{6,9},{7,13},{8,2},{9,6},{10,... | collective-permute-start | bytes 786440 | tf_op jit(solution)/shard_map/ppermute | solution.py:85
  18.9 8.9 %collective-permute-start.2 = (f32[512,128]{1,0:T(8,128)S(1)}, f32[512,128]{1,0:T(8,128)S(1)}, u32[]{:S(2)}, u32[]{:S(2)}) collective-permute-start(f32[512,128]{1,0:T(8,128)S(1)} %collective-permute-done.refs_0_), channel_id=1, source_target_pairs={{0,8},{4,12},{8,0},{12,4},{1,9},{5,13},{9,1},{13,5},{2,10},{6,14},... | collective-permute-start | bytes 786440 | tf_op jit(solution)/shard_map/ppermute | solution.py:75
  18.9 9.0 %collective-permute-start.1 = (f32[512,128]{1,0:T(8,128)S(1)}, f32[512,128]{1,0:T(8,128)S(1)}, u32[]{:S(2)}, u32[]{:S(2)}) collective-permute-start(f32[512,128]{1,0:T(8,128)S(1)} %collective-permute-done.refs_0_), channel_id=1, source_target_pairs={{0,4},{4,0},{8,12},{12,8},{1,5},{5,1},{9,13},{13,9},{2,6},{6,2},{1... | collective-permute-start | bytes 786440 | tf_op jit(solution)/shard_map/ppermute | solution.py:75
  27.8 1.5 %collective-permute-start.3 = (f32[512,128]{1,0:T(8,128)S(1)}, f32[512,128]{1,0:T(8,128)S(1)}, u32[]{:S(2)}, u32[]{:S(2)}) collective-permute-start(f32[512,128]{1,0:T(8,128)S(1)} %collective-permute-done.2.refs_2_), channel_id=1, source_target_pairs={{0,4},{4,0},{8,12},{12,8},{1,5},{5,1},{9,13},{13,9},{2,6},{6,2},{1... | collective-permute-start | bytes 786440 | tf_op jit(solution)/shard_map/ppermute | solution.py:75
  29.3 1.2 %copy-start = (f32[512,512]{1,0:T(8,128)S(1)}, f32[512,512]{1,0:T(8,128)}, u32[]{:S(2)}) copy-start(f32[512,512]{1,0:T(8,128)} %a_ref.1) | copy-start | bytes 3145732
  30.6 27.8 %copy-start.1 = (f32[512,128]{1,0:T(8,128)S(1)}, f32[512,128]{1,0:T(8,128)}, u32[]{:S(2)}) copy-start(f32[512,128]{1,0:T(8,128)} %masking.1.masked_ref) | copy-start | bytes 786436
  31.8 10.0 %collective-permute-start.4 = (f32[512,128]{1,0:T(8,128)S(1)}, f32[512,128]{1,0:T(8,128)S(1)}, u32[]{:S(2)}, u32[]{:S(2)}) collective-permute-start(f32[512,128]{1,0:T(8,128)S(1)} %get-tuple-element.9), channel_id=1, source_target_pairs={{0,1},{1,0},{2,3},{3,2},{4,5},{5,4},{6,7},{7,6},{8,9},{9,8},{10,11... | collective-permute-start | bytes 786440 | tf_op jit(solution)/shard_map/ppermute | solution.py:75
  31.9 26.4 %copy-start.2 = (s32[4,1]{1,0:T(4,128)S(1)}, s32[4,1]{1,0:T(4,128)}, u32[]{:S(2)}) copy-start(s32[4,1]{1,0:T(4,128)} %copy.7.mask_ref) | copy-start | bytes 52
  31.9 19.1 %collective-permute-start.5 = (f32[512,128]{1,0:T(8,128)S(1)}, f32[512,128]{1,0:T(8,128)S(1)}, u32[]{:S(2)}, u32[]{:S(2)}) collective-permute-start(f32[512,128]{1,0:T(8,128)S(1)} %get-tuple-element.10), channel_id=1, source_target_pairs={{0,2},{1,3},{2,0},{3,1},{4,6},{5,7},{6,4},{7,5},{8,10},{9,11},{10,... | collective-permute-start | bytes 786440 | tf_op jit(solution)/shard_map/ppermute | solution.py:75
  33.2 25.1 %collective-permute-start.6 = (f32[512,128]{1,0:T(8,128)S(1)}, f32[512,128]{1,0:T(8,128)S(1)}, u32[]{:S(2)}, u32[]{:S(2)}) collective-permute-start(f32[512,128]{1,0:T(8,128)S(1)} %get-tuple-element.11), channel_id=1, source_target_pairs={{0,3},{1,2},{2,1},{3,0},{4,7},{5,6},{6,5},{7,4},{8,11},{9,10},{10,... | collective-permute-start | bytes 786440 | tf_op jit(solution)/shard_map/ppermute | solution.py:75
  59.7 5.6 %copy-start.3 = (f32[128,128]{1,0:T(8,128)S(1)}, f32[128,128]{1,0:T(8,128)}, u32[]{:S(2)}) copy-start(f32[128,128]{1,0:T(8,128)} %param.7) | copy-start | bytes 196612
  59.7 1.3 %collective-permute-start.7 = (f32[128,128]{1,0:T(8,128)S(1)}, f32[128,128]{1,0:T(8,128)S(1)}, u32[]{:S(2)}, u32[]{:S(2)}) collective-permute-start(f32[128,128]{1,0:T(8,128)S(1)} %get-tuple-element.13), channel_id=1, source_target_pairs={{0,4},{4,0},{8,12},{12,8},{1,5},{5,1},{9,13},{13,9},{2,6},{6,2},{1... | collective-permute-start | bytes 196616 | tf_op jit(solution)/shard_map/ppermute | solution.py:75
  61.0 4.3 %collective-permute-start.8 = (f32[128,128]{1,0:T(8,128)S(1)}, f32[128,128]{1,0:T(8,128)S(1)}, u32[]{:S(2)}, u32[]{:S(2)}) collective-permute-start(f32[128,128]{1,0:T(8,128)S(1)} %add.9), channel_id=1, source_target_pairs={{0,8},{4,12},{8,0},{12,4},{1,9},{5,13},{9,1},{13,5},{2,10},{6,14},... | collective-permute-start | bytes 196616 | tf_op jit(solution)/shard_map/ppermute | solution.py:75

commit v2 on v1

--- a/solution.py
+++ b/solution.py
@@ -23,17 +23,21 @@
 
 
 def masking(mask_ref, panel_ref, out_ref):
-    blocks, supers = mask_ref.shape
+    supers, blocks = mask_ref.shape
     tall, wide = panel_ref.shape[0] // blocks, panel_ref.shape[1] // supers
     for b in range(blocks):
         for s in range(supers):
             at = (slice(b * tall, (b + 1) * tall), slice(s * wide, (s + 1) * wide))
-            out_ref[at] = panel_ref[at] * mask_ref[b, s].astype(jnp.float32)
+            out_ref[at] = panel_ref[at] * mask_ref[s, b].astype(jnp.float32)
 
 
-def products(count, shift_ref, a_ref, *refs):
+def splitting(a_ref, high_ref, low_ref):
+    high_ref[...], low_ref[...] = split(a_ref[...])
+
+
+def products(count, shift_ref, high_ref, low_ref, *refs):
     panels, outs = refs[:count], refs[count:]
-    ah, al = split(a_ref[...])
+    ah, al = high_ref[...], low_ref[...]
     shift = shift_ref[0]
     for i in range(count):
         m = panels[0][...]
@@ -51,12 +55,12 @@
     total = parts[0][...]
     for part in parts[1:]:
         total = total + part[...]
-    blocks, supers = mask_ref.shape
+    supers, blocks = mask_ref.shape
     tall = total.shape[0] // blocks
     for b in range(blocks):
         for s in range(supers):
             at = (slice(b * tall, (b + 1) * tall), slice(s * width, (s + 1) * width))
-            g_ref[at] = total[at] * -mask_ref[b, s].astype(jnp.float32)
+            g_ref[at] = total[at] * -mask_ref[s, b].astype(jnp.float32)
     for s in range(supers):
         cols = slice(s * width, (s + 1) * width)
         mh, ml = split(masked_ref[:, cols])
@@ -74,17 +78,26 @@
     def swap(x, axis, bit):
         return lax.ppermute(x, axis, [(i, i ^ bit) for i in range(side)])
 
+    mask = struct_mask.T
     masked = pl.pallas_call(
         masking,
         out_shape=jax.ShapeDtypeStruct((rows, cols), f32),
         in_specs=[SMEM, VMEM],
         out_specs=VMEM,
         name="masking",
-    )(struct_mask, lower_panel)
+    )(mask, lower_panel)
+    halves = pl.pallas_call(
+        splitting,
+        out_shape=[jax.ShapeDtypeStruct(inverse_blocks.shape, jnp.bfloat16)] * 2,
+        in_specs=[VMEM],
+        out_specs=[VMEM, VMEM],
+        name="splitting",
+    )(inverse_blocks)
 
     turned = lax.ppermute(
         masked, GRID, [(r * side + c, c * side + r) for r in range(side) for c in range(side)]
     )
+    turned, *halves = lax.optimization_barrier((turned, *halves))
     panels = {0: turned}
     bit = side // 2
     while bit:
@@ -96,25 +109,32 @@
     partials = pl.pallas_call(
         functools.partial(products, side),
         out_shape=[jax.ShapeDtypeStruct((rows, cols), f32)] * side,
-        in_specs=[SMEM] + [VMEM] * (1 + side),
+        in_specs=[SMEM] + [VMEM] * (2 + side),
         out_specs=[VMEM] * side,
         compiler_params=LIMIT,
         name="products",
-    )(shift, inverse_blocks, *[panels[j] for j in range(side)])
+    )(shift, *halves, *[panels[j] for j in range(side)])
 
-    arrived = [partials[0]] + [swap(partials[i], "col", i) for i in range(1, side)]
+    if side == 4:
+        relayed = lax.ppermute(partials[3], "col", [(0, 1), (3, 2)])
+        inner = lax.ppermute(partials[3], "col", [(1, 2), (2, 1)])
+        near = swap(partials[1], "col", 1)
+        far = swap(partials[2] + relayed, "col", 2)
+        arrived = [partials[0], near, inner, far]
+    else:
+        arrived = [partials[0]] + [swap(partials[i], "col", i) for i in range(1, side)]
 
     g_panel, quad = pl.pallas_call(
-        functools.partial(finish, side, width),
+        functools.partial(finish, len(arrived), width),
         out_shape=[
             jax.ShapeDtypeStruct((rows, cols), f32),
             jax.ShapeDtypeStruct((cols, width), f32),
         ],
-        in_specs=[SMEM] + [VMEM] * (1 + side),
+        in_specs=[SMEM] + [VMEM] * (1 + len(arrived)),
         out_specs=[VMEM, VMEM],
         compiler_params=LIMIT,
         name="finish",
-    )(struct_mask, masked, *arrived)
+    )(mask, masked, *arrived)
 
     bit = 1
     while bit < side:

time: 66.2 us -> 65.1 us (0.983)
  the two profiles are of different devices: /device:TPU:20 before, /device:TPU:0 now
where the time goes in v2:
time: 65.1 us; the launch traced here: 64.8 us
  starting transfers between devices  30.2 us (46%)
  waiting for transfers between devices  24.5 us (38%)
  Pallas kernels  6.55 us (10%)
  local copies, waits for them, and re-layouts  2.1 us (3%)
  other arithmetic  0.68 us (1%)
  between operations  0.68 us (1%)
    ppermute x7, starting transfers between devices, swap(): return lax.ppermute(x, axis, [(i, i ^ bit) for i in range(side)])  25.1 us
    ppermute x7, waiting for transfers between devices, swap(): return lax.ppermute(x, axis, [(i, i ^ bit) for i in range(side)])  21.4 us
    ppermute x1, waiting for transfers between devices, on_device(): relayed = lax.ppermute(partials[3], 'col', [(0, 1), (3, 2)])  3.1 us
    ppermute x1, starting transfers between devices, on_device(): relayed = lax.ppermute(partials[3], 'col', [(0, 1), (3, 2)])  2.9 us
    pallas_call x1, Pallas kernels, on_device(): pl.pallas_call(splitting, out_shape=[jax.ShapeDtypeStruct(inverse_blocks....  2.28 us
    unnamed x10, local copies, waits for them, and re-layouts  2.1 us
    pallas_call x1, Pallas kernels, on_device(): pl.pallas_call(masking, out_shape=jax.ShapeDtypeStruct((rows, cols), f32)...  1.69 us
    ppermute x1, starting transfers between devices, on_device(): lax.ppermute(masked, GRID, [(r * side + c, c * side + r) for r in range(s...  1.6 us
  transfers between devices with their start and end apart: 10, of which 7 were waited for; matrix products, arithmetic and copies ran while one was open for 0% of the time, Pallas kernels for 4%

profile of v2, /device:TPU:0, one launch (start us, length us, event | category | flops | bytes accessed | tf_op | source)
XLA Modules:
  0.0 64.8 jit_solution(1236741619484227886)
XLA Ops:
  0.6 1.7 %masking.1.masked_ref = f32[512,128]{1,0:T(8,128)} custom-call(s32[1,4]{1,0:T(1,128)} %bitcast.2, f32[512,128]{1,0:T(8,128)} %panel_ref.1), custom_call_target="tpu_custom_call" | custom-call | tf_op jit(solution)/shard_map/masking/pallas_call | solution.py:82
  2.3 1.6 %collective-permute-start = (f32[512,128]{1,0:T(8,128)}, f32[512,128]{1,0:T(8,128)S(1)}, u32[]{:S(2)}, u32[]{:S(2)}) collective-permute-start(f32[512,128]{1,0:T(8,128)} %masking.1.masked_ref), channel_id=1, source_target_pairs={{0,0},{1,4},{2,8},{3,12},{4,1},{5,5},{6,9},{7,13},{8,2},{9,6},{10,... | collective-permute-start | bytes 786440 | tf_op jit(solution)/shard_map/ppermute | solution.py:97
  3.9 2.3 %splitting.1 = (bf16[512,512]{1,0:T(8,128)(2,1)}, bf16[512,512]{1,0:T(8,128)(2,1)}) custom-call(f32[512,512]{1,0:T(8,128)} %a_ref.1), custom_call_target="tpu_custom_call" | custom-call | tf_op jit(solution)/shard_map/splitting/pallas_call | solution.py:89
  6.2 0.0 collective-permute-done.refs_0_
  6.2 17.4 %collective-permute-start.2 = (f32[512,128]{1,0:T(8,128)S(1)}, f32[512,128]{1,0:T(8,128)S(1)}, u32[]{:S(2)}, u32[]{:S(2)}) collective-permute-start(f32[512,128]{1,0:T(8,128)S(1)} %collective-permute-done.refs_0_), channel_id=1, source_target_pairs={{0,8},{4,12},{8,0},{12,4},{1,9},{5,13},{9,1},{13,5},{2,10},{6,14},... | collective-permute-start | bytes 786440 | tf_op jit(solution)/shard_map/ppermute | solution.py:79
  23.6 0.0 collective-permute-start.1
  23.6 4.3 %collective-permute-done.2.refs_2_ = f32[512,128]{1,0:T(8,128)S(1)} collective-permute-done((f32[512,128]{1,0:T(8,128)S(1)}, f32[512,128]{1,0:T(8,128)S(1)}, u32[]{:S(2)}, u32[]{:S(2)}) %collective-permute-start.2) | collective-permute-done | bytes 262176 | tf_op jit(solution)/shard_map/ppermute | solution.py:79
  27.9 0.0 collective-permute-start.3
  27.9 0.0 collective-permute-done.1.refs_1_
  27.9 1.5 %collective-permute-done.3.refs_3_ = f32[512,128]{1,0:T(8,128)S(1)} collective-permute-done((f32[512,128]{1,0:T(8,128)S(1)}, f32[512,128]{1,0:T(8,128)S(1)}, u32[]{:S(2)}, u32[]{:S(2)}) %collective-permute-start.3) | collective-permute-done | bytes 262176 | tf_op jit(solution)/shard_map/ppermute | solution.py:79
  29.5 1.0 %copy-done.1 = bf16[512,512]{1,0:T(8,128)(2,1)S(1)} copy-done((bf16[512,512]{1,0:T(8,128)(2,1)S(1)}, bf16[512,512]{1,0:T(8,128)(2,1)}, u32[]{:S(2)}) %copy-start.1) | copy-done | bytes 524312
  30.5 0.0 copy-start.2
  30.5 1.0 %copy-done.2 = bf16[512,512]{1,0:T(8,128)(2,1)S(1)} copy-done((bf16[512,512]{1,0:T(8,128)(2,1)S(1)}, bf16[512,512]{1,0:T(8,128)(2,1)}, u32[]{:S(2)}) %copy-start.2) | copy-done | bytes 524312
  31.6 1.3 %products.1 = (f32[512,128]{1,0:T(8,128)S(1)}, f32[512,128]{1,0:T(8,128)S(1)}, f32[512,128]{1,0:T(8,128)S(1)}, f32[512,128]{1,0:T(8,128)S(1)}) custom-call(s32[1]{0:T(128)} %bitcast.1.shift_ref, bf16[512,512]{1,0:T(8,128)(2,1)S(1)} %copy-done.1, bf16[512,512]{1,0:T(8,128)(2,1)S(1)} %copy-done.2, f32[512,128]{1,0:T(8,128)S(1)} %collective-permute-done.refs_0_, ...), custom_call_target="tpu_custom_call" | custom-call | tf_op jit(solution)/shard_map/products/pallas_call | solution.py:109
  32.8 2.9 %collective-permute-start.6 = (f32[512,128]{1,0:T(8,128)S(1)}, f32[512,128]{1,0:T(8,128)S(1)}, u32[]{:S(2)}, u32[]{:S(2)}) collective-permute-start(f32[512,128]{1,0:T(8,128)S(1)} %get-tuple-element.20), channel_id=1, source_target_pairs={{0,1},{3,2},{4,5},{7,6},{8,9},{11,10},{12,13},{15,14},{16,17},{19,... | collective-permute-start | bytes 786440 | tf_op jit(solution)/shard_map/ppermute | solution.py:119
  35.7 0.7 %collective-permute-start.5 = (f32[512,128]{1,0:T(8,128)S(1)}, f32[512,128]{1,0:T(8,128)S(1)}, u32[]{:S(2)}, u32[]{:S(2)}) collective-permute-start(f32[512,128]{1,0:T(8,128)S(1)} %get-tuple-element.20), channel_id=1, source_target_pairs={{1,2},{2,1},{5,6},{6,5},{9,10},{10,9},{13,14},{14,13},{17,18},{18,... | collective-permute-start | bytes 786440 | tf_op jit(solution)/shard_map/ppermute | solution.py:120
  36.4 2.8 %collective-permute-start.4 = (f32[512,128]{1,0:T(8,128)S(1)}, f32[512,128]{1,0:T(8,128)S(1)}, u32[]{:S(2)}, u32[]{:S(2)}) collective-permute-start(f32[512,128]{1,0:T(8,128)S(1)} %get-tuple-element.19), channel_id=1, source_target_pairs={{0,1},{1,0},{2,3},{3,2},{4,5},{5,4},{6,7},{7,6},{8,9},{9,8},{10,11... | collective-permute-start | bytes 786440 | tf_op jit(solution)/shard_map/ppermute | solution.py:79
  39.3 3.1 %collective-permute-done.6 = f32[512,128]{1,0:T(8,128)S(1)} collective-permute-done((f32[512,128]{1,0:T(8,128)S(1)}, f32[512,128]{1,0:T(8,128)S(1)}, u32[]{:S(2)}, u32[]{:S(2)}) %collective-permute-start.6) | collective-permute-done | bytes 262176 | tf_op jit(solution)/shard_map/ppermute | solution.py:119
  42.4 0.0 copy-start.3
  42.4 4.2 %collective-permute-start.7 = (f32[512,128]{1,0:T(8,128)S(1)}, f32[512,128]{1,0:T(8,128)S(1)}, u32[]{:S(2)}, u32[]{:S(2)}) collective-permute-start(f32[512,128]{1,0:T(8,128)S(1)} %add.12), channel_id=1, source_target_pairs={{0,2},{1,3},{2,0},{3,1},{4,6},{5,7},{6,4},{7,5},{8,10},{9,11},{10,... | collective-permute-start | bytes 786440 | tf_op jit(solution)/shard_map/ppermute | solution.py:79
  46.6 1.4 %collective-permute-done.4.refs_1_ = f32[512,128]{1,0:T(8,128)S(1)} collective-permute-done((f32[512,128]{1,0:T(8,128)S(1)}, f32[512,128]{1,0:T(8,128)S(1)}, u32[]{:S(2)}, u32[]{:S(2)}) %collective-permute-start.4) | collective-permute-done | bytes 262176 | tf_op jit(solution)/shard_map/ppermute | solution.py:79
  48.0 0.0 collective-permute-done.5.refs_2_
  48.0 9.2 %collective-permute-done.7.refs_3_ = f32[512,128]{1,0:T(8,128)S(1)} collective-permute-done((f32[512,128]{1,0:T(8,128)S(1)}, f32[512,128]{1,0:T(8,128)S(1)}, u32[]{:S(2)}, u32[]{:S(2)}) %collective-permute-start.7) | collective-permute-done | bytes 262176 | tf_op jit(solution)/shard_map/ppermute | solution.py:79
  57.2 0.0 copy-done
  57.2 0.0 copy-done.3
  57.2 1.3 %finish.1 = (f32[512,128]{1,0:T(8,128)}, f32[128,128]{1,0:T(8,128)S(1)}) custom-call(s32[1,4]{1,0:T(1,128)S(1)} %bitcast.3, f32[512,128]{1,0:T(8,128)S(1)} %copy-done, f32[512,128]{1,0:T(8,128)S(1)} %get-tuple-element.18.refs_0_, f32[512,128]{1,0:T(8,128)S(1)} %collective-permute-done.4.refs_1_, f32[512,128]{1,0:T(8,128)S(1)} %collective-permute-done.5.refs_2_, ...), custom_call_target="tpu_custom_call" | custom-call | tf_op jit(solution)/shard_map/finish/pallas_call | solution.py:127
  58.5 0.0 collective-permute-start.8
  58.5 1.3 %collective-permute-done.8 = f32[128,128]{1,0:T(8,128)S(1)} collective-permute-done((f32[128,128]{1,0:T(8,128)S(1)}, f32[128,128]{1,0:T(8,128)S(1)}, u32[]{:S(2)}, u32[]{:S(2)}) %collective-permute-start.8) | collective-permute-done | bytes 65568 | tf_op jit(solution)/shard_map/ppermute | solution.py:79
  59.8 0.7 %collective-permute-start.9 = (f32[128,128]{1,0:T(8,128)S(1)}, f32[128,128]{1,0:T(8,128)S(1)}, u32[]{:S(2)}, u32[]{:S(2)}) collective-permute-start(f32[128,128]{1,0:T(8,128)S(1)} %add.13), channel_id=1, source_target_pairs={{0,8},{4,12},{8,0},{12,4},{1,9},{5,13},{9,1},{13,5},{2,10},{6,14},... | collective-permute-start | bytes 196616 | tf_op jit(solution)/shard_map/ppermute | solution.py:79
  60.4 3.7 %collective-permute-done.9 = f32[128,128]{1,0:T(8,128)S(1)} collective-permute-done((f32[128,128]{1,0:T(8,128)S(1)}, f32[128,128]{1,0:T(8,128)S(1)}, u32[]{:S(2)}, u32[]{:S(2)}) %collective-permute-start.9) | collective-permute-done | bytes 65568 | tf_op jit(solution)/shard_map/ppermute | solution.py:79
  64.1 0.0 copy-done.4
  64.1 0.6 add_add_fusion
  (5 shorter events, 0.0 us)
Async XLA Ops:
  2.3 3.9 %collective-permute-start = (f32[512,128]{1,0:T(8,128)}, f32[512,128]{1,0:T(8,128)S(1)}, u32[]{:S(2)}, u32[]{:S(2)}) collective-permute-start(f32[512,128]{1,0:T(8,128)} %masking.1.masked_ref), channel_id=1, source_target_pairs={{0,0},{1,4},{2,8},{3,12},{4,1},{5,5},{6,9},{7,13},{8,2},{9,6},{10,... | collective-permute-start | bytes 786440 | tf_op jit(solution)/shard_map/ppermute | solution.py:97
  6.2 21.7 %collective-permute-start.2 = (f32[512,128]{1,0:T(8,128)S(1)}, f32[512,128]{1,0:T(8,128)S(1)}, u32[]{:S(2)}, u32[]{:S(2)}) collective-permute-start(f32[512,128]{1,0:T(8,128)S(1)} %collective-permute-done.refs_0_), channel_id=1, source_target_pairs={{0,8},{4,12},{8,0},{12,4},{1,9},{5,13},{9,1},{13,5},{2,10},{6,14},... | collective-permute-start | bytes 786440 | tf_op jit(solution)/shard_map/ppermute | solution.py:79
  23.6 4.4 %collective-permute-start.1 = (f32[512,128]{1,0:T(8,128)S(1)}, f32[512,128]{1,0:T(8,128)S(1)}, u32[]{:S(2)}, u32[]{:S(2)}) collective-permute-start(f32[512,128]{1,0:T(8,128)S(1)} %collective-permute-done.refs_0_), channel_id=1, source_target_pairs={{0,4},{4,0},{8,12},{12,8},{1,5},{5,1},{9,13},{13,9},{2,6},{6,2},{1... | collective-permute-start | bytes 786440 | tf_op jit(solution)/shard_map/ppermute | solution.py:79
  27.9 1.5 %collective-permute-start.3 = (f32[512,128]{1,0:T(8,128)S(1)}, f32[512,128]{1,0:T(8,128)S(1)}, u32[]{:S(2)}, u32[]{:S(2)}) collective-permute-start(f32[512,128]{1,0:T(8,128)S(1)} %collective-permute-done.2.refs_2_), channel_id=1, source_target_pairs={{0,4},{4,0},{8,12},{12,8},{1,5},{5,1},{9,13},{13,9},{2,6},{6,2},{1... | collective-permute-start | bytes 786440 | tf_op jit(solution)/shard_map/ppermute | solution.py:79
  29.5 1.0 %copy-start.1 = (bf16[512,512]{1,0:T(8,128)(2,1)S(1)}, bf16[512,512]{1,0:T(8,128)(2,1)}, u32[]{:S(2)}) copy-start(bf16[512,512]{1,0:T(8,128)(2,1)} %get-tuple-element.15.high_ref) | copy-start | bytes 1572868
  30.5 1.0 %copy-start.2 = (bf16[512,512]{1,0:T(8,128)(2,1)S(1)}, bf16[512,512]{1,0:T(8,128)(2,1)}, u32[]{:S(2)}) copy-start(bf16[512,512]{1,0:T(8,128)(2,1)} %get-tuple-element.16.low_ref) | copy-start | bytes 1572868
  32.8 9.5 %collective-permute-start.6 = (f32[512,128]{1,0:T(8,128)S(1)}, f32[512,128]{1,0:T(8,128)S(1)}, u32[]{:S(2)}, u32[]{:S(2)}) collective-permute-start(f32[512,128]{1,0:T(8,128)S(1)} %get-tuple-element.20), channel_id=1, source_target_pairs={{0,1},{3,2},{4,5},{7,6},{8,9},{11,10},{12,13},{15,14},{16,17},{19,... | collective-permute-start | bytes 786440 | tf_op jit(solution)/shard_map/ppermute | solution.py:119
  35.7 12.3 %collective-permute-start.5 = (f32[512,128]{1,0:T(8,128)S(1)}, f32[512,128]{1,0:T(8,128)S(1)}, u32[]{:S(2)}, u32[]{:S(2)}) collective-permute-start(f32[512,128]{1,0:T(8,128)S(1)} %get-tuple-element.20), channel_id=1, source_target_pairs={{1,2},{2,1},{5,6},{6,5},{9,10},{10,9},{13,14},{14,13},{17,18},{18,... | collective-permute-start | bytes 786440 | tf_op jit(solution)/shard_map/ppermute | solution.py:120
  36.4 11.6 %collective-permute-start.4 = (f32[512,128]{1,0:T(8,128)S(1)}, f32[512,128]{1,0:T(8,128)S(1)}, u32[]{:S(2)}, u32[]{:S(2)}) collective-permute-start(f32[512,128]{1,0:T(8,128)S(1)} %get-tuple-element.19), channel_id=1, source_target_pairs={{0,1},{1,0},{2,3},{3,2},{4,5},{5,4},{6,7},{7,6},{8,9},{9,8},{10,11... | collective-permute-start | bytes 786440 | tf_op jit(solution)/shard_map/ppermute | solution.py:79
  42.4 14.8 %copy-start = (f32[512,128]{1,0:T(8,128)S(1)}, f32[512,128]{1,0:T(8,128)}, u32[]{:S(2)}) copy-start(f32[512,128]{1,0:T(8,128)} %masking.1.masked_ref) | copy-start | bytes 786436
  42.4 14.8 %copy-start.3 = (s32[4,1]{0,1:T(1,128)S(1)}, s32[4,1]{0,1:T(1,128)}, u32[]{:S(2)}) copy-start(s32[4,1]{0,1:T(1,128)} %param.6) | copy-start | bytes 52
  42.4 14.8 %collective-permute-start.7 = (f32[512,128]{1,0:T(8,128)S(1)}, f32[512,128]{1,0:T(8,128)S(1)}, u32[]{:S(2)}, u32[]{:S(2)}) collective-permute-start(f32[512,128]{1,0:T(8,128)S(1)} %add.12), channel_id=1, source_target_pairs={{0,2},{1,3},{2,0},{3,1},{4,6},{5,7},{6,4},{7,5},{8,10},{9,11},{10,... | collective-permute-start | bytes 786440 | tf_op jit(solution)/shard_map/ppermute | solution.py:79
  58.5 5.6 %copy-start.4 = (f32[128,128]{1,0:T(8,128)S(1)}, f32[128,128]{1,0:T(8,128)}, u32[]{:S(2)}) copy-start(f32[128,128]{1,0:T(8,128)} %param.7) | copy-start | bytes 196612
  58.5 1.3 %collective-permute-start.8 = (f32[128,128]{1,0:T(8,128)S(1)}, f32[128,128]{1,0:T(8,128)S(1)}, u32[]{:S(2)}, u32[]{:S(2)}) collective-permute-start(f32[128,128]{1,0:T(8,128)S(1)} %get-tuple-element.23), channel_id=1, source_target_pairs={{0,4},{4,0},{8,12},{12,8},{1,5},{5,1},{9,13},{13,9},{2,6},{6,2},{1... | collective-permute-start | bytes 196616 | tf_op jit(solution)/shard_map/ppermute | solution.py:79
  59.8 4.3 %collective-permute-start.9 = (f32[128,128]{1,0:T(8,128)S(1)}, f32[128,128]{1,0:T(8,128)S(1)}, u32[]{:S(2)}, u32[]{:S(2)}) collective-permute-start(f32[128,128]{1,0:T(8,128)S(1)} %add.13), channel_id=1, source_target_pairs={{0,8},{4,12},{8,0},{12,4},{1,9},{5,13},{9,1},{13,5},{2,10},{6,14},... | collective-permute-start | bytes 196616 | tf_op jit(solution)/shard_map/ppermute | solution.py:79

commit v3 on v2

v3 whole, which is shorter than its diff:
```python
import functools

import jax
import jax.numpy as jnp
from jax import lax
from jax.experimental import pallas as pl
from jax.experimental.pallas import tpu as pltpu
from jax.sharding import PartitionSpec as P

GRID = ("row", "col")
VMEM = pl.BlockSpec(memory_space=pltpu.VMEM)
SMEM = pl.BlockSpec(memory_space=pltpu.SMEM)
F32 = jnp.float32
ROWS = ((0,), (0,))
INNER = ((1,), (0,))


def split(x):
    high = x.astype(jnp.bfloat16)
    return high, (x - high.astype(F32)).astype(jnp.bfloat16)


def dot(a, b, dims):
    return lax.dot_general(a, b, (dims, ((), ())), preferred_element_type=F32)


def call(body, ins, outs, args, grant, name, flops=None):
    return pl.pallas_call(
        body,
        out_shape=[jax.ShapeDtypeStruct(shape, dtype) for shape, dtype in outs],
        in_specs=ins,
        out_specs=[VMEM] * len(outs),
        compiler_params=pltpu.CompilerParams(vmem_limit_bytes=grant << 20),
        cost_estimate=flops
        and pl.CostEstimate(flops=flops, bytes_accessed=0, transcendentals=0),
        name=name,
    )(*args)


def masking(spans, mask_ref, panel_ref, *out_refs):
    supers, blocks = mask_ref.shape
    tall, wide = panel_ref.shape[0] // blocks, panel_ref.shape[1] // supers
    for (first, last), ref in zip(spans, out_refs):
        for b in range(first, last):
            for s in range(supers):
                cols = slice(s * wide, (s + 1) * wide)
                block = panel_ref[b * tall : (b + 1) * tall, cols]
                at = (b - first) * tall
                ref[at : at + tall, cols] = block * mask_ref[s, b].astype(F32)


def splitting(a_ref, high_ref, low_ref):
    high_ref[...], low_ref[...] = split(a_ref[...])


def product(ah, al, m):
    mh, ml = split(m)
    width = m.shape[1]
    first = dot(ah, jnp.concatenate([mh, ml], axis=1), INNER)
    return first[:, :width] + (first[:, width:] + dot(al, mh, INNER))


def products(count, shift_ref, high_ref, low_ref, *refs):
    panels, outs = refs[:count], refs[count:]
    ah, al = high_ref[...], low_ref[...]
    shift = shift_ref[0]
    for i in range(count):
        m = panels[0][...]
        for j in range(1, count):
            m = jnp.where(shift == (i ^ j), panels[j][...], m)
        outs[i][...] = product(ah, al, m)


def pair(same_ref, high_ref, low_ref, mine_ref, other_ref, *outs):
    ah, al = high_ref[...], low_ref[...]
    same = same_ref[0] == 1
    mine, other = mine_ref[...], other_ref[...]
    for m, refs in (
        (jnp.where(same, mine, other), outs[: len(outs) // 2]),
        (jnp.where(same, other, mine), outs[len(outs) // 2 :]),
    ):
        out = product(ah, al, m)
        tall = out.shape[0] // len(refs)
        for i, ref in enumerate(refs):
            ref[...] = out[i * tall : (i + 1) * tall, :]


def finish(width, mask_ref, masked_ref, *refs):
    parts, g_ref, quad_ref = refs[:-2], refs[-2], refs[-1]
    rows = g_ref.shape[0]
    supers, blocks = mask_ref.shape
    tall = rows // blocks
    for b in range(blocks):
        for s in range(supers):
            cols = slice(s * width, (s + 1) * width)
            total = None
            for whole in parts:
                pieces = whole if isinstance(whole, tuple) else (whole,)
                depth = rows // len(pieces)
                ref, at = pieces[b * tall // depth], b * tall % depth
                term = ref[at : at + tall, cols]
                total = term if total is None else total + term
            g_ref[b * tall : (b + 1) * tall, cols] = total * -mask_ref[s, b].astype(F32)
    for s in range(supers):
        cols = slice(s * width, (s + 1) * width)
        mh, ml = split(masked_ref[:, cols])
        gh, gl = split(g_ref[:, cols])
        quad_ref[cols, :] = -(dot(mh, gh, ROWS) + (dot(mh, gl, ROWS) + dot(ml, gh, ROWS)))


def finish_paired(width, mask_ref, masked_ref, own, near, far0, far1, g_ref, quad_ref):
    finish(width, mask_ref, masked_ref, own, near, (far0, far1), g_ref, quad_ref)


def gather_any(side, masked, halves, swap):
    rows, cols = masked.shape
    turned = lax.ppermute(
        masked, GRID, [(r * side + c, c * side + r) for r in range(side) for c in range(side)]
    )
    turned, *halves = lax.optimization_barrier((turned, *halves))
    panels = {0: turned}
    bit = side // 2
    while bit:
        for j, x in list(panels.items()):
            panels[j ^ bit] = swap(x, "row", bit)
        bit //= 2
    shift = jnp.bitwise_xor(lax.axis_index("row"), lax.axis_index("col"))
    partials = call(
        functools.partial(products, side),
        [SMEM] + [VMEM] * (2 + side),
        [((rows, cols), F32)] * side,
        (shift.astype(jnp.int32).reshape(1), *halves, *[panels[j] for j in range(side)]),
        48,
        "products",
    )
    return [partials[0]] + [swap(partials[i], "col", i) for i in range(1, side)]


def route(rule):
    pairs = []
    for x in range(2):
        for t in range(2):
            for h in range(2):
                for l in range(2):
                    to = rule(x, t, h, l)
                    if to is not None:
                        (x2, t2), z2 = to
                        pairs.append((8 * x + 4 * t + 2 * h + l, 8 * x2 + 4 * t2 + z2))
    return pairs


def to_plane(x, t, h, l):
    return ((1 - h, t), 2 * h + l) if t == l else ((1 - h, 1 - t), 2 * h + t)


def cross_early(x, t, h, l):
    return to_plane(x, t, h, l) if x == h else ((1 - x, t), 2 * h + l)


def far_direct(x, t, h, l):
    return to_plane(x, t, h, l) if x == h else ((x, l), 2 * x + t)


def far_both(x, t, h, l):
    return ((x, l), 2 * (1 - x) + t) if x == h else ((x, l), 2 * x + t)


def near_here(x, t, h, l):
    if x != h:
        return None
    return ((x, t), 2 * h + l) if t == l else ((x, 1 - t), 2 * h + t)


def cross_late(x, t, h, l):
    return ((1 - x, t), 2 * h + l) if x == h else None


def gather_four(masked, top, low, inverse_blocks, halved, swap):
    rows, cols = masked.shape
    row, col = lax.axis_index("row"), lax.axis_index("col")
    near_side = (row // 2) == (col // 2)
    same = ((row % 2) == (col % 2)).astype(jnp.int32).reshape(1)

    low_crossed = lax.ppermute(low, GRID, route(cross_early))
    top_moved = lax.ppermute(top, GRID, route(far_direct))
    low_next = jnp.where(near_side, low_crossed, low)
    low_moved = lax.ppermute(low_next, GRID, route(far_both))
    near = lax.ppermute(lax.optimization_barrier((masked, low_next))[0], GRID, route(near_here))
    halves = halved(lax.optimization_barrier((inverse_blocks, low_next))[0])
    top_next, *halves = lax.optimization_barrier((top_moved, *halves))
    top_crossed = lax.ppermute(top_next, GRID, route(cross_late))
    far = jnp.concatenate([jnp.where(near_side, top_moved, top_crossed), low_moved])
    near = jnp.where(near_side, near, jnp.concatenate([top_moved, low_crossed]))
    far_other = swap(far, "row", 1)
    near_other = swap(near, "row", 1)

    half = ((rows // 2, cols), F32)
    far2a, far2b, far3a, far3b = call(
        pair, [SMEM] + [VMEM] * 4, [half] * 4, (same, *halves, far, far_other), 12, "far_pair"
    )
    own, near1 = call(
        pair,
        [SMEM] + [VMEM] * 4,
        [((rows, cols), F32)] * 2,
        (same, *halves, near, near_other),
        12,
        "near_pair",
    )
    first = swap(far3a, "col", 1)
    second = swap(far3b, "col", 1)
    near1 = swap(near1, "col", 1)
    return [own, near1, swap(far2a + first, "col", 2), swap(far2b + second, "col", 2)]


def on_device(side, inverse_blocks, lower_panel, struct_mask, diag_inverse):
    width = diag_inverse.shape[1]
    rows, cols = lower_panel.shape

    def swap(x, axis, bit):
        return lax.ppermute(x, axis, [(i, i ^ bit) for i in range(side)])

    mask = struct_mask.T
    blocks = struct_mask.shape[0]
    four = side == 4 and blocks % 2 == 0

    def masked_rows(*spans):
        return call(
            functools.partial(masking, spans),
            [SMEM, VMEM],
            [((rows * (last - first) // blocks, cols), F32) for first, last in spans],
            (mask, lower_panel),
            4,
            "masking",
        )

    def halved(matrix):
        return call(
            splitting,
            [VMEM],
            [(matrix.shape, jnp.bfloat16)] * 2,
            (matrix,),
            8,
            "splitting",
            20_000_000_000,
        )

    if four:
        (low,) = masked_rows((blocks // 2, blocks))
        masked, top = masked_rows((0, blocks), (0, blocks // 2))
        arrived, body = gather_four(masked, top, low, inverse_blocks, halved, swap), finish_paired
    else:
        (masked,) = masked_rows((0, blocks))
        arrived, body = gather_any(side, masked, halved(inverse_blocks), swap), finish

    g_panel, quad = call(
        functools.partial(body, width),
        [SMEM] + [VMEM] * (1 + len(arrived)),
        [((rows, cols), F32), ((cols, width), F32)],
        (mask, masked, *arrived),
        16,
        "finish",
    )
    bit = 1
    while bit < side:
        quad = quad + swap(quad, "row", bit)
        bit *= 2
    return g_panel, diag_inverse + quad


def solution(mesh):
    side = mesh.shape["row"]
    assert side == mesh.shape["col"] and side & (side - 1) == 0
    placed = (
        P(("pole", "row"), "col"),
        P(("pole", "row"), "col"),
        P("row", "col"),
        P(("pole", "col"), None),
    )
    return jax.shard_map(
        functools.partial(on_device, side),
        mesh=mesh,
        in_specs=placed,
        out_specs=(P(("pole", "row"), "col"), P(("pole", "col"), None)),
        check_vma=False,
    )
```

time: 65.1 us -> 56.7 us (0.87)
  starting transfers between devices: 30.2 us -> 11.5 us
  waiting for transfers between devices: 24.5 us -> 37.9 us
  Pallas kernels: 6.55 us -> 4.04 us
    ppermute x7 -> x9, starting transfers between devices: 25.1 us -> 5.69 us  [swap(): return lax.ppermute(x, axis, [(i, i ^ bit) for i in range(side)])]
    ppermute x3 -> x5, waiting for transfers between devices: 3.11 us -> 16.3 us  [the longest x1 6.26 us: gather_four(): low_moved = lax.ppermute(low_next, GRID, route(far_both))]
    pallas_call x4 -> x6, Pallas kernels: 6.55 us -> 4.04 us  [call(): pl.pallas_call(body, out_shape=[jax.ShapeDtypeStruct(shape, dtype) for sh...]
    ppermute x3 -> x5, starting transfers between devices: 5.17 us -> 5.78 us  [the longest x1 3 us: gather_four(): low_crossed = lax.ppermute(low, GRID, route(cross_early))]
    unnamed x10 -> x8, local copies, waits for them, and re-layouts: 2.1 us -> 1.61 us
    ppermute x7 -> x9, waiting for transfers between devices: 21.4 us -> 21.6 us  [swap(): return lax.ppermute(x, axis, [(i, i ^ bit) for i in range(side)])]
  transfers between devices with their start and end apart: 10 -> 14, of which waited for: 7 -> 10; matrix products, arithmetic and copies ran while one was open for 0% -> 0% of each run, Pallas kernels for 4% -> 4%
where the time goes in v3:
time: 56.7 us; the launch traced here: 56.6 us
  waiting for transfers between devices  37.9 us (67%)
  starting transfers between devices  11.5 us (20%)
  Pallas kernels  4.04 us (7%)
  local copies, waits for them, and re-layouts  1.61 us (3%)
  between operations  0.78 us (1%)
  other arithmetic  0.77 us (1%)
    ppermute x9, waiting for transfers between devices, swap(): return lax.ppermute(x, axis, [(i, i ^ bit) for i in range(side)])  21.6 us
    ppermute x1, waiting for transfers between devices, gather_four(): low_moved = lax.ppermute(low_next, GRID, route(far_both))  6.26 us
    ppermute x9, starting transfers between devices, swap(): return lax.ppermute(x, axis, [(i, i ^ bit) for i in range(side)])  5.69 us
    ppermute x1, waiting for transfers between devices, gather_four(): low_crossed = lax.ppermute(low, GRID, route(cross_early))  4.63 us
    ppermute x1, waiting for transfers between devices, gather_four(): top_moved = lax.ppermute(top, GRID, route(far_direct))  4.09 us
    pallas_call x6, Pallas kernels, call(): pl.pallas_call(body, out_shape=[jax.ShapeDtypeStruct(shape, dtype) for sh...  4.04 us
    ppermute x1, starting transfers between devices, gather_four(): low_crossed = lax.ppermute(low, GRID, route(cross_early))  3 us
    unnamed x8, local copies, waits for them, and re-layouts  1.61 us
  transfers between devices with their start and end apart: 14, of which 10 were waited for; matrix products, arithmetic and copies ran while one was open for 0% of the time, Pallas kernels for 4%

profile of v3, /device:TPU:0, one launch (start us, length us, event | category | flops | bytes accessed | tf_op | source)
XLA Modules:
  0.0 56.6 jit_solution(13868995759695215040)
XLA Ops:
  0.6 0.6 %copy-done.1 = s32[4,1]{0,1:T(1,128)S(1)} copy-done((s32[4,1]{0,1:T(1,128)S(1)}, s32[4,1]{0,1:T(1,128)}, u32[]{:S(2)}) %copy-start.1) | copy-done | bytes 40
  1.3 0.9 %copy-done = f32[512,128]{1,0:T(8,128)S(1)} copy-done((f32[512,128]{1,0:T(8,128)S(1)}, f32[512,128]{1,0:T(8,128)}, u32[]{:S(2)}) %copy-start) | copy-done | bytes 262168
  2.2 0.6 masking.3
  2.8 3.0 %collective-permute-start.1 = (f32[256,128]{1,0:T(8,128)S(1)}, f32[256,128]{1,0:T(8,128)S(1)}, u32[]{:S(2)}, u32[]{:S(2)}) collective-permute-start(f32[256,128]{1,0:T(8,128)S(1)} %masking.3), channel_id=1, source_target_pairs={{0,8},{1,12},{2,10},{3,11},{4,9},{5,13},{6,14},{7,15},{8,0},{9,1},... | collective-permute-start | bytes 393224 | tf_op jit(solution)/shard_map/ppermute | solution.py:184
  5.8 0.6 %masking.2 = (f32[512,128]{1,0:T(8,128)S(1)}, f32[256,128]{1,0:T(8,128)S(1)}) custom-call(s32[1,4]{1,0:T(1,128)S(1)} %bitcast.3, f32[512,128]{1,0:T(8,128)S(1)} %copy-done), custom_call_target="tpu_custom_call" | custom-call | tf_op jit(solution)/shard_map/masking/pallas_call | solution.py:28
  6.4 0.1 collective-permute-start
  6.5 4.6 %collective-permute-done.1 = f32[256,128]{1,0:T(8,128)S(1)} collective-permute-done((f32[256,128]{1,0:T(8,128)S(1)}, f32[256,128]{1,0:T(8,128)S(1)}, u32[]{:S(2)}, u32[]{:S(2)}) %collective-permute-start.1) | collective-permute-done | bytes 131104 | tf_op jit(solution)/shard_map/ppermute | solution.py:184
  11.1 0.2 splitting.1
  11.3 4.1 %collective-permute-done = f32[256,128]{1,0:T(8,128)S(1)} collective-permute-done((f32[256,128]{1,0:T(8,128)S(1)}, f32[256,128]{1,0:T(8,128)S(1)}, u32[]{:S(2)}, u32[]{:S(2)}) %collective-permute-start) | collective-permute-done | bytes 131104 | tf_op jit(solution)/shard_map/ppermute | solution.py:185
  15.4 1.5 %collective-permute-start.5 = (f32[256,128]{1,0:T(8,128)S(1)}, f32[256,128]{1,0:T(8,128)S(1)}, u32[]{:S(2)}, u32[]{:S(2)}) collective-permute-start(f32[256,128]{1,0:T(8,128)S(1)} %collective-permute-done), channel_id=1, source_target_pairs={{0,8},{1,9},{4,12},{5,13},{10,2},{11,3},{14,6},{15,7},{16,24},{17,... | collective-permute-start | bytes 393224 | tf_op jit(solution)/shard_map/ppermute | solution.py:191
  16.9 0.5 collective-permute-start.6
  17.4 0.7 %collective-permute-start.2 = (f32[512,128]{1,0:T(8,128)S(1)}, f32[512,128]{1,0:T(8,128)S(1)}, u32[]{:S(2)}, u32[]{:S(2)}) collective-permute-start(f32[512,128]{1,0:T(8,128)S(1)} %get-tuple-element.26.masked_ref), channel_id=1, source_target_pairs={{0,0},{1,4},{4,1},{5,5},{10,10},{11,14},{14,11},{15,15},{16,16},{1... | collective-permute-start | bytes 786440 | tf_op jit(solution)/shard_map/ppermute | solution.py:188
  18.1 1.3 %collective-permute-done.5 = f32[256,128]{1,0:T(8,128)S(1)} collective-permute-done((f32[256,128]{1,0:T(8,128)S(1)}, f32[256,128]{1,0:T(8,128)S(1)}, u32[]{:S(2)}, u32[]{:S(2)}) %collective-permute-start.5) | collective-permute-done | bytes 131104 | tf_op jit(solution)/shard_map/ppermute | solution.py:191
  19.4 6.3 %collective-permute-done.6 = f32[256,128]{1,0:T(8,128)S(1)} collective-permute-done((f32[256,128]{1,0:T(8,128)S(1)}, f32[256,128]{1,0:T(8,128)S(1)}, u32[]{:S(2)}, u32[]{:S(2)}) %collective-permute-start.6) | collective-permute-done | bytes 131104 | tf_op jit(solution)/shard_map/ppermute | solution.py:187
  25.7 0.1 collective-permute-start.7
  25.8 1.6 %collective-permute-start.3 = (f32[512,128]{1,0:T(8,128)S(1)}, f32[512,128]{1,0:T(8,128)S(1)}, u32[]{:S(2)}, u32[]{:S(2)}) collective-permute-start(f32[512,128]{1,0:T(8,128)S(1)} %maximum_select_fusion.mine_ref), channel_id=1, source_target_pairs={{0,4},{4,0},{8,12},{12,8},{1,5},{5,1},{9,13},{13,9},{2,6},{6,2},{1... | collective-permute-start | bytes 786440 | tf_op jit(solution)/shard_map/ppermute | solution.py:220
  27.4 0.7 %far_pair.1 = (f32[256,128]{1,0:T(8,128)S(1)}, f32[256,128]{1,0:T(8,128)S(1)}, f32[256,128]{1,0:T(8,128)S(1)}, f32[256,128]{1,0:T(8,128)S(1)}) custom-call(s32[1]{0:T(128)} %bitcast.1.same_ref, bf16[512,512]{1,0:T(8,128)(2,1)S(1)} %get-tuple-element.24.high_ref, bf16[512,512]{1,0:T(8,128)(2,1)S(1)} %get-tuple-element.25.low_ref, ...), custom_call_target="tpu_custom_call" | custom-call | tf_op jit(solution)/shard_map/far_pair/pallas_call | solution.py:28
  28.1 0.3 collective-permute-start.10
  28.5 1.7 %collective-permute-start.8 = (f32[256,128]{1,0:T(8,128)S(1)}, f32[256,128]{1,0:T(8,128)S(1)}, u32[]{:S(2)}, u32[]{:S(2)}) collective-permute-start(f32[256,128]{1,0:T(8,128)S(1)} %get-tuple-element.31), channel_id=1, source_target_pairs={{0,1},{1,0},{2,3},{3,2},{4,5},{5,4},{6,7},{7,6},{8,9},{9,8},{10,11... | collective-permute-start | bytes 393224 | tf_op jit(solution)/shard_map/ppermute | solution.py:220
  30.2 0.7 %near_pair.1 = (f32[512,128]{1,0:T(8,128)S(1)}, f32[512,128]{1,0:T(8,128)S(1)}) custom-call(s32[1]{0:T(128)} %bitcast.1.same_ref, bf16[512,512]{1,0:T(8,128)(2,1)S(1)} %get-tuple-element.24.high_ref, bf16[512,512]{1,0:T(8,128)(2,1)S(1)} %get-tuple-element.25.low_ref, f32[512,128]{1,0:T(8,128)S(1)} %maximum_select_fusion.mine_ref, ...), custom_call_target="tpu_custom_call" | custom-call | tf_op jit(solution)/shard_map/near_pair/pallas_call | solution.py:28
  31.0 0.3 collective-permute-start.4
  31.3 3.3 %collective-permute-done.10 = f32[256,128]{1,0:T(8,128)S(1)} collective-permute-done((f32[256,128]{1,0:T(8,128)S(1)}, f32[256,128]{1,0:T(8,128)S(1)}, u32[]{:S(2)}, u32[]{:S(2)}) %collective-permute-start.10) | collective-permute-done | bytes 131104 | tf_op jit(solution)/shard_map/ppermute | solution.py:220
  34.6 0.1 collective-permute-start.11
  34.7 4.1 %collective-permute-done.8 = f32[256,128]{1,0:T(8,128)S(1)} collective-permute-done((f32[256,128]{1,0:T(8,128)S(1)}, f32[256,128]{1,0:T(8,128)S(1)}, u32[]{:S(2)}, u32[]{:S(2)}) %collective-permute-start.8) | collective-permute-done | bytes 131104 | tf_op jit(solution)/shard_map/ppermute | solution.py:220
  38.8 0.1 collective-permute-start.9
  38.9 8.6 %collective-permute-done.11.far1 = f32[256,128]{1,0:T(8,128)S(1)} collective-permute-done((f32[256,128]{1,0:T(8,128)S(1)}, f32[256,128]{1,0:T(8,128)S(1)}, u32[]{:S(2)}, u32[]{:S(2)}) %collective-permute-start.11) | collective-permute-done | bytes 131104 | tf_op jit(solution)/shard_map/ppermute | solution.py:220
  47.4 1.5 %collective-permute-done.9.far0 = f32[256,128]{1,0:T(8,128)S(1)} collective-permute-done((f32[256,128]{1,0:T(8,128)S(1)}, f32[256,128]{1,0:T(8,128)S(1)}, u32[]{:S(2)}, u32[]{:S(2)}) %collective-permute-start.9) | collective-permute-done | bytes 131104 | tf_op jit(solution)/shard_map/ppermute | solution.py:220
  49.0 1.3 %finish.1 = (f32[512,128]{1,0:T(8,128)}, f32[128,128]{1,0:T(8,128)S(1)}) custom-call(s32[1,4]{1,0:T(1,128)S(1)} %bitcast.4, f32[512,128]{1,0:T(8,128)S(1)} %get-tuple-element.26.masked_ref, f32[512,128]{1,0:T(8,128)S(1)} %get-tuple-element.27.own, f32[512,128]{1,0:T(8,128)S(1)} %collective-permute-done.4.near, f32[256,128]{1,0:T(8,128)S(1)} %collective-permute-done.9.far0, ...), custom_call_target="tpu_custom_call" | custom-call | tf_op jit(solution)/shard_map/finish/pallas_call | solution.py:28
  50.3 1.3 %collective-permute-done.12 = f32[128,128]{1,0:T(8,128)S(1)} collective-permute-done((f32[128,128]{1,0:T(8,128)S(1)}, f32[128,128]{1,0:T(8,128)S(1)}, u32[]{:S(2)}, u32[]{:S(2)}) %collective-permute-start.12) | collective-permute-done | bytes 65568 | tf_op jit(solution)/shard_map/ppermute | solution.py:220
  51.6 1.4 %collective-permute-start.13 = (f32[128,128]{1,0:T(8,128)S(1)}, f32[128,128]{1,0:T(8,128)S(1)}, u32[]{:S(2)}, u32[]{:S(2)}) collective-permute-start(f32[128,128]{1,0:T(8,128)S(1)} %add.28), channel_id=1, source_target_pairs={{0,8},{4,12},{8,0},{12,4},{1,9},{5,13},{9,1},{13,5},{2,10},{6,14},... | collective-permute-start | bytes 196616 | tf_op jit(solution)/shard_map/ppermute | solution.py:220
  53.0 2.9 %collective-permute-done.13 = f32[128,128]{1,0:T(8,128)S(1)} collective-permute-done((f32[128,128]{1,0:T(8,128)S(1)}, f32[128,128]{1,0:T(8,128)S(1)}, u32[]{:S(2)}, u32[]{:S(2)}) %collective-permute-start.13) | collective-permute-done | bytes 65568 | tf_op jit(solution)/shard_map/ppermute | solution.py:220
  55.9 0.6 %add_add_fusion = f32[128,128]{1,0:T(8,128)} fusion(f32[128,128]{1,0:T(8,128)S(1)} %copy-done.3, f32[128,128]{1,0:T(8,128)S(1)} %add.28, f32[128,128]{1,0:T(8,128)S(1)} %collective-permute-done.13), kind=kLoop, calls=%fused_computation.2 | loop fusion | flops 32768 | bytes 262144 | tf_op jit(solution)/shard_map/add | solution.py:267
  (18 shorter events, 0.2 us)
Async XLA Ops:
  0.6 0.7 %copy-start.1 = (s32[4,1]{0,1:T(1,128)S(1)}, s32[4,1]{0,1:T(1,128)}, u32[]{:S(2)}) copy-start(s32[4,1]{0,1:T(1,128)} %param.6) | copy-start | bytes 52
  1.3 0.9 %copy-start = (f32[512,128]{1,0:T(8,128)S(1)}, f32[512,128]{1,0:T(8,128)}, u32[]{:S(2)}) copy-start(f32[512,128]{1,0:T(8,128)} %panel_ref.3) | copy-start | bytes 786436
  2.2 8.9 %copy-start.2 = (f32[512,512]{1,0:T(8,128)S(1)}, f32[512,512]{1,0:T(8,128)}, u32[]{:S(2)}) copy-start(f32[512,512]{1,0:T(8,128)} %a_ref) | copy-start | bytes 3145732
  2.8 8.3 %collective-permute-start.1 = (f32[256,128]{1,0:T(8,128)S(1)}, f32[256,128]{1,0:T(8,128)S(1)}, u32[]{:S(2)}, u32[]{:S(2)}) collective-permute-start(f32[256,128]{1,0:T(8,128)S(1)} %masking.3), channel_id=1, source_target_pairs={{0,8},{1,12},{2,10},{3,11},{4,9},{5,13},{6,14},{7,15},{8,0},{9,1},... | collective-permute-start | bytes 393224 | tf_op jit(solution)/shard_map/ppermute | solution.py:184
  6.4 9.0 %collective-permute-start = (f32[256,128]{1,0:T(8,128)S(1)}, f32[256,128]{1,0:T(8,128)S(1)}, u32[]{:S(2)}, u32[]{:S(2)}) collective-permute-start(f32[256,128]{1,0:T(8,128)S(1)} %get-tuple-element.20), channel_id=1, source_target_pairs={{0,8},{1,12},{2,0},{3,4},{4,9},{5,13},{6,1},{7,5},{8,10},{9,14},{1... | collective-permute-start | bytes 393224 | tf_op jit(solution)/shard_map/ppermute | solution.py:185
  15.4 4.0 %collective-permute-start.5 = (f32[256,128]{1,0:T(8,128)S(1)}, f32[256,128]{1,0:T(8,128)S(1)}, u32[]{:S(2)}, u32[]{:S(2)}) collective-permute-start(f32[256,128]{1,0:T(8,128)S(1)} %collective-permute-done), channel_id=1, source_target_pairs={{0,8},{1,9},{4,12},{5,13},{10,2},{11,3},{14,6},{15,7},{16,24},{17,... | collective-permute-start | bytes 393224 | tf_op jit(solution)/shard_map/ppermute | solution.py:191
  16.9 8.8 %collective-permute-start.6 = (f32[256,128]{1,0:T(8,128)S(1)}, f32[256,128]{1,0:T(8,128)S(1)}, u32[]{:S(2)}, u32[]{:S(2)}) collective-permute-start(f32[256,128]{1,0:T(8,128)S(1)} %broadcast_select_fusion.1), channel_id=1, source_target_pairs={{0,2},{1,6},{2,0},{3,4},{4,3},{5,7},{6,1},{7,5},{8,10},{9,14},{10,... | collective-permute-start | bytes 393224 | tf_op jit(solution)/shard_map/ppermute | solution.py:187
  17.4 8.3 %collective-permute-start.2 = (f32[512,128]{1,0:T(8,128)S(1)}, f32[512,128]{1,0:T(8,128)S(1)}, u32[]{:S(2)}, u32[]{:S(2)}) collective-permute-start(f32[512,128]{1,0:T(8,128)S(1)} %get-tuple-element.26.masked_ref), channel_id=1, source_target_pairs={{0,0},{1,4},{4,1},{5,5},{10,10},{11,14},{14,11},{15,15},{16,16},{1... | collective-permute-start | bytes 786440 | tf_op jit(solution)/shard_map/ppermute | solution.py:188
  25.7 1.7 %collective-permute-start.7 = (f32[512,128]{1,0:T(8,128)S(1)}, f32[512,128]{1,0:T(8,128)S(1)}, u32[]{:S(2)}, u32[]{:S(2)}) collective-permute-start(f32[512,128]{1,0:T(8,128)S(1)} %pad_maximum_fusion.mine_ref), channel_id=1, source_target_pairs={{0,4},{4,0},{8,12},{12,8},{1,5},{5,1},{9,13},{13,9},{2,6},{6,2},{1... | collective-permute-start | bytes 786440 | tf_op jit(solution)/shard_map/ppermute | solution.py:220
  25.8 4.4 %collective-permute-start.3 = (f32[512,128]{1,0:T(8,128)S(1)}, f32[512,128]{1,0:T(8,128)S(1)}, u32[]{:S(2)}, u32[]{:S(2)}) collective-permute-start(f32[512,128]{1,0:T(8,128)S(1)} %maximum_select_fusion.mine_ref), channel_id=1, source_target_pairs={{0,4},{4,0},{8,12},{12,8},{1,5},{5,1},{9,13},{13,9},{2,6},{6,2},{1... | collective-permute-start | bytes 786440 | tf_op jit(solution)/shard_map/ppermute | solution.py:220
  28.1 6.4 %collective-permute-start.10 = (f32[256,128]{1,0:T(8,128)S(1)}, f32[256,128]{1,0:T(8,128)S(1)}, u32[]{:S(2)}, u32[]{:S(2)}) collective-permute-start(f32[256,128]{1,0:T(8,128)S(1)} %get-tuple-element.33), channel_id=1, source_target_pairs={{0,1},{1,0},{2,3},{3,2},{4,5},{5,4},{6,7},{7,6},{8,9},{9,8},{10,11... | collective-permute-start | bytes 393224 | tf_op jit(solution)/shard_map/ppermute | solution.py:220
  28.5 10.3 %collective-permute-start.8 = (f32[256,128]{1,0:T(8,128)S(1)}, f32[256,128]{1,0:T(8,128)S(1)}, u32[]{:S(2)}, u32[]{:S(2)}) collective-permute-start(f32[256,128]{1,0:T(8,128)S(1)} %get-tuple-element.31), channel_id=1, source_target_pairs={{0,1},{1,0},{2,3},{3,2},{4,5},{5,4},{6,7},{7,6},{8,9},{9,8},{10,11... | collective-permute-start | bytes 393224 | tf_op jit(solution)/shard_map/ppermute | solution.py:220
  31.0 18.0 %collective-permute-start.4 = (f32[512,128]{1,0:T(8,128)S(1)}, f32[512,128]{1,0:T(8,128)S(1)}, u32[]{:S(2)}, u32[]{:S(2)}) collective-permute-start(f32[512,128]{1,0:T(8,128)S(1)} %get-tuple-element.28), channel_id=1, source_target_pairs={{0,1},{1,0},{2,3},{3,2},{4,5},{5,4},{6,7},{7,6},{8,9},{9,8},{10,11... | collective-permute-start | bytes 786440 | tf_op jit(solution)/shard_map/ppermute | solution.py:220
  34.6 12.9 %collective-permute-start.11 = (f32[256,128]{1,0:T(8,128)S(1)}, f32[256,128]{1,0:T(8,128)S(1)}, u32[]{:S(2)}, u32[]{:S(2)}) collective-permute-start(f32[256,128]{1,0:T(8,128)S(1)} %add.27), channel_id=1, source_target_pairs={{0,2},{1,3},{2,0},{3,1},{4,6},{5,7},{6,4},{7,5},{8,10},{9,11},{10,... | collective-permute-start | bytes 393224 | tf_op jit(solution)/shard_map/ppermute | solution.py:220
  38.8 10.2 %collective-permute-start.9 = (f32[256,128]{1,0:T(8,128)S(1)}, f32[256,128]{1,0:T(8,128)S(1)}, u32[]{:S(2)}, u32[]{:S(2)}) collective-permute-start(f32[256,128]{1,0:T(8,128)S(1)} %add.26), channel_id=1, source_target_pairs={{0,2},{1,3},{2,0},{3,1},{4,6},{5,7},{6,4},{7,5},{8,10},{9,11},{10,... | collective-permute-start | bytes 393224 | tf_op jit(solution)/shard_map/ppermute | solution.py:220
  50.3 5.6 %copy-start.3 = (f32[128,128]{1,0:T(8,128)S(1)}, f32[128,128]{1,0:T(8,128)}, u32[]{:S(2)}) copy-start(f32[128,128]{1,0:T(8,128)} %param.7) | copy-start | bytes 196612
  50.3 1.3 %collective-permute-start.12 = (f32[128,128]{1,0:T(8,128)S(1)}, f32[128,128]{1,0:T(8,128)S(1)}, u32[]{:S(2)}, u32[]{:S(2)}) collective-permute-start(f32[128,128]{1,0:T(8,128)S(1)} %get-tuple-element.35), channel_id=1, source_target_pairs={{0,4},{4,0},{8,12},{12,8},{1,5},{5,1},{9,13},{13,9},{2,6},{6,2},{1... | collective-permute-start | bytes 196616 | tf_op jit(solution)/shard_map/ppermute | solution.py:220
  51.6 4.3 %collective-permute-start.13 = (f32[128,128]{1,0:T(8,128)S(1)}, f32[128,128]{1,0:T(8,128)S(1)}, u32[]{:S(2)}, u32[]{:S(2)}) collective-permute-start(f32[128,128]{1,0:T(8,128)S(1)} %add.28), channel_id=1, source_target_pairs={{0,8},{4,12},{8,0},{12,4},{1,9},{5,13},{9,1},{13,5},{2,10},{6,14},... | collective-permute-start | bytes 196616 | tf_op jit(solution)/shard_map/ppermute | solution.py:220

commit v4 on v3

v4 whole, which is shorter than its diff:
```python
import functools

import jax
import jax.numpy as jnp
from jax import lax
from jax.experimental import pallas as pl
from jax.experimental.pallas import tpu as pltpu
from jax.sharding import PartitionSpec as P

GRID = ("row", "col")
VMEM = pl.BlockSpec(memory_space=pltpu.VMEM)
SMEM = pl.BlockSpec(memory_space=pltpu.SMEM)
HBM = pl.BlockSpec(memory_space=pltpu.HBM)
F32 = jnp.float32
ROWS = ((0,), (0,))
INNER = ((1,), (0,))


def split(x):
    high = x.astype(jnp.bfloat16)
    return high, (x - high.astype(F32)).astype(jnp.bfloat16)


def dot(a, b, dims):
    return lax.dot_general(a, b, (dims, ((), ())), preferred_element_type=F32)


def call(body, ins, outs, args, grant, name, flops=None, scratch=()):
    return pl.pallas_call(
        body,
        out_shape=[jax.ShapeDtypeStruct(shape, dtype) for shape, dtype in outs],
        in_specs=ins,
        out_specs=[VMEM] * len(outs),
        scratch_shapes=scratch,
        compiler_params=pltpu.CompilerParams(vmem_limit_bytes=grant << 20),
        cost_estimate=flops
        and pl.CostEstimate(flops=flops, bytes_accessed=0, transcendentals=0),
        name=name,
    )(*args)


def fold(x):
    tall = x.shape[0] // 2
    return jnp.concatenate([x[:tall], x[tall:]], axis=1)


def unfold(x):
    wide = x.shape[1] // 2
    return jnp.concatenate([x[:, :wide], x[:, wide:]], axis=0)


def masked_part(mask_ref, panel_ref, cols):
    supers, blocks = mask_ref.shape
    tall, wide = panel_ref.shape[0] // blocks, panel_ref.shape[1] // supers
    rows = []
    for b in range(blocks):
        at = slice(b * tall, (b + 1) * tall)
        row = [
            panel_ref[at, s * wide : (s + 1) * wide] * mask_ref[s, b].astype(F32)
            for s in range(supers)
        ]
        rows.append((row[0] if supers == 1 else jnp.concatenate(row, axis=1))[:, cols])
    return jnp.concatenate(rows, axis=0)


def masking(mask_ref, panel_ref, out_ref):
    out_ref[...] = masked_part(mask_ref, panel_ref, slice(None))


def masking_first(mask_hbm, panel_hbm, first_ref, mask_ref, panel_ref, sems):
    rows = panel_ref.shape[0] // 4
    copies = [pltpu.make_async_copy(mask_hbm, mask_ref, sems.at[4])]
    for i in range(4):
        at = pl.ds(i * rows, rows)
        copies.append(pltpu.make_async_copy(panel_hbm.at[at], panel_ref.at[at], sems.at[i]))
    for copy in copies:
        copy.start()
    for copy in copies:
        copy.wait()
    first_ref[...] = fold(masked_part(mask_ref, panel_ref, slice(0, panel_ref.shape[1] // 2)))


def masking_rest(mask_ref, panel_ref, out_ref, second_ref):
    whole = masked_part(mask_ref, panel_ref, slice(None))
    out_ref[...] = whole
    second_ref[...] = fold(whole[:, panel_ref.shape[1] // 2 :])


def splitting(a_ref, high_ref, low_ref):
    high_ref[...], low_ref[...] = split(a_ref[...])


def product(ah, al, m):
    mh, ml = split(m)
    width = m.shape[1]
    first = dot(ah, jnp.concatenate([mh, ml], axis=1), INNER)
    return first[:, :width] + (first[:, width:] + dot(al, mh, INNER))


def products(count, shift_ref, high_ref, low_ref, *refs):
    panels, outs = refs[:count], refs[count:]
    ah, al = high_ref[...], low_ref[...]
    shift = shift_ref[0]
    for i in range(count):
        m = panels[0][...]
        for j in range(1, count):
            m = jnp.where(shift == (i ^ j), panels[j][...], m)
        outs[i][...] = product(ah, al, m)


def near_pair(same_ref, high_ref, low_ref, mine_ref, other_ref, own_ref, next_ref):
    same = same_ref[0] == 1
    mine, other = mine_ref[...], other_ref[...]
    ah, al = high_ref[...], low_ref[...]
    next_ref[...] = product(ah, al, jnp.where(same, other, mine))
    own_ref[...] = product(ah, al, jnp.where(same, mine, other))


def far_pair(same_ref, high_ref, low_ref, mine_ref, other_ref, two_ref, three_ref):
    same = same_ref[0] == 1
    mine, other = unfold(mine_ref[...]), unfold(other_ref[...])
    two, three = jnp.where(same, mine, other), jnp.where(same, other, mine)
    out = product(high_ref[...], low_ref[...], jnp.concatenate([two, three], axis=1))
    wide = two.shape[1]
    two_ref[...], three_ref[...] = fold(out[:, :wide]), fold(out[:, wide:])


def finish_sum(width, mask_ref, masked_ref, total, g_ref, quad_ref):
    supers, blocks = mask_ref.shape
    tall = total.shape[0] // blocks
    for b in range(blocks):
        for s in range(supers):
            at = (slice(b * tall, (b + 1) * tall), slice(s * width, (s + 1) * width))
            g_ref[at] = total[at] * -mask_ref[s, b].astype(F32)
    for s in range(supers):
        cols = slice(s * width, (s + 1) * width)
        mh, ml = split(masked_ref[:, cols])
        gh, gl = split(g_ref[:, cols])
        quad_ref[cols, :] = -(dot(mh, gh, ROWS) + (dot(mh, gl, ROWS) + dot(ml, gh, ROWS)))


def finish(width, mask_ref, masked_ref, *refs):
    total = refs[0][...]
    for ref in refs[1:-2]:
        total = total + ref[...]
    finish_sum(width, mask_ref, masked_ref, total, *refs[-2:])


def finish_folded(width, mask_ref, masked_ref, own, near, far0, far1, g_ref, quad_ref):
    far = jnp.concatenate([unfold(far0[...]), unfold(far1[...])], axis=1)
    finish_sum(width, mask_ref, masked_ref, own[...] + near[...] + far, g_ref, quad_ref)


def gather_any(side, masked, halves, swap):
    rows, cols = masked.shape
    turned = lax.ppermute(
        masked, GRID, [(r * side + c, c * side + r) for r in range(side) for c in range(side)]
    )
    turned, *halves = lax.optimization_barrier((turned, *halves))
    panels = {0: turned}
    bit = side // 2
    while bit:
        for j, x in list(panels.items()):
            panels[j ^ bit] = swap(x, "row", bit)
        bit //= 2
    shift = jnp.bitwise_xor(lax.axis_index("row"), lax.axis_index("col"))
    partials = call(
        functools.partial(products, side),
        [SMEM] + [VMEM] * (2 + side),
        [((rows, cols), F32)] * side,
        (shift.astype(jnp.int32).reshape(1), *halves, *[panels[j] for j in range(side)]),
        48,
        "products",
    )
    return [partials[0]] + [swap(partials[i], "col", i) for i in range(1, side)]


def route(rule):
    pairs = []
    for x in range(2):
        for t in range(2):
            for h in range(2):
                for l in range(2):
                    to = rule(x, t, h, l)
                    if to is not None:
                        (x2, t2), z2 = to
                        pairs.append((8 * x + 4 * t + 2 * h + l, 8 * x2 + 4 * t2 + z2))
    return pairs


def cross_early(x, t, h, l):
    return ((1 - x, t), 2 * h + l) if x != h else None


def far_direct(x, t, h, l):
    return ((x, l), 2 * x + t) if x != h else None


def far_crossed(x, t, h, l):
    return ((x, l), 2 * (1 - x) + t) if x == h else None


def cross_late(x, t, h, l):
    return ((1 - x, t), 2 * h + l) if x == h else None


def near_here(x, t, h, l):
    if x != h:
        return None
    return ((x, t), 2 * h + l) if t == l else ((x, 1 - t), 2 * h + t)


def near_across(x, t, h, l):
    if x != h:
        return None
    return ((1 - x, t), 2 * h + l) if t == l else ((1 - x, 1 - t), 2 * h + t)


def move(x, rule, name):
    with jax.named_scope(name):
        return lax.ppermute(x, GRID, route(rule))


def after(x, *others):
    return lax.optimization_barrier((x, *others))[0]


def gather_four(first, rest, panel, matrix, halved, swap):
    row, col = lax.axis_index("row"), lax.axis_index("col")
    near_side = (row // 2) == (col // 2)
    same = ((row % 2) == (col % 2)).astype(jnp.int32).reshape(1)
    half, whole = (first.shape, F32), (panel.shape, F32)

    crossing = move(first, cross_early, "cross0")
    direct0 = move(first, far_direct, "direct0")
    crossed0 = move(crossing, far_crossed, "crossed0")
    masked, second = rest(after(panel, first))
    direct1 = move(second, far_direct, "direct1")
    halves = halved(after(matrix, crossing))

    def partials(mine, name):
        return call(
            far_pair,
            [SMEM] + [VMEM] * 4,
            [half] * 2,
            (same, *halves, mine, swap(mine, "row", 1, name)),
            12,
            "far_pair",
        )

    mine0 = jnp.where(near_side, direct0, crossed0)
    two0, three0 = partials(mine0, "cores0")
    sum0 = two0 + swap(three0, "col", 1, "next0")
    direct1 = after(direct1, three0)
    mine1 = jnp.where(near_side, direct1, move(direct1, cross_late, "cross1"))
    two1, three1 = partials(after(mine1, sum0), "cores1")
    far0 = swap(sum0, "col", 2, "across0")
    sum1 = two1 + swap(three1, "col", 1, "next1")
    far1 = swap(sum1, "col", 2, "across1")
    near_panel = after(masked, direct0)
    near_mine = jnp.where(
        near_side,
        move(near_panel, near_here, "near_here"),
        move(near_panel, near_across, "near_across"),
    )
    own, near1 = call(
        near_pair,
        [SMEM] + [VMEM] * 4,
        [whole] * 2,
        (same, *halves, near_mine, swap(near_mine, "row", 1, "near_cores")),
        12,
        "near_pair",
    )
    near1 = swap(after(near1, sum0), "col", 1, "near_partial")
    return [own, near1, far0, far1, masked]


def on_device(side, inverse_blocks, lower_panel, struct_mask, diag_inverse):
    width = diag_inverse.shape[1]
    rows, cols = lower_panel.shape

    def swap(x, axis, bit, name="swap"):
        with jax.named_scope(name):
            return lax.ppermute(x, axis, [(i, i ^ bit) for i in range(side)])

    mask = struct_mask.T
    blocks = struct_mask.shape[0]
    four = side == 4 and blocks % 2 == 0

    whole, half = ((rows, cols), F32), ((rows // 2, cols), F32)

    def mask_panel(body, outs, panel):
        return call(body, [SMEM, VMEM], outs, (mask, panel), 4, "masking")

    def halved(matrix):
        return call(
            splitting,
            [VMEM],
            [(matrix.shape, jnp.bfloat16)] * 2,
            (matrix,),
            8,
            "splitting",
            20_000_000_000,
        )

    if four:
        (first,) = call(
            masking_first,
            [HBM, HBM],
            [half],
            (mask, lower_panel),
            4,
            "masking_first",
            scratch=[
                pltpu.SMEM(mask.shape, mask.dtype),
                pltpu.VMEM((rows, cols), F32),
                pltpu.SemaphoreType.DMA((5,)),
            ],
        )
        rest = functools.partial(mask_panel, masking_rest, [whole, half])
        arrived = gather_four(first, rest, lower_panel, inverse_blocks, halved, swap)
        masked = arrived.pop()
        body = finish_folded
    else:
        (masked,) = mask_panel(masking, [whole], lower_panel)
        arrived, body = gather_any(side, masked, halved(inverse_blocks), swap), finish

    g_panel, quad = call(
        functools.partial(body, width),
        [SMEM] + [VMEM] * (1 + len(arrived)),
        [((rows, cols), F32), ((cols, width), F32)],
        (mask, masked, *arrived),
        16,
        "finish",
    )
    bit = 1
    while bit < side:
        quad = quad + swap(quad, "row", bit)
        bit *= 2
    return g_panel, diag_inverse + quad


def solution(mesh):
    side = mesh.shape["row"]
    assert side == mesh.shape["col"] and side & (side - 1) == 0
    placed = (
        P(("pole", "row"), "col"),
        P(("pole", "row"), "col"),
        P("row", "col"),
        P(("pole", "col"), None),
    )
    return jax.shard_map(
        functools.partial(on_device, side),
        mesh=mesh,
        in_specs=placed,
        out_specs=(P(("pole", "row"), "col"), P(("pole", "col"), None)),
        check_vma=False,
    )
```

time: 56.7 us -> 62.8 us (1.11)
  starting transfers between devices: 11.5 us -> 20.6 us
  waiting for transfers between devices: 37.9 us -> 33.8 us
  Pallas kernels: 4.04 us -> 4.87 us
    ppermute x5 -> x7, waiting for transfers between devices: 16.3 us -> 5.83 us  [move(): return lax.ppermute(x, GRID, route(rule))]
    ppermute x5 -> x7, starting transfers between devices: 5.78 us -> 13.9 us  [move(): return lax.ppermute(x, GRID, route(rule))]
    ppermute x9 -> x10, waiting for transfers between devices: 21.6 us -> 28 us  [swap(): return lax.ppermute(x, axis, [(i, i ^ bit) for i in range(side)])]
    ppermute x9 -> x10, starting transfers between devices: 5.69 us -> 6.7 us  [swap(): return lax.ppermute(x, axis, [(i, i ^ bit) for i in range(side)])]
    pallas_call x6 -> x7, Pallas kernels: 4.04 us -> 4.87 us  [call(): pl.pallas_call(body, out_shape=[jax.ShapeDtypeStruct(shape, dtype) for sh...]
  transfers between devices with their start and end apart: 14 -> 17, of which waited for: 10 -> 10; matrix products, arithmetic and copies ran while one was open for 0% -> 0% of each run, Pallas kernels for 4% -> 4%
where the time goes in v4:
time: 62.8 us; the launch traced here: 62.6 us
  waiting for transfers between devices  33.8 us (54%)
  starting transfers between devices  20.6 us (33%)
  Pallas kernels  4.87 us (8%)
  local copies, waits for them, and re-layouts  1.61 us (3%)
  between operations  0.89 us (1%)
  other arithmetic  0.75 us (1%)
    ppermute x10, waiting for transfers between devices, swap(): return lax.ppermute(x, axis, [(i, i ^ bit) for i in range(side)])  28 us
    ppermute x7, starting transfers between devices, move(): return lax.ppermute(x, GRID, route(rule))  13.9 us
    ppermute x10, starting transfers between devices, swap(): return lax.ppermute(x, axis, [(i, i ^ bit) for i in range(side)])  6.7 us
    ppermute x7, waiting for transfers between devices, move(): return lax.ppermute(x, GRID, route(rule))  5.83 us
    pallas_call x7, Pallas kernels, call(): pl.pallas_call(body, out_shape=[jax.ShapeDtypeStruct(shape, dtype) for sh...  4.87 us
    unnamed x8, local copies, waits for them, and re-layouts  1.61 us
  transfers between devices with their start and end apart: 17, of which 10 were waited for; matrix products, arithmetic and copies ran while one was open for 0% of the time, Pallas kernels for 4%

profile of v4, /device:TPU:0, one launch (start us, length us, event | category | flops | bytes accessed | tf_op | source)
XLA Modules:
  0.0 62.6 jit_solution(18371227554152414566)
XLA Ops:
  0.6 0.6 %copy-done.1 = s32[4,1]{0,1:T(1,128)S(1)} copy-done((s32[4,1]{0,1:T(1,128)S(1)}, s32[4,1]{0,1:T(1,128)}, u32[]{:S(2)}) %copy-start.1) | copy-done | bytes 40
  1.3 0.9 %copy-done = f32[512,128]{1,0:T(8,128)S(1)} copy-done((f32[512,128]{1,0:T(8,128)S(1)}, f32[512,128]{1,0:T(8,128)}, u32[]{:S(2)}) %copy-start) | copy-done | bytes 262168
  2.2 0.7 %masking_first.1 = f32[256,128]{1,0:T(8,128)S(1)} custom-call(s32[1,4]{1,0:T(1,128)S(1)} %bitcast.2, f32[512,128]{1,0:T(8,128)S(1)} %copy-done), custom_call_target="tpu_custom_call" | custom-call | tf_op jit(solution)/shard_map/masking_first/pallas_call | solution.py:29
  2.9 1.3 %collective-permute-start = (f32[256,128]{1,0:T(8,128)S(1)}, f32[256,128]{1,0:T(8,128)S(1)}, u32[]{:S(2)}, u32[]{:S(2)}) collective-permute-start(f32[256,128]{1,0:T(8,128)S(1)} %masking_first.1), channel_id=1, source_target_pairs={{2,10},{3,11},{6,14},{7,15},{8,0},{9,1},{12,4},{13,5},{18,26},{19,... | collective-permute-start | bytes 393224 | tf_op jit(solution)/shard_map/cross0/ppermute | solution.py:221
  4.2 1.3 %collective-permute-start.1 = (f32[256,128]{1,0:T(8,128)S(1)}, f32[256,128]{1,0:T(8,128)S(1)}, u32[]{:S(2)}, u32[]{:S(2)}) collective-permute-start(f32[256,128]{1,0:T(8,128)S(1)} %masking_first.1), channel_id=1, source_target_pairs={{2,0},{3,4},{6,1},{7,5},{8,10},{9,14},{12,11},{13,15},{18,16},{19,... | collective-permute-start | bytes 393224 | tf_op jit(solution)/shard_map/direct0/ppermute | solution.py:221
  5.5 5.1 %collective-permute-done = f32[256,128]{1,0:T(8,128)S(1)} collective-permute-done((f32[256,128]{1,0:T(8,128)S(1)}, f32[256,128]{1,0:T(8,128)S(1)}, u32[]{:S(2)}, u32[]{:S(2)}) %collective-permute-start) | collective-permute-done | bytes 131104 | tf_op jit(solution)/shard_map/cross0/ppermute | solution.py:221
  10.7 4.3 %collective-permute-start.5 = (f32[256,128]{1,0:T(8,128)S(1)}, f32[256,128]{1,0:T(8,128)S(1)}, u32[]{:S(2)}, u32[]{:S(2)}) collective-permute-start(f32[256,128]{1,0:T(8,128)S(1)} %collective-permute-done), channel_id=1, source_target_pairs={{0,2},{1,6},{4,3},{5,7},{10,8},{11,12},{14,9},{15,13},{16,18},{17,... | collective-permute-start | bytes 393224 | tf_op jit(solution)/shard_map/crossed0/ppermute | solution.py:221
  15.0 0.6 %masking.1 = (f32[512,128]{1,0:T(8,128)S(1)}, f32[256,128]{1,0:T(8,128)S(1)}) custom-call(s32[1,4]{1,0:T(1,128)S(1)} %bitcast.3, f32[512,128]{1,0:T(8,128)S(1)} %copy-done), custom_call_target="tpu_custom_call" | custom-call | tf_op jit(solution)/shard_map/masking/pallas_call | solution.py:29
  15.7 1.3 %collective-permute-start.10 = (f32[256,128]{1,0:T(8,128)S(1)}, f32[256,128]{1,0:T(8,128)S(1)}, u32[]{:S(2)}, u32[]{:S(2)}) collective-permute-start(f32[256,128]{1,0:T(8,128)S(1)} %get-tuple-element.31), channel_id=1, source_target_pairs={{2,0},{3,4},{6,1},{7,5},{8,10},{9,14},{12,11},{13,15},{18,16},{19,... | collective-permute-start | bytes 393224 | tf_op jit(solution)/shard_map/direct1/ppermute | solution.py:221
  17.0 0.7 %collective-permute-done.1 = f32[256,128]{1,0:T(8,128)S(1)} collective-permute-done((f32[256,128]{1,0:T(8,128)S(1)}, f32[256,128]{1,0:T(8,128)S(1)}, u32[]{:S(2)}, u32[]{:S(2)}) %collective-permute-start.1) | collective-permute-done | bytes 131104 | tf_op jit(solution)/shard_map/direct0/ppermute | solution.py:221
  17.7 0.7 %collective-permute-start.2 = (f32[512,128]{1,0:T(8,128)S(1)}, f32[512,128]{1,0:T(8,128)S(1)}, u32[]{:S(2)}, u32[]{:S(2)}) collective-permute-start(f32[512,128]{1,0:T(8,128)S(1)} %get-tuple-element.25.masked_ref), channel_id=1, source_target_pairs={{0,0},{1,4},{4,1},{5,5},{10,10},{11,14},{14,11},{15,15},{16,16},{1... | collective-permute-start | bytes 786440 | tf_op jit(solution)/shard_map/near_here/ppermute | solution.py:221
  18.4 3.8 %collective-permute-start.3 = (f32[512,128]{1,0:T(8,128)S(1)}, f32[512,128]{1,0:T(8,128)S(1)}, u32[]{:S(2)}, u32[]{:S(2)}) collective-permute-start(f32[512,128]{1,0:T(8,128)S(1)} %get-tuple-element.25.masked_ref), channel_id=1, source_target_pairs={{0,8},{1,12},{4,9},{5,13},{10,2},{11,6},{14,3},{15,7},{16,24},{17,... | collective-permute-start | bytes 786440 | tf_op jit(solution)/shard_map/near_across/ppermute | solution.py:221
  22.2 0.1 collective-permute-start.6
  22.3 0.2 splitting.1
  22.4 1.2 %collective-permute-done.6.other_ref = f32[256,128]{1,0:T(8,128)S(1)} collective-permute-done((f32[256,128]{1,0:T(8,128)S(1)}, f32[256,128]{1,0:T(8,128)S(1)}, u32[]{:S(2)}, u32[]{:S(2)}) %collective-permute-start.6) | collective-permute-done | bytes 131104 | tf_op jit(solution)/shard_map/cores0/ppermute | solution.py:284
  23.6 0.6 far_pair.2
  24.2 2.5 %collective-permute-start.7 = (f32[256,128]{1,0:T(8,128)S(1)}, f32[256,128]{1,0:T(8,128)S(1)}, u32[]{:S(2)}, u32[]{:S(2)}) collective-permute-start(f32[256,128]{1,0:T(8,128)S(1)} %get-tuple-element.29), channel_id=1, source_target_pairs={{0,1},{1,0},{2,3},{3,2},{4,5},{5,4},{6,7},{7,6},{8,9},{9,8},{10,11... | collective-permute-start | bytes 393224 | tf_op jit(solution)/shard_map/next0/ppermute | solution.py:284
  26.7 1.3 %collective-permute-start.11 = (f32[256,128]{1,0:T(8,128)S(1)}, f32[256,128]{1,0:T(8,128)S(1)}, u32[]{:S(2)}, u32[]{:S(2)}) collective-permute-start(f32[256,128]{1,0:T(8,128)S(1)} %collective-permute-done.10), channel_id=1, source_target_pairs={{0,8},{1,9},{4,12},{5,13},{10,2},{11,3},{14,6},{15,7},{16,24},{17,... | collective-permute-start | bytes 393224 | tf_op jit(solution)/shard_map/cross1/ppermute | solution.py:221
  28.1 5.3 %collective-permute-done.7 = f32[256,128]{1,0:T(8,128)S(1)} collective-permute-done((f32[256,128]{1,0:T(8,128)S(1)}, f32[256,128]{1,0:T(8,128)S(1)}, u32[]{:S(2)}, u32[]{:S(2)}) %collective-permute-start.7) | collective-permute-done | bytes 131104 | tf_op jit(solution)/shard_map/next0/ppermute | solution.py:284
  33.6 1.3 %collective-permute-done.12.other_ref = f32[256,128]{1,0:T(8,128)S(1)} collective-permute-done((f32[256,128]{1,0:T(8,128)S(1)}, f32[256,128]{1,0:T(8,128)S(1)}, u32[]{:S(2)}, u32[]{:S(2)}) %collective-permute-start.12) | collective-permute-done | bytes 131104 | tf_op jit(solution)/shard_map/cores1/ppermute | solution.py:284
  34.9 0.6 far_pair.3
  35.6 0.7 %near_pair.1 = (f32[512,128]{1,0:T(8,128)S(1)}, f32[512,128]{1,0:T(8,128)S(1)}) custom-call(s32[1]{0:T(128)} %bitcast.1.same_ref, bf16[512,512]{1,0:T(8,128)(2,1)S(1)} %get-tuple-element.23.high_ref, bf16[512,512]{1,0:T(8,128)(2,1)S(1)} %get-tuple-element.24.low_ref, f32[512,128]{1,0:T(8,128)S(1)} %broadcast_select_fusion.mine_ref, ...), custom_call_target="tpu_custom_call" | custom-call | tf_op jit(solution)/shard_map/near_pair/pallas_call | solution.py:29
  36.4 2.1 %collective-permute-start.8 = (f32[512,128]{1,0:T(8,128)S(1)}, f32[512,128]{1,0:T(8,128)S(1)}, u32[]{:S(2)}, u32[]{:S(2)}) collective-permute-start(f32[512,128]{1,0:T(8,128)S(1)} %get-tuple-element.30), channel_id=1, source_target_pairs={{0,1},{1,0},{2,3},{3,2},{4,5},{5,4},{6,7},{7,6},{8,9},{9,8},{10,11... | collective-permute-start | bytes 786440 | tf_op jit(solution)/shard_map/near_partial/ppermute | solution.py:284
  38.4 1.6 %collective-permute-start.9 = (f32[256,128]{1,0:T(8,128)S(1)}, f32[256,128]{1,0:T(8,128)S(1)}, u32[]{:S(2)}, u32[]{:S(2)}) collective-permute-start(f32[256,128]{1,0:T(8,128)S(1)} %add.26), channel_id=1, source_target_pairs={{0,2},{1,3},{2,0},{3,1},{4,6},{5,7},{6,4},{7,5},{8,10},{9,11},{10,... | collective-permute-start | bytes 393224 | tf_op jit(solution)/shard_map/across0/ppermute | solution.py:284
  40.1 6.1 %collective-permute-done.13 = f32[256,128]{1,0:T(8,128)S(1)} collective-permute-done((f32[256,128]{1,0:T(8,128)S(1)}, f32[256,128]{1,0:T(8,128)S(1)}, u32[]{:S(2)}, u32[]{:S(2)}) %collective-permute-start.13) | collective-permute-done | bytes 131104 | tf_op jit(solution)/shard_map/next1/ppermute | solution.py:284
  46.2 1.8 %collective-permute-done.9.far0 = f32[256,128]{1,0:T(8,128)S(1)} collective-permute-done((f32[256,128]{1,0:T(8,128)S(1)}, f32[256,128]{1,0:T(8,128)S(1)}, u32[]{:S(2)}, u32[]{:S(2)}) %collective-permute-start.9) | collective-permute-done | bytes 131104 | tf_op jit(solution)/shard_map/across0/ppermute | solution.py:284
  48.0 6.9 %collective-permute-done.14.far1 = f32[256,128]{1,0:T(8,128)S(1)} collective-permute-done((f32[256,128]{1,0:T(8,128)S(1)}, f32[256,128]{1,0:T(8,128)S(1)}, u32[]{:S(2)}, u32[]{:S(2)}) %collective-permute-start.14) | collective-permute-done | bytes 131104 | tf_op jit(solution)/shard_map/across1/ppermute | solution.py:284
  54.9 1.4 %finish.1 = (f32[512,128]{1,0:T(8,128)}, f32[128,128]{1,0:T(8,128)S(1)}) custom-call(s32[1,4]{1,0:T(1,128)S(1)} %bitcast.4, f32[512,128]{1,0:T(8,128)S(1)} %get-tuple-element.25.masked_ref, f32[512,128]{1,0:T(8,128)S(1)} %get-tuple-element.26.own, f32[512,128]{1,0:T(8,128)S(1)} %collective-permute-done.8.near, f32[256,128]{1,0:T(8,128)S(1)} %collective-permute-done.9.far0, ...), custom_call_target="tpu_custom_call" | custom-call | tf_op jit(solution)/shard_map/finish/pallas_call | solution.py:29
  56.3 1.3 %collective-permute-done.15 = f32[128,128]{1,0:T(8,128)S(1)} collective-permute-done((f32[128,128]{1,0:T(8,128)S(1)}, f32[128,128]{1,0:T(8,128)S(1)}, u32[]{:S(2)}, u32[]{:S(2)}) %collective-permute-start.15) | collective-permute-done | bytes 65568 | tf_op jit(solution)/shard_map/swap/ppermute | solution.py:284
  57.6 0.1 collective-permute-start.16
  57.7 4.2 %collective-permute-done.16 = f32[128,128]{1,0:T(8,128)S(1)} collective-permute-done((f32[128,128]{1,0:T(8,128)S(1)}, f32[128,128]{1,0:T(8,128)S(1)}, u32[]{:S(2)}, u32[]{:S(2)}) %collective-permute-start.16) | collective-permute-done | bytes 65568 | tf_op jit(solution)/shard_map/swap/ppermute | solution.py:284
  61.9 0.6 %add_add_fusion = f32[128,128]{1,0:T(8,128)} fusion(f32[128,128]{1,0:T(8,128)S(1)} %copy-done.3, f32[128,128]{1,0:T(8,128)S(1)} %add.28, f32[128,128]{1,0:T(8,128)S(1)} %collective-permute-done.16), kind=kLoop, calls=%fused_computation.1 | loop fusion | flops 32768 | bytes 262144 | tf_op jit(solution)/shard_map/add | solution.py:340
  (24 shorter events, 0.4 us)
Async XLA Ops:
  0.6 0.7 %copy-start.1 = (s32[4,1]{0,1:T(1,128)S(1)}, s32[4,1]{0,1:T(1,128)}, u32[]{:S(2)}) copy-start(s32[4,1]{0,1:T(1,128)} %param.6) | copy-start | bytes 52
  1.3 0.9 %copy-start = (f32[512,128]{1,0:T(8,128)S(1)}, f32[512,128]{1,0:T(8,128)}, u32[]{:S(2)}) copy-start(f32[512,128]{1,0:T(8,128)} %panel_ref) | copy-start | bytes 786436
  2.2 20.0 %copy-start.2 = (f32[512,512]{1,0:T(8,128)S(1)}, f32[512,512]{1,0:T(8,128)}, u32[]{:S(2)}) copy-start(f32[512,512]{1,0:T(8,128)} %a_ref) | copy-start | bytes 3145732
  2.9 7.7 %collective-permute-start = (f32[256,128]{1,0:T(8,128)S(1)}, f32[256,128]{1,0:T(8,128)S(1)}, u32[]{:S(2)}, u32[]{:S(2)}) collective-permute-start(f32[256,128]{1,0:T(8,128)S(1)} %masking_first.1), channel_id=1, source_target_pairs={{2,10},{3,11},{6,14},{7,15},{8,0},{9,1},{12,4},{13,5},{18,26},{19,... | collective-permute-start | bytes 393224 | tf_op jit(solution)/shard_map/cross0/ppermute | solution.py:221
  4.2 13.4 %collective-permute-start.1 = (f32[256,128]{1,0:T(8,128)S(1)}, f32[256,128]{1,0:T(8,128)S(1)}, u32[]{:S(2)}, u32[]{:S(2)}) collective-permute-start(f32[256,128]{1,0:T(8,128)S(1)} %masking_first.1), channel_id=1, source_target_pairs={{2,0},{3,4},{6,1},{7,5},{8,10},{9,14},{12,11},{13,15},{18,16},{19,... | collective-permute-start | bytes 393224 | tf_op jit(solution)/shard_map/direct0/ppermute | solution.py:221
  10.7 11.4 %collective-permute-start.5 = (f32[256,128]{1,0:T(8,128)S(1)}, f32[256,128]{1,0:T(8,128)S(1)}, u32[]{:S(2)}, u32[]{:S(2)}) collective-permute-start(f32[256,128]{1,0:T(8,128)S(1)} %collective-permute-done), channel_id=1, source_target_pairs={{0,2},{1,6},{4,3},{5,7},{10,8},{11,12},{14,9},{15,13},{16,18},{17,... | collective-permute-start | bytes 393224 | tf_op jit(solution)/shard_map/crossed0/ppermute | solution.py:221
  15.7 11.0 %collective-permute-start.10 = (f32[256,128]{1,0:T(8,128)S(1)}, f32[256,128]{1,0:T(8,128)S(1)}, u32[]{:S(2)}, u32[]{:S(2)}) collective-permute-start(f32[256,128]{1,0:T(8,128)S(1)} %get-tuple-element.31), channel_id=1, source_target_pairs={{2,0},{3,4},{6,1},{7,5},{8,10},{9,14},{12,11},{13,15},{18,16},{19,... | collective-permute-start | bytes 393224 | tf_op jit(solution)/shard_map/direct1/ppermute | solution.py:221
  17.7 10.3 %collective-permute-start.2 = (f32[512,128]{1,0:T(8,128)S(1)}, f32[512,128]{1,0:T(8,128)S(1)}, u32[]{:S(2)}, u32[]{:S(2)}) collective-permute-start(f32[512,128]{1,0:T(8,128)S(1)} %get-tuple-element.25.masked_ref), channel_id=1, source_target_pairs={{0,0},{1,4},{4,1},{5,5},{10,10},{11,14},{14,11},{15,15},{16,16},{1... | collective-permute-start | bytes 786440 | tf_op jit(solution)/shard_map/near_here/ppermute | solution.py:221
  18.4 9.7 %collective-permute-start.3 = (f32[512,128]{1,0:T(8,128)S(1)}, f32[512,128]{1,0:T(8,128)S(1)}, u32[]{:S(2)}, u32[]{:S(2)}) collective-permute-start(f32[512,128]{1,0:T(8,128)S(1)} %get-tuple-element.25.masked_ref), channel_id=1, source_target_pairs={{0,8},{1,12},{4,9},{5,13},{10,2},{11,6},{14,3},{15,7},{16,24},{17,... | collective-permute-start | bytes 786440 | tf_op jit(solution)/shard_map/near_across/ppermute | solution.py:221
  22.2 1.4 %collective-permute-start.6 = (f32[256,128]{1,0:T(8,128)S(1)}, f32[256,128]{1,0:T(8,128)S(1)}, u32[]{:S(2)}, u32[]{:S(2)}) collective-permute-start(f32[256,128]{1,0:T(8,128)S(1)} %broadcast_select_fusion.2.mine_ref), channel_id=1, source_target_pairs={{0,4},{4,0},{8,12},{12,8},{1,5},{5,1},{9,13},{13,9},{2,6},{6,2},{1... | collective-permute-start | bytes 393224 | tf_op jit(solution)/shard_map/cores0/ppermute | solution.py:284
  24.2 9.3 %collective-permute-start.7 = (f32[256,128]{1,0:T(8,128)S(1)}, f32[256,128]{1,0:T(8,128)S(1)}, u32[]{:S(2)}, u32[]{:S(2)}) collective-permute-start(f32[256,128]{1,0:T(8,128)S(1)} %get-tuple-element.29), channel_id=1, source_target_pairs={{0,1},{1,0},{2,3},{3,2},{4,5},{5,4},{6,7},{7,6},{8,9},{9,8},{10,11... | collective-permute-start | bytes 393224 | tf_op jit(solution)/shard_map/next0/ppermute | solution.py:284
  26.7 6.8 %collective-permute-start.11 = (f32[256,128]{1,0:T(8,128)S(1)}, f32[256,128]{1,0:T(8,128)S(1)}, u32[]{:S(2)}, u32[]{:S(2)}) collective-permute-start(f32[256,128]{1,0:T(8,128)S(1)} %collective-permute-done.10), channel_id=1, source_target_pairs={{0,8},{1,9},{4,12},{5,13},{10,2},{11,3},{14,6},{15,7},{16,24},{17,... | collective-permute-start | bytes 393224 | tf_op jit(solution)/shard_map/cross1/ppermute | solution.py:221
  28.1 7.5 %collective-permute-start.4 = (f32[512,128]{1,0:T(8,128)S(1)}, f32[512,128]{1,0:T(8,128)S(1)}, u32[]{:S(2)}, u32[]{:S(2)}) collective-permute-start(f32[512,128]{1,0:T(8,128)S(1)} %broadcast_select_fusion.mine_ref), channel_id=1, source_target_pairs={{0,4},{4,0},{8,12},{12,8},{1,5},{5,1},{9,13},{13,9},{2,6},{6,2},{1... | collective-permute-start | bytes 786440 | tf_op jit(solution)/shard_map/near_cores/ppermute | solution.py:284
  33.5 1.4 %collective-permute-start.12 = (f32[256,128]{1,0:T(8,128)S(1)}, f32[256,128]{1,0:T(8,128)S(1)}, u32[]{:S(2)}, u32[]{:S(2)}) collective-permute-start(f32[256,128]{1,0:T(8,128)S(1)} %broadcast_select_fusion.1.mine_ref), channel_id=1, source_target_pairs={{0,4},{4,0},{8,12},{12,8},{1,5},{5,1},{9,13},{13,9},{2,6},{6,2},{1... | collective-permute-start | bytes 393224 | tf_op jit(solution)/shard_map/cores1/ppermute | solution.py:284
  35.5 10.6 %collective-permute-start.13 = (f32[256,128]{1,0:T(8,128)S(1)}, f32[256,128]{1,0:T(8,128)S(1)}, u32[]{:S(2)}, u32[]{:S(2)}) collective-permute-start(f32[256,128]{1,0:T(8,128)S(1)} %get-tuple-element.35), channel_id=1, source_target_pairs={{0,1},{1,0},{2,3},{3,2},{4,5},{5,4},{6,7},{7,6},{8,9},{9,8},{10,11... | collective-permute-start | bytes 393224 | tf_op jit(solution)/shard_map/next1/ppermute | solution.py:284
  36.4 18.5 %collective-permute-start.8 = (f32[512,128]{1,0:T(8,128)S(1)}, f32[512,128]{1,0:T(8,128)S(1)}, u32[]{:S(2)}, u32[]{:S(2)}) collective-permute-start(f32[512,128]{1,0:T(8,128)S(1)} %get-tuple-element.30), channel_id=1, source_target_pairs={{0,1},{1,0},{2,3},{3,2},{4,5},{5,4},{6,7},{7,6},{8,9},{9,8},{10,11... | collective-permute-start | bytes 786440 | tf_op jit(solution)/shard_map/near_partial/ppermute | solution.py:284
  38.4 9.6 %collective-permute-start.9 = (f32[256,128]{1,0:T(8,128)S(1)}, f32[256,128]{1,0:T(8,128)S(1)}, u32[]{:S(2)}, u32[]{:S(2)}) collective-permute-start(f32[256,128]{1,0:T(8,128)S(1)} %add.26), channel_id=1, source_target_pairs={{0,2},{1,3},{2,0},{3,1},{4,6},{5,7},{6,4},{7,5},{8,10},{9,11},{10,... | collective-permute-start | bytes 393224 | tf_op jit(solution)/shard_map/across0/ppermute | solution.py:284
  46.2 8.7 %collective-permute-start.14 = (f32[256,128]{1,0:T(8,128)S(1)}, f32[256,128]{1,0:T(8,128)S(1)}, u32[]{:S(2)}, u32[]{:S(2)}) collective-permute-start(f32[256,128]{1,0:T(8,128)S(1)} %add.27), channel_id=1, source_target_pairs={{0,2},{1,3},{2,0},{3,1},{4,6},{5,7},{6,4},{7,5},{8,10},{9,11},{10,... | collective-permute-start | bytes 393224 | tf_op jit(solution)/shard_map/across1/ppermute | solution.py:284
  56.3 5.6 %copy-start.3 = (f32[128,128]{1,0:T(8,128)S(1)}, f32[128,128]{1,0:T(8,128)}, u32[]{:S(2)}) copy-start(f32[128,128]{1,0:T(8,128)} %param.7) | copy-start | bytes 196612
  56.3 1.3 %collective-permute-start.15 = (f32[128,128]{1,0:T(8,128)S(1)}, f32[128,128]{1,0:T(8,128)S(1)}, u32[]{:S(2)}, u32[]{:S(2)}) collective-permute-start(f32[128,128]{1,0:T(8,128)S(1)} %get-tuple-element.37), channel_id=1, source_target_pairs={{0,4},{4,0},{8,12},{12,8},{1,5},{5,1},{9,13},{13,9},{2,6},{6,2},{1... | collective-permute-start | bytes 196616 | tf_op jit(solution)/shard_map/swap/ppermute | solution.py:284
  57.6 4.3 %collective-permute-start.16 = (f32[128,128]{1,0:T(8,128)S(1)}, f32[128,128]{1,0:T(8,128)S(1)}, u32[]{:S(2)}, u32[]{:S(2)}) collective-permute-start(f32[128,128]{1,0:T(8,128)S(1)} %add.28), channel_id=1, source_target_pairs={{0,8},{4,12},{8,0},{12,4},{1,9},{5,13},{9,1},{13,5},{2,10},{6,14},... | collective-permute-start | bytes 196616 | tf_op jit(solution)/shard_map/swap/ppermute | solution.py:284

commit v5 on v2

v5 whole, which is shorter than its diff:
```python
import functools

import jax
import jax.numpy as jnp
from jax import lax
from jax.experimental import pallas as pl
from jax.experimental.pallas import tpu as pltpu
from jax.sharding import PartitionSpec as P

GRID = ("row", "col")
VMEM = pl.BlockSpec(memory_space=pltpu.VMEM)
SMEM = pl.BlockSpec(memory_space=pltpu.SMEM)
F32 = jnp.float32
ROWS = ((0,), (0,))
INNER = ((1,), (0,))


def split(x):
    high = x.astype(jnp.bfloat16)
    return high, (x - high.astype(F32)).astype(jnp.bfloat16)


def dot(a, b, dims):
    return lax.dot_general(a, b, (dims, ((), ())), preferred_element_type=F32)


def call(body, ins, outs, args, grant, name, flops=None):
    return pl.pallas_call(
        body,
        out_shape=[jax.ShapeDtypeStruct(shape, dtype) for shape, dtype in outs],
        in_specs=ins,
        out_specs=[VMEM] * len(outs),
        compiler_params=pltpu.CompilerParams(vmem_limit_bytes=grant << 20),
        cost_estimate=flops
        and pl.CostEstimate(flops=flops, bytes_accessed=0, transcendentals=0),
        name=name,
    )(*args)


def masking(mask_ref, panel_ref, out_ref):
    supers, blocks = mask_ref.shape
    tall, wide = panel_ref.shape[0] // blocks, panel_ref.shape[1] // supers
    for b in range(blocks):
        for s in range(supers):
            at = (slice(b * tall, (b + 1) * tall), slice(s * wide, (s + 1) * wide))
            out_ref[at] = panel_ref[at] * mask_ref[s, b].astype(F32)


def splitting(a_ref, high_ref, low_ref):
    high_ref[...], low_ref[...] = split(a_ref[...])


def product(ah, al, m):
    mh, ml = split(m)
    width = m.shape[1]
    first = dot(ah, jnp.concatenate([mh, ml], axis=1), INNER)
    return first[:, :width] + (first[:, width:] + dot(al, mh, INNER))


def products(count, shift_ref, high_ref, low_ref, *refs):
    panels, outs = refs[:count], refs[count:]
    ah, al = high_ref[...], low_ref[...]
    shift = shift_ref[0]
    for i in range(count):
        m = panels[0][...]
        for j in range(1, count):
            m = jnp.where(shift == (i ^ j), panels[j][...], m)
        outs[i][...] = product(ah, al, m)


def block_product(high_ref, low_ref, held_ref, sent_ref, out_ref):
    out_ref[...] = product(high_ref[...], low_ref[...], held_ref[...] + sent_ref[...])


def finish(width, mask_ref, masked_ref, *refs):
    parts, g_ref, quad_ref = refs[:-2], refs[-2], refs[-1]
    total = parts[0][...]
    for part in parts[1:]:
        total = total + part[...]
    supers, blocks = mask_ref.shape
    tall = total.shape[0] // blocks
    for b in range(blocks):
        for s in range(supers):
            at = (slice(b * tall, (b + 1) * tall), slice(s * width, (s + 1) * width))
            g_ref[at] = total[at] * -mask_ref[s, b].astype(F32)
    for s in range(supers):
        cols = slice(s * width, (s + 1) * width)
        mh, ml = split(masked_ref[:, cols])
        gh, gl = split(g_ref[:, cols])
        quad_ref[cols, :] = -(dot(mh, gh, ROWS) + (dot(mh, gl, ROWS) + dot(ml, gh, ROWS)))


def gather_any(side, masked, halves, swap):
    rows, cols = masked.shape
    turned = lax.ppermute(
        masked, GRID, [(r * side + c, c * side + r) for r in range(side) for c in range(side)]
    )
    turned, *halves = lax.optimization_barrier((turned, *halves))
    panels = {0: turned}
    bit = side // 2
    while bit:
        for j, x in list(panels.items()):
            panels[j ^ bit] = swap(x, "row", bit)
        bit //= 2
    shift = jnp.bitwise_xor(lax.axis_index("row"), lax.axis_index("col"))
    partials = call(
        functools.partial(products, side),
        [SMEM] + [VMEM] * (2 + side),
        [((rows, cols), F32)] * side,
        (shift.astype(jnp.int32).reshape(1), *halves, *[panels[j] for j in range(side)]),
        48,
        "products",
    )
    return [partials[0]] + [swap(partials[i], "col", i) for i in range(1, side)]


def move(x, name, pairs):
    with jax.named_scope(name):
        return lax.ppermute(x, GRID, [(4 * r + c, 4 * r2 + c2) for (r, c), (r2, c2) in pairs])


def after(x, *others):
    return lax.optimization_barrier((x, *others))[0]


def pinned(x_ref, out_ref):
    del x_ref, out_ref


def pin(x, flops):
    return pl.pallas_call(
        pinned,
        out_shape=jax.ShapeDtypeStruct(x.shape, x.dtype),
        in_specs=[VMEM],
        out_specs=VMEM,
        input_output_aliases={0: 0},
        compiler_params=pltpu.CompilerParams(vmem_limit_bytes=4 << 20),
        cost_estimate=pl.CostEstimate(flops=flops, bytes_accessed=1, transcendentals=0),
        name="pinned",
    )(x)


def gather_four(masked, matrix, halved, swap):
    root = lax.axis_index("row") == lax.axis_index("col")

    def to_root(x, j):
        return move(x, f"root{j}", [((r, r ^ j), (r, r)) for r in range(4)])

    def cross(x, j):
        return move(x, f"cross{j}", [((r, r), (r ^ 2, r)) for r in range(4)])

    def cores(x, j):
        return move(x, f"cores{j}", [((r ^ i, r), (r ^ i ^ 1, r)) for r in range(4) for i in (0, 2)])

    def partial(held, j):
        return call(
            block_product,
            [VMEM] * 4,
            [(held.shape, F32)],
            (*halves, held, cores(held, j)),
            8,
            f"block{j}",
        )[0]

    root3 = to_root(masked, 3)
    root2 = to_root(masked, 2)
    halves = halved(after(matrix, masked))
    held3 = root3 + cross(root3, 3)
    three = partial(held3, 3)
    first = swap(three, "col", 1, "first")
    root2 = pin(root2, 5_000_000_000)
    root2 = after(root2, three)
    held2 = root2 + cross(root2, 2)
    two = partial(held2, 2)
    total = two + pin(first, 50_000_000_000)
    far = pin(swap(total, "col", 2, "second"), 5_000_000_000)
    near_panel = after(masked, *halves)
    root1 = pin(to_root(near_panel, 1), 5_000_000_000)
    one = partial(root1 + cross(after(root1, held2), 1), 1)
    near = swap(after(one, total), "col", 1, "near")
    own = partial(jnp.where(root, masked, pin(cross(after(masked, *halves), 0), 5_000_000_000)), 0)
    return [own, near, far]


def on_device(side, inverse_blocks, lower_panel, struct_mask, diag_inverse):
    width = diag_inverse.shape[1]
    rows, cols = lower_panel.shape

    def swap(x, axis, bit, name="swap"):
        with jax.named_scope(name):
            return lax.ppermute(x, axis, [(i, i ^ bit) for i in range(side)])

    mask = struct_mask.T
    whole = ((rows, cols), F32)
    (masked,) = call(masking, [SMEM, VMEM], [whole], (mask, lower_panel), 4, "masking")

    def halved(matrix):
        return call(
            splitting,
            [VMEM],
            [(matrix.shape, jnp.bfloat16)] * 2,
            (matrix,),
            8,
            "splitting",
            20_000_000_000,
        )

    if side == 4:
        arrived = gather_four(masked, inverse_blocks, halved, swap)
    else:
        arrived = gather_any(side, masked, halved(inverse_blocks), swap)

    g_panel, quad = call(
        functools.partial(finish, width),
        [SMEM] + [VMEM] * (1 + len(arrived)),
        [whole, ((cols, width), F32)],
        (mask, masked, *arrived),
        16,
        "finish",
    )
    bit = 1
    while bit < side:
        quad = quad + swap(quad, "row", bit)
        bit *= 2
    return g_panel, diag_inverse + quad


def solution(mesh):
    side = mesh.shape["row"]
    assert side == mesh.shape["col"] and side & (side - 1) == 0
    placed = (
        P(("pole", "row"), "col"),
        P(("pole", "row"), "col"),
        P("row", "col"),
        P(("pole", "col"), None),
    )
    return jax.shard_map(
        functools.partial(on_device, side),
        mesh=mesh,
        in_specs=placed,
        out_specs=(P(("pole", "row"), "col"), P(("pole", "col"), None)),
        check_vma=False,
    )
```

time: 65.1 us -> 70.3 us (1.080)
  waiting for transfers between devices: 24.5 us -> 29.9 us
  Pallas kernels: 6.55 us -> 3.83 us
  starting transfers between devices: 30.2 us -> 31.7 us
  local copies, waits for them, and re-layouts: 2.1 us -> 2.82 us
    ppermute x3 -> x11, starting transfers between devices: 5.17 us -> 22.8 us  [move(): lax.ppermute(x, GRID, [(4 * r + c, 4 * r2 + c2) for (r, c), (r2, c2) in p...]
    ppermute x7 -> x5, starting transfers between devices: 25.1 us -> 8.87 us  [swap(): return lax.ppermute(x, axis, [(i, i ^ bit) for i in range(side)])]
    ppermute x3 -> x11, waiting for transfers between devices: 3.11 us -> 15.9 us  [move(): lax.ppermute(x, GRID, [(4 * r + c, 4 * r2 + c2) for (r, c), (r2, c2) in p...]
    ppermute x7 -> x5, waiting for transfers between devices: 21.4 us -> 14 us  [swap(): return lax.ppermute(x, axis, [(i, i ^ bit) for i in range(side)])]
    pallas_call x4 -> x12, Pallas kernels: 6.55 us -> 3.83 us  [the longest x7 3.82 us: call(): pl.pallas_call(body, out_shape=[jax.ShapeDtypeStruct(shape, dtype) for sh...]
    unnamed x10 -> x8, local copies, waits for them, and re-layouts: 2.1 us -> 2.82 us
  transfers between devices with their start and end apart: 10 -> 16, of which waited for: 7 -> 8; matrix products, arithmetic and copies ran while one was open for 0% -> 0% of each run, Pallas kernels for 4% -> 3%
where the time goes in v5:
time: 70.3 us; the launch traced here: 69.9 us
  starting transfers between devices  31.7 us (45%)
  waiting for transfers between devices  29.9 us (43%)
  Pallas kernels  3.83 us (5%)
  local copies, waits for them, and re-layouts  2.82 us (4%)
  between operations  0.91 us (1%)
  other arithmetic  0.82 us (1%)
    ppermute x11, starting transfers between devices, move(): lax.ppermute(x, GRID, [(4 * r + c, 4 * r2 + c2) for (r, c), (r2, c2) in p...  22.8 us
    ppermute x11, waiting for transfers between devices, move(): lax.ppermute(x, GRID, [(4 * r + c, 4 * r2 + c2) for (r, c), (r2, c2) in p...  15.9 us
    ppermute x5, waiting for transfers between devices, swap(): return lax.ppermute(x, axis, [(i, i ^ bit) for i in range(side)])  14 us
    ppermute x5, starting transfers between devices, swap(): return lax.ppermute(x, axis, [(i, i ^ bit) for i in range(side)])  8.87 us
    pallas_call x7, Pallas kernels, call(): pl.pallas_call(body, out_shape=[jax.ShapeDtypeStruct(shape, dtype) for sh...  3.82 us
    unnamed x8, local copies, waits for them, and re-layouts  2.82 us
  transfers between devices with their start and end apart: 16, of which 8 were waited for; matrix products, arithmetic and copies ran while one was open for 0% of the time, Pallas kernels for 3%

profile of v5, /device:TPU:0, one launch (start us, length us, event | category | flops | bytes accessed | tf_op | source)
XLA Modules:
  0.0 69.9 jit_solution(9230815332510542213)
XLA Ops:
  0.6 0.6 copy-done.1
  1.3 0.9 %copy-done = f32[512,128]{1,0:T(8,128)S(1)} copy-done((f32[512,128]{1,0:T(8,128)S(1)}, f32[512,128]{1,0:T(8,128)}, u32[]{:S(2)}) %copy-start) | copy-done | bytes 262168
  2.2 0.6 masking.1.masked_ref
  2.8 1.3 %collective-permute-start.4 = (f32[512,128]{1,0:T(8,128)S(1)}, f32[512,128]{1,0:T(8,128)S(1)}, u32[]{:S(2)}, u32[]{:S(2)}) collective-permute-start(f32[512,128]{1,0:T(8,128)S(1)} %masking.1.masked_ref), channel_id=1, source_target_pairs={{3,0},{6,5},{9,10},{12,15},{19,16},{22,21},{25,26},{28,31}} | collective-permute-start | bytes 786440 | tf_op jit(solution)/shard_map/root3/ppermute | solution.py:119
  4.1 1.3 %collective-permute-start.3 = (f32[512,128]{1,0:T(8,128)S(1)}, f32[512,128]{1,0:T(8,128)S(1)}, u32[]{:S(2)}, u32[]{:S(2)}) collective-permute-start(f32[512,128]{1,0:T(8,128)S(1)} %masking.1.masked_ref), channel_id=1, source_target_pairs={{2,0},{7,5},{8,10},{13,15},{18,16},{23,21},{24,26},{29,31}} | collective-permute-start | bytes 786440 | tf_op jit(solution)/shard_map/root2/ppermute | solution.py:119
  5.4 9.9 %collective-permute-done.4 = f32[512,128]{1,0:T(8,128)S(1)} collective-permute-done((f32[512,128]{1,0:T(8,128)S(1)}, f32[512,128]{1,0:T(8,128)S(1)}, u32[]{:S(2)}, u32[]{:S(2)}) %collective-permute-start.4) | collective-permute-done | bytes 262176 | tf_op jit(solution)/shard_map/root3/ppermute | solution.py:119
  15.3 1.3 %collective-permute-start.5 = (f32[512,128]{1,0:T(8,128)S(1)}, f32[512,128]{1,0:T(8,128)S(1)}, u32[]{:S(2)}, u32[]{:S(2)}) collective-permute-start(f32[512,128]{1,0:T(8,128)S(1)} %collective-permute-done.4), channel_id=1, source_target_pairs={{0,8},{5,13},{10,2},{15,7},{16,24},{21,29},{26,18},{31,23}} | collective-permute-start | bytes 786440 | tf_op jit(solution)/shard_map/cross3/ppermute | solution.py:119
  16.6 1.2 %copy-done.2 = f32[512,512]{1,0:T(8,128)S(1)} copy-done((f32[512,512]{1,0:T(8,128)S(1)}, f32[512,512]{1,0:T(8,128)}, u32[]{:S(2)}) %copy-start.2) | copy-done | bytes 1048600
  17.8 0.1 splitting.1
  18.0 1.3 %collective-permute-start.2 = (f32[512,128]{1,0:T(8,128)S(1)}, f32[512,128]{1,0:T(8,128)S(1)}, u32[]{:S(2)}, u32[]{:S(2)}) collective-permute-start(f32[512,128]{1,0:T(8,128)S(1)} %masking.1.masked_ref), channel_id=1, source_target_pairs={{1,0},{4,5},{11,10},{14,15},{17,16},{20,21},{27,26},{30,31}} | collective-permute-start | bytes 786440 | tf_op jit(solution)/shard_map/root1/ppermute | solution.py:119
  19.3 1.3 %collective-permute-start = (f32[512,128]{1,0:T(8,128)S(1)}, f32[512,128]{1,0:T(8,128)S(1)}, u32[]{:S(2)}, u32[]{:S(2)}) collective-permute-start(f32[512,128]{1,0:T(8,128)S(1)} %masking.1.masked_ref), channel_id=1, source_target_pairs={{0,8},{5,13},{10,2},{15,7},{16,24},{21,29},{26,18},{31,23}} | collective-permute-start | bytes 786440 | tf_op jit(solution)/shard_map/cross0/ppermute | solution.py:119
  20.6 6.7 %collective-permute-start.6 = (f32[512,128]{1,0:T(8,128)S(1)}, f32[512,128]{1,0:T(8,128)S(1)}, u32[]{:S(2)}, u32[]{:S(2)}) collective-permute-start(f32[512,128]{1,0:T(8,128)S(1)} %add.21.held_ref), channel_id=1, source_target_pairs={{0,4},{8,12},{5,1},{13,9},{10,14},{2,6},{15,11},{7,3},{16,20},{24,... | collective-permute-start | bytes 786440 | tf_op jit(solution)/shard_map/cores3/ppermute | solution.py:119
  27.4 1.1 %collective-permute-done.6.sent_ref = f32[512,128]{1,0:T(8,128)S(1)} collective-permute-done((f32[512,128]{1,0:T(8,128)S(1)}, f32[512,128]{1,0:T(8,128)S(1)}, u32[]{:S(2)}, u32[]{:S(2)}) %collective-permute-start.6) | collective-permute-done | bytes 262176 | tf_op jit(solution)/shard_map/cores3/ppermute | solution.py:119
  28.5 0.5 block3.1
  28.9 1.3 %collective-permute-start.7 = (f32[512,128]{1,0:T(8,128)S(1)}, f32[512,128]{1,0:T(8,128)S(1)}, u32[]{:S(2)}, u32[]{:S(2)}) collective-permute-start(f32[512,128]{1,0:T(8,128)S(1)} %pinned.7), channel_id=1, source_target_pairs={{0,8},{5,13},{10,2},{15,7},{16,24},{21,29},{26,18},{31,23}} | collective-permute-start | bytes 786440 | tf_op jit(solution)/shard_map/cross2/ppermute | solution.py:119
  30.3 3.8 %collective-permute-done.7 = f32[512,128]{1,0:T(8,128)S(1)} collective-permute-done((f32[512,128]{1,0:T(8,128)S(1)}, f32[512,128]{1,0:T(8,128)S(1)}, u32[]{:S(2)}, u32[]{:S(2)}) %collective-permute-start.7) | collective-permute-done | bytes 262176 | tf_op jit(solution)/shard_map/cross2/ppermute | solution.py:119
  34.1 4.4 %collective-permute-start.8 = (f32[512,128]{1,0:T(8,128)S(1)}, f32[512,128]{1,0:T(8,128)S(1)}, u32[]{:S(2)}, u32[]{:S(2)}) collective-permute-start(f32[512,128]{1,0:T(8,128)S(1)} %pinned.6), channel_id=1, source_target_pairs={{0,8},{5,13},{10,2},{15,7},{16,24},{21,29},{26,18},{31,23}} | collective-permute-start | bytes 786440 | tf_op jit(solution)/shard_map/cross1/ppermute | solution.py:119
  38.6 1.3 %collective-permute-start.1 = (f32[512,128]{1,0:T(8,128)S(1)}, f32[512,128]{1,0:T(8,128)S(1)}, u32[]{:S(2)}, u32[]{:S(2)}) collective-permute-start(f32[512,128]{1,0:T(8,128)S(1)} %broadcast_select_fusion.held_ref), channel_id=1, source_target_pairs={{0,4},{8,12},{5,1},{13,9},{10,14},{2,6},{15,11},{7,3},{16,20},{24,... | collective-permute-start | bytes 786440 | tf_op jit(solution)/shard_map/cores0/ppermute | solution.py:119
  39.9 1.3 %collective-permute-start.10 = (f32[512,128]{1,0:T(8,128)S(1)}, f32[512,128]{1,0:T(8,128)S(1)}, u32[]{:S(2)}, u32[]{:S(2)}) collective-permute-start(f32[512,128]{1,0:T(8,128)S(1)} %add.22.held_ref), channel_id=1, source_target_pairs={{0,4},{8,12},{5,1},{13,9},{10,14},{2,6},{15,11},{7,3},{16,20},{24,... | collective-permute-start | bytes 786440 | tf_op jit(solution)/shard_map/cores2/ppermute | solution.py:119
  41.2 1.2 %collective-permute-done.8 = f32[512,128]{1,0:T(8,128)S(1)} collective-permute-done((f32[512,128]{1,0:T(8,128)S(1)}, f32[512,128]{1,0:T(8,128)S(1)}, u32[]{:S(2)}, u32[]{:S(2)}) %collective-permute-start.8) | collective-permute-done | bytes 262176 | tf_op jit(solution)/shard_map/cross1/ppermute | solution.py:119
  42.4 1.3 %collective-permute-start.9 = (f32[512,128]{1,0:T(8,128)S(1)}, f32[512,128]{1,0:T(8,128)S(1)}, u32[]{:S(2)}, u32[]{:S(2)}) collective-permute-start(f32[512,128]{1,0:T(8,128)S(1)} %add.23.held_ref), channel_id=1, source_target_pairs={{0,4},{8,12},{5,1},{13,9},{10,14},{2,6},{15,11},{7,3},{16,20},{24,... | collective-permute-start | bytes 786440 | tf_op jit(solution)/shard_map/cores1/ppermute | solution.py:119
  43.8 0.5 block2.1
  44.3 6.9 %collective-permute-start.13 = (f32[512,128]{1,0:T(8,128)S(1)}, f32[512,128]{1,0:T(8,128)S(1)}, u32[]{:S(2)}, u32[]{:S(2)}) collective-permute-start(f32[512,128]{1,0:T(8,128)S(1)} %add.24), channel_id=1, source_target_pairs={{0,2},{1,3},{2,0},{3,1},{4,6},{5,7},{6,4},{7,5},{8,10},{9,11},{10,... | collective-permute-start | bytes 786440 | tf_op jit(solution)/shard_map/second/ppermute | solution.py:191
  51.2 0.5 block0.1.refs_0_
  51.7 0.5 block1.1
  52.2 6.4 %collective-permute-done.13.x_ref = f32[512,128]{1,0:T(8,128)S(1)} collective-permute-done((f32[512,128]{1,0:T(8,128)S(1)}, f32[512,128]{1,0:T(8,128)S(1)}, u32[]{:S(2)}, u32[]{:S(2)}) %collective-permute-start.13) | collective-permute-done | bytes 262176 | tf_op jit(solution)/shard_map/second/ppermute | solution.py:191
  58.6 3.7 %collective-permute-done.12.refs_1_ = f32[512,128]{1,0:T(8,128)S(1)} collective-permute-done((f32[512,128]{1,0:T(8,128)S(1)}, f32[512,128]{1,0:T(8,128)S(1)}, u32[]{:S(2)}, u32[]{:S(2)}) %collective-permute-start.12) | collective-permute-done | bytes 262176 | tf_op jit(solution)/shard_map/near/ppermute | solution.py:191
  62.4 1.3 %finish.1 = (f32[512,128]{1,0:T(8,128)}, f32[128,128]{1,0:T(8,128)S(1)}) custom-call(s32[1,4]{1,0:T(1,128)S(1)} %bitcast.2, f32[512,128]{1,0:T(8,128)S(1)} %masking.1.masked_ref, f32[512,128]{1,0:T(8,128)S(1)} %block0.1.refs_0_, f32[512,128]{1,0:T(8,128)S(1)} %collective-permute-done.12.refs_1_, f32[512,128]{1,0:T(8,128)S(1)} %pinned.9.refs_2_), custom_call_target="tpu_custom_call" | custom-call | tf_op jit(solution)/shard_map/finish/pallas_call | solution.py:28
  63.7 1.3 %collective-permute-done.14 = f32[128,128]{1,0:T(8,128)S(1)} collective-permute-done((f32[128,128]{1,0:T(8,128)S(1)}, f32[128,128]{1,0:T(8,128)S(1)}, u32[]{:S(2)}, u32[]{:S(2)}) %collective-permute-start.14) | collective-permute-done | bytes 65568 | tf_op jit(solution)/shard_map/swap/ppermute | solution.py:191
  65.0 1.8 %collective-permute-start.15 = (f32[128,128]{1,0:T(8,128)S(1)}, f32[128,128]{1,0:T(8,128)S(1)}, u32[]{:S(2)}, u32[]{:S(2)}) collective-permute-start(f32[128,128]{1,0:T(8,128)S(1)} %add.25), channel_id=1, source_target_pairs={{0,8},{4,12},{8,0},{12,4},{1,9},{5,13},{9,1},{13,5},{2,10},{6,14},... | collective-permute-start | bytes 196616 | tf_op jit(solution)/shard_map/swap/ppermute | solution.py:191
  66.8 2.5 %collective-permute-done.15 = f32[128,128]{1,0:T(8,128)S(1)} collective-permute-done((f32[128,128]{1,0:T(8,128)S(1)}, f32[128,128]{1,0:T(8,128)S(1)}, u32[]{:S(2)}, u32[]{:S(2)}) %collective-permute-start.15) | collective-permute-done | bytes 65568 | tf_op jit(solution)/shard_map/swap/ppermute | solution.py:191
  69.3 0.6 add_add_fusion
  (27 shorter events, 0.4 us)
Async XLA Ops:
  0.6 0.7 copy-start.1
  1.3 0.9 %copy-start = (f32[512,128]{1,0:T(8,128)S(1)}, f32[512,128]{1,0:T(8,128)}, u32[]{:S(2)}) copy-start(f32[512,128]{1,0:T(8,128)} %panel_ref.1) | copy-start | bytes 786436
  2.8 12.5 %collective-permute-start.4 = (f32[512,128]{1,0:T(8,128)S(1)}, f32[512,128]{1,0:T(8,128)S(1)}, u32[]{:S(2)}, u32[]{:S(2)}) collective-permute-start(f32[512,128]{1,0:T(8,128)S(1)} %masking.1.masked_ref), channel_id=1, source_target_pairs={{3,0},{6,5},{9,10},{12,15},{19,16},{22,21},{25,26},{28,31}} | collective-permute-start | bytes 786440 | tf_op jit(solution)/shard_map/root3/ppermute | solution.py:119
  4.1 23.2 %collective-permute-start.3 = (f32[512,128]{1,0:T(8,128)S(1)}, f32[512,128]{1,0:T(8,128)S(1)}, u32[]{:S(2)}, u32[]{:S(2)}) collective-permute-start(f32[512,128]{1,0:T(8,128)S(1)} %masking.1.masked_ref), channel_id=1, source_target_pairs={{2,0},{7,5},{8,10},{13,15},{18,16},{23,21},{24,26},{29,31}} | collective-permute-start | bytes 786440 | tf_op jit(solution)/shard_map/root2/ppermute | solution.py:119
  15.3 5.3 %collective-permute-start.5 = (f32[512,128]{1,0:T(8,128)S(1)}, f32[512,128]{1,0:T(8,128)S(1)}, u32[]{:S(2)}, u32[]{:S(2)}) collective-permute-start(f32[512,128]{1,0:T(8,128)S(1)} %collective-permute-done.4), channel_id=1, source_target_pairs={{0,8},{5,13},{10,2},{15,7},{16,24},{21,29},{26,18},{31,23}} | collective-permute-start | bytes 786440 | tf_op jit(solution)/shard_map/cross3/ppermute | solution.py:119
  16.6 1.2 %copy-start.2 = (f32[512,512]{1,0:T(8,128)S(1)}, f32[512,512]{1,0:T(8,128)}, u32[]{:S(2)}) copy-start(f32[512,512]{1,0:T(8,128)} %a_ref) | copy-start | bytes 3145732
  18.0 12.3 %collective-permute-start.2 = (f32[512,128]{1,0:T(8,128)S(1)}, f32[512,128]{1,0:T(8,128)S(1)}, u32[]{:S(2)}, u32[]{:S(2)}) collective-permute-start(f32[512,128]{1,0:T(8,128)S(1)} %masking.1.masked_ref), channel_id=1, source_target_pairs={{1,0},{4,5},{11,10},{14,15},{17,16},{20,21},{27,26},{30,31}} | collective-permute-start | bytes 786440 | tf_op jit(solution)/shard_map/root1/ppermute | solution.py:119
  19.3 19.3 %collective-permute-start = (f32[512,128]{1,0:T(8,128)S(1)}, f32[512,128]{1,0:T(8,128)S(1)}, u32[]{:S(2)}, u32[]{:S(2)}) collective-permute-start(f32[512,128]{1,0:T(8,128)S(1)} %masking.1.masked_ref), channel_id=1, source_target_pairs={{0,8},{5,13},{10,2},{15,7},{16,24},{21,29},{26,18},{31,23}} | collective-permute-start | bytes 786440 | tf_op jit(solution)/shard_map/cross0/ppermute | solution.py:119
  20.6 7.8 %collective-permute-start.6 = (f32[512,128]{1,0:T(8,128)S(1)}, f32[512,128]{1,0:T(8,128)S(1)}, u32[]{:S(2)}, u32[]{:S(2)}) collective-permute-start(f32[512,128]{1,0:T(8,128)S(1)} %add.21.held_ref), channel_id=1, source_target_pairs={{0,4},{8,12},{5,1},{13,9},{10,14},{2,6},{15,11},{7,3},{16,20},{24,... | collective-permute-start | bytes 786440 | tf_op jit(solution)/shard_map/cores3/ppermute | solution.py:119
  28.9 5.2 %collective-permute-start.7 = (f32[512,128]{1,0:T(8,128)S(1)}, f32[512,128]{1,0:T(8,128)S(1)}, u32[]{:S(2)}, u32[]{:S(2)}) collective-permute-start(f32[512,128]{1,0:T(8,128)S(1)} %pinned.7), channel_id=1, source_target_pairs={{0,8},{5,13},{10,2},{15,7},{16,24},{21,29},{26,18},{31,23}} | collective-permute-start | bytes 786440 | tf_op jit(solution)/shard_map/cross2/ppermute | solution.py:119
  30.3 13.5 %collective-permute-start.11 = (f32[512,128]{1,0:T(8,128)S(1)}, f32[512,128]{1,0:T(8,128)S(1)}, u32[]{:S(2)}, u32[]{:S(2)}) collective-permute-start(f32[512,128]{1,0:T(8,128)S(1)} %block3.1), channel_id=1, source_target_pairs={{0,1},{1,0},{2,3},{3,2},{4,5},{5,4},{6,7},{7,6},{8,9},{9,8},{10,11... | collective-permute-start | bytes 786440 | tf_op jit(solution)/shard_map/first/ppermute | solution.py:191
  34.1 8.3 %collective-permute-start.8 = (f32[512,128]{1,0:T(8,128)S(1)}, f32[512,128]{1,0:T(8,128)S(1)}, u32[]{:S(2)}, u32[]{:S(2)}) collective-permute-start(f32[512,128]{1,0:T(8,128)S(1)} %pinned.6), channel_id=1, source_target_pairs={{0,8},{5,13},{10,2},{15,7},{16,24},{21,29},{26,18},{31,23}} | collective-permute-start | bytes 786440 | tf_op jit(solution)/shard_map/cross1/ppermute | solution.py:119
  38.6 12.6 %collective-permute-start.1 = (f32[512,128]{1,0:T(8,128)S(1)}, f32[512,128]{1,0:T(8,128)S(1)}, u32[]{:S(2)}, u32[]{:S(2)}) collective-permute-start(f32[512,128]{1,0:T(8,128)S(1)} %broadcast_select_fusion.held_ref), channel_id=1, source_target_pairs={{0,4},{8,12},{5,1},{13,9},{10,14},{2,6},{15,11},{7,3},{16,20},{24,... | collective-permute-start | bytes 786440 | tf_op jit(solution)/shard_map/cores0/ppermute | solution.py:119
  39.9 3.9 %collective-permute-start.10 = (f32[512,128]{1,0:T(8,128)S(1)}, f32[512,128]{1,0:T(8,128)S(1)}, u32[]{:S(2)}, u32[]{:S(2)}) collective-permute-start(f32[512,128]{1,0:T(8,128)S(1)} %add.22.held_ref), channel_id=1, source_target_pairs={{0,4},{8,12},{5,1},{13,9},{10,14},{2,6},{15,11},{7,3},{16,20},{24,... | collective-permute-start | bytes 786440 | tf_op jit(solution)/shard_map/cores2/ppermute | solution.py:119
  42.4 9.2 %collective-permute-start.9 = (f32[512,128]{1,0:T(8,128)S(1)}, f32[512,128]{1,0:T(8,128)S(1)}, u32[]{:S(2)}, u32[]{:S(2)}) collective-permute-start(f32[512,128]{1,0:T(8,128)S(1)} %add.23.held_ref), channel_id=1, source_target_pairs={{0,4},{8,12},{5,1},{13,9},{10,14},{2,6},{15,11},{7,3},{16,20},{24,... | collective-permute-start | bytes 786440 | tf_op jit(solution)/shard_map/cores1/ppermute | solution.py:119
  44.3 14.4 %collective-permute-start.13 = (f32[512,128]{1,0:T(8,128)S(1)}, f32[512,128]{1,0:T(8,128)S(1)}, u32[]{:S(2)}, u32[]{:S(2)}) collective-permute-start(f32[512,128]{1,0:T(8,128)S(1)} %add.24), channel_id=1, source_target_pairs={{0,2},{1,3},{2,0},{3,1},{4,6},{5,7},{6,4},{7,5},{8,10},{9,11},{10,... | collective-permute-start | bytes 786440 | tf_op jit(solution)/shard_map/second/ppermute | solution.py:191
  52.1 10.3 %collective-permute-start.12 = (f32[512,128]{1,0:T(8,128)S(1)}, f32[512,128]{1,0:T(8,128)S(1)}, u32[]{:S(2)}, u32[]{:S(2)}) collective-permute-start(f32[512,128]{1,0:T(8,128)S(1)} %block1.1), channel_id=1, source_target_pairs={{0,1},{1,0},{2,3},{3,2},{4,5},{5,4},{6,7},{7,6},{8,9},{9,8},{10,11... | collective-permute-start | bytes 786440 | tf_op jit(solution)/shard_map/near/ppermute | solution.py:191
  63.7 5.6 %copy-start.3 = (f32[128,128]{1,0:T(8,128)S(1)}, f32[128,128]{1,0:T(8,128)}, u32[]{:S(2)}) copy-start(f32[128,128]{1,0:T(8,128)} %param.7) | copy-start | bytes 196612
  63.7 1.3 %collective-permute-start.14 = (f32[128,128]{1,0:T(8,128)S(1)}, f32[128,128]{1,0:T(8,128)S(1)}, u32[]{:S(2)}, u32[]{:S(2)}) collective-permute-start(f32[128,128]{1,0:T(8,128)S(1)} %get-tuple-element.19), channel_id=1, source_target_pairs={{0,4},{4,0},{8,12},{12,8},{1,5},{5,1},{9,13},{13,9},{2,6},{6,2},{1... | collective-permute-start | bytes 196616 | tf_op jit(solution)/shard_map/swap/ppermute | solution.py:191
  65.0 4.3 %collective-permute-start.15 = (f32[128,128]{1,0:T(8,128)S(1)}, f32[128,128]{1,0:T(8,128)S(1)}, u32[]{:S(2)}, u32[]{:S(2)}) collective-permute-start(f32[128,128]{1,0:T(8,128)S(1)} %add.25), channel_id=1, source_target_pairs={{0,8},{4,12},{8,0},{12,4},{1,9},{5,13},{9,1},{13,5},{2,10},{6,14},... | collective-permute-start | bytes 196616 | tf_op jit(solution)/shard_map/swap/ppermute | solution.py:191

commit v6 on v3

--- a/solution.py
+++ b/solution.py
@@ -175,24 +175,50 @@
     return ((1 - x, t), 2 * h + l) if x == h else None
 
 
+def pinned(x_ref, out_ref):
+    del x_ref, out_ref
+
+
+def pin(x, flops):
+    return pl.pallas_call(
+        pinned,
+        out_shape=jax.ShapeDtypeStruct(x.shape, x.dtype),
+        in_specs=[VMEM],
+        out_specs=VMEM,
+        input_output_aliases={0: 0},
+        compiler_params=pltpu.CompilerParams(vmem_limit_bytes=4 << 20),
+        cost_estimate=pl.CostEstimate(flops=flops, bytes_accessed=1, transcendentals=0),
+        name="pinned",
+    )(x)
+
+
+def move(x, rule, name):
+    with jax.named_scope(name):
+        return lax.ppermute(x, GRID, route(rule))
+
+
+def after(x, *others):
+    return lax.optimization_barrier((x, *others))[0]
+
+
 def gather_four(masked, top, low, inverse_blocks, halved, swap):
     rows, cols = masked.shape
     row, col = lax.axis_index("row"), lax.axis_index("col")
     near_side = (row // 2) == (col // 2)
     same = ((row % 2) == (col % 2)).astype(jnp.int32).reshape(1)
 
-    low_crossed = lax.ppermute(low, GRID, route(cross_early))
-    top_moved = lax.ppermute(top, GRID, route(far_direct))
+    low_crossed = move(low, cross_early, "low_crossed")
+    top_moved = move(top, far_direct, "top_moved")
     low_next = jnp.where(near_side, low_crossed, low)
-    low_moved = lax.ppermute(low_next, GRID, route(far_both))
-    near = lax.ppermute(lax.optimization_barrier((masked, low_next))[0], GRID, route(near_here))
-    halves = halved(lax.optimization_barrier((inverse_blocks, low_next))[0])
-    top_next, *halves = lax.optimization_barrier((top_moved, *halves))
-    top_crossed = lax.ppermute(top_next, GRID, route(cross_late))
+    low_moved = pin(move(low_next, far_both, "low_moved"), 100_000_000_000)
+    near = move(after(masked, low_next), near_here, "near_here")
+    halves = halved(after(inverse_blocks, low_next))
+    top_next = after(top_moved, *halves)
+    top_crossed = move(top_next, cross_late, "top_crossed")
     far = jnp.concatenate([jnp.where(near_side, top_moved, top_crossed), low_moved])
     near = jnp.where(near_side, near, jnp.concatenate([top_moved, low_crossed]))
-    far_other = swap(far, "row", 1)
-    near_other = swap(near, "row", 1)
+    far_other = swap(far, "row", 1, "far_cores")
+    near_other = swap(near, "row", 1, "near_cores")
 
     half = ((rows // 2, cols), F32)
     far2a, far2b, far3a, far3b = call(
@@ -206,18 +232,21 @@
         12,
         "near_pair",
     )
-    first = swap(far3a, "col", 1)
-    second = swap(far3b, "col", 1)
-    near1 = swap(near1, "col", 1)
-    return [own, near1, swap(far2a + first, "col", 2), swap(far2b + second, "col", 2)]
+    sum_a = far2a + swap(far3a, "col", 1, "next_a")
+    sum_b = far2b + swap(far3b, "col", 1, "next_b")
+    far_a = pin(swap(sum_a, "col", 2, "across_a"), 3_000_000_000)
+    far_b = swap(sum_b, "col", 2, "across_b")
+    near1 = swap(after(near1, sum_b), "col", 1, "near_partial")
+    return [own, near1, far_a, far_b]
 
 
 def on_device(side, inverse_blocks, lower_panel, struct_mask, diag_inverse):
     width = diag_inverse.shape[1]
     rows, cols = lower_panel.shape
 
-    def swap(x, axis, bit):
-        return lax.ppermute(x, axis, [(i, i ^ bit) for i in range(side)])
+    def swap(x, axis, bit, name="swap"):
+        with jax.named_scope(name):
+            return lax.ppermute(x, axis, [(i, i ^ bit) for i in range(side)])
 
     mask = struct_mask.T
     blocks = struct_mask.shape[0]

time: 56.7 us -> 58.5 us (1.032)
  starting transfers between devices: 11.5 us -> 20.1 us
  waiting for transfers between devices: 37.9 us -> 31 us
    ppermute x9, starting transfers between devices: 5.69 us -> 11.4 us  [swap(): return lax.ppermute(x, axis, [(i, i ^ bit) for i in range(side)])]
    ppermute x5, waiting for transfers between devices: 16.3 us -> 10.5 us  [move(): return lax.ppermute(x, GRID, route(rule))]
    ppermute x5, starting transfers between devices: 5.78 us -> 8.67 us  [move(): return lax.ppermute(x, GRID, route(rule))]
    ppermute x9, waiting for transfers between devices: 21.6 us -> 20.4 us  [swap(): return lax.ppermute(x, axis, [(i, i ^ bit) for i in range(side)])]
where the time goes in v6:
time: 58.5 us; the launch traced here: 58.3 us
  waiting for transfers between devices  31 us (53%)
  starting transfers between devices  20.1 us (34%)
  Pallas kernels  4.05 us (7%)
  local copies, waits for them, and re-layouts  1.61 us (3%)
  between operations  0.78 us (1%)
  other arithmetic  0.76 us (1%)
    ppermute x9, waiting for transfers between devices, swap(): return lax.ppermute(x, axis, [(i, i ^ bit) for i in range(side)])  20.4 us
    ppermute x9, starting transfers between devices, swap(): return lax.ppermute(x, axis, [(i, i ^ bit) for i in range(side)])  11.4 us
    ppermute x5, waiting for transfers between devices, move(): return lax.ppermute(x, GRID, route(rule))  10.5 us
    ppermute x5, starting transfers between devices, move(): return lax.ppermute(x, GRID, route(rule))  8.67 us
    pallas_call x6, Pallas kernels, call(): pl.pallas_call(body, out_shape=[jax.ShapeDtypeStruct(shape, dtype) for sh...  4.05 us
    unnamed x8, local copies, waits for them, and re-layouts  1.61 us
  transfers between devices with their start and end apart: 14, of which 10 were waited for; matrix products, arithmetic and copies ran while one was open for 0% of the time, Pallas kernels for 4%

profile of v6, /device:TPU:0, one launch (start us, length us, event | category | flops | bytes accessed | tf_op | source)
XLA Modules:
  0.0 58.3 jit_solution(14081989975887949179)
XLA Ops:
  0.6 0.6 %copy-done.1 = s32[4,1]{0,1:T(1,128)S(1)} copy-done((s32[4,1]{0,1:T(1,128)S(1)}, s32[4,1]{0,1:T(1,128)}, u32[]{:S(2)}) %copy-start.1) | copy-done | bytes 40
  1.3 0.9 %copy-done = f32[512,128]{1,0:T(8,128)S(1)} copy-done((f32[512,128]{1,0:T(8,128)S(1)}, f32[512,128]{1,0:T(8,128)}, u32[]{:S(2)}) %copy-start) | copy-done | bytes 262168
  2.2 0.6 masking.3
  2.8 3.0 %collective-permute-start = (f32[256,128]{1,0:T(8,128)S(1)}, f32[256,128]{1,0:T(8,128)S(1)}, u32[]{:S(2)}, u32[]{:S(2)}) collective-permute-start(f32[256,128]{1,0:T(8,128)S(1)} %masking.3), channel_id=1, source_target_pairs={{0,8},{1,12},{2,10},{3,11},{4,9},{5,13},{6,14},{7,15},{8,0},{9,1},... | collective-permute-start | bytes 393224 | tf_op jit(solution)/shard_map/low_crossed/ppermute | solution.py:197
  5.8 0.6 masking.2
  6.4 0.1 collective-permute-start.2
  6.5 4.6 %collective-permute-done = f32[256,128]{1,0:T(8,128)S(1)} collective-permute-done((f32[256,128]{1,0:T(8,128)S(1)}, f32[256,128]{1,0:T(8,128)S(1)}, u32[]{:S(2)}, u32[]{:S(2)}) %collective-permute-start) | collective-permute-done | bytes 131104 | tf_op jit(solution)/shard_map/low_crossed/ppermute | solution.py:197
  11.1 3.6 %collective-permute-start.5 = (f32[256,128]{1,0:T(8,128)S(1)}, f32[256,128]{1,0:T(8,128)S(1)}, u32[]{:S(2)}, u32[]{:S(2)}) collective-permute-start(f32[256,128]{1,0:T(8,128)S(1)} %broadcast_select_fusion.1), channel_id=1, source_target_pairs={{0,2},{1,6},{2,0},{3,4},{4,3},{5,7},{6,1},{7,5},{8,10},{9,14},{10,... | collective-permute-start | bytes 393224 | tf_op jit(solution)/shard_map/low_moved/ppermute | solution.py:197
  14.8 0.2 splitting.1
  14.9 4.1 %collective-permute-done.2 = f32[256,128]{1,0:T(8,128)S(1)} collective-permute-done((f32[256,128]{1,0:T(8,128)S(1)}, f32[256,128]{1,0:T(8,128)S(1)}, u32[]{:S(2)}, u32[]{:S(2)}) %collective-permute-start.2) | collective-permute-done | bytes 131104 | tf_op jit(solution)/shard_map/top_moved/ppermute | solution.py:197
  19.0 1.3 %collective-permute-start.4 = (f32[256,128]{1,0:T(8,128)S(1)}, f32[256,128]{1,0:T(8,128)S(1)}, u32[]{:S(2)}, u32[]{:S(2)}) collective-permute-start(f32[256,128]{1,0:T(8,128)S(1)} %collective-permute-done.2), channel_id=1, source_target_pairs={{0,8},{1,9},{4,12},{5,13},{10,2},{11,3},{14,6},{15,7},{16,24},{17,... | collective-permute-start | bytes 393224 | tf_op jit(solution)/shard_map/top_crossed/ppermute | solution.py:197
  20.3 0.7 %collective-permute-start.1 = (f32[512,128]{1,0:T(8,128)S(1)}, f32[512,128]{1,0:T(8,128)S(1)}, u32[]{:S(2)}, u32[]{:S(2)}) collective-permute-start(f32[512,128]{1,0:T(8,128)S(1)} %get-tuple-element.22.masked_ref), channel_id=1, source_target_pairs={{0,0},{1,4},{4,1},{5,5},{10,10},{11,14},{14,11},{15,15},{16,16},{1... | collective-permute-start | bytes 786440 | tf_op jit(solution)/shard_map/near_here/ppermute | solution.py:197
  21.0 1.8 %collective-permute-done.4 = f32[256,128]{1,0:T(8,128)S(1)} collective-permute-done((f32[256,128]{1,0:T(8,128)S(1)}, f32[256,128]{1,0:T(8,128)S(1)}, u32[]{:S(2)}, u32[]{:S(2)}) %collective-permute-start.4) | collective-permute-done | bytes 131104 | tf_op jit(solution)/shard_map/top_crossed/ppermute | solution.py:197
  22.9 1.5 %collective-permute-start.6 = (f32[512,128]{1,0:T(8,128)S(1)}, f32[512,128]{1,0:T(8,128)S(1)}, u32[]{:S(2)}, u32[]{:S(2)}) collective-permute-start(f32[512,128]{1,0:T(8,128)S(1)} %pad_maximum_fusion.mine_ref), channel_id=1, source_target_pairs={{0,4},{4,0},{8,12},{12,8},{1,5},{5,1},{9,13},{13,9},{2,6},{6,2},{1... | collective-permute-start | bytes 786440 | tf_op jit(solution)/shard_map/far_cores/ppermute | solution.py:249
  24.4 4.0 %collective-permute-start.3 = (f32[512,128]{1,0:T(8,128)S(1)}, f32[512,128]{1,0:T(8,128)S(1)}, u32[]{:S(2)}, u32[]{:S(2)}) collective-permute-start(f32[512,128]{1,0:T(8,128)S(1)} %maximum_select_fusion.mine_ref), channel_id=1, source_target_pairs={{0,4},{4,0},{8,12},{12,8},{1,5},{5,1},{9,13},{13,9},{2,6},{6,2},{1... | collective-permute-start | bytes 786440 | tf_op jit(solution)/shard_map/near_cores/ppermute | solution.py:249
  28.3 0.7 %far_pair.1 = (f32[256,128]{1,0:T(8,128)S(1)}, f32[256,128]{1,0:T(8,128)S(1)}, f32[256,128]{1,0:T(8,128)S(1)}, f32[256,128]{1,0:T(8,128)S(1)}) custom-call(s32[1]{0:T(128)} %bitcast.1.same_ref, bf16[512,512]{1,0:T(8,128)(2,1)S(1)} %get-tuple-element.20.high_ref, bf16[512,512]{1,0:T(8,128)(2,1)S(1)} %get-tuple-element.21.low_ref, ...), custom_call_target="tpu_custom_call" | custom-call | tf_op jit(solution)/shard_map/far_pair/pallas_call | solution.py:28
  29.0 1.7 %collective-permute-start.9 = (f32[256,128]{1,0:T(8,128)S(1)}, f32[256,128]{1,0:T(8,128)S(1)}, u32[]{:S(2)}, u32[]{:S(2)}) collective-permute-start(f32[256,128]{1,0:T(8,128)S(1)} %get-tuple-element.31), channel_id=1, source_target_pairs={{0,1},{1,0},{2,3},{3,2},{4,5},{5,4},{6,7},{7,6},{8,9},{9,8},{10,11... | collective-permute-start | bytes 393224 | tf_op jit(solution)/shard_map/next_a/ppermute | solution.py:249
  30.7 0.4 collective-permute-start.7
  31.1 4.3 %collective-permute-done.9 = f32[256,128]{1,0:T(8,128)S(1)} collective-permute-done((f32[256,128]{1,0:T(8,128)S(1)}, f32[256,128]{1,0:T(8,128)S(1)}, u32[]{:S(2)}, u32[]{:S(2)}) %collective-permute-start.9) | collective-permute-done | bytes 131104 | tf_op jit(solution)/shard_map/next_a/ppermute | solution.py:249
  35.4 0.1 collective-permute-start.10
  35.5 2.2 %collective-permute-done.7 = f32[256,128]{1,0:T(8,128)S(1)} collective-permute-done((f32[256,128]{1,0:T(8,128)S(1)}, f32[256,128]{1,0:T(8,128)S(1)}, u32[]{:S(2)}, u32[]{:S(2)}) %collective-permute-start.7) | collective-permute-done | bytes 131104 | tf_op jit(solution)/shard_map/next_b/ppermute | solution.py:249
  37.7 0.8 %collective-permute-start.11 = (f32[256,128]{1,0:T(8,128)S(1)}, f32[256,128]{1,0:T(8,128)S(1)}, u32[]{:S(2)}, u32[]{:S(2)}) collective-permute-start(f32[256,128]{1,0:T(8,128)S(1)} %add.26), channel_id=1, source_target_pairs={{0,2},{1,3},{2,0},{3,1},{4,6},{5,7},{6,4},{7,5},{8,10},{9,11},{10,... | collective-permute-start | bytes 393224 | tf_op jit(solution)/shard_map/across_b/ppermute | solution.py:249
  38.5 0.7 %near_pair.1 = (f32[512,128]{1,0:T(8,128)S(1)}, f32[512,128]{1,0:T(8,128)S(1)}) custom-call(s32[1]{0:T(128)} %bitcast.1.same_ref, bf16[512,512]{1,0:T(8,128)(2,1)S(1)} %get-tuple-element.20.high_ref, bf16[512,512]{1,0:T(8,128)(2,1)S(1)} %get-tuple-element.21.low_ref, f32[512,128]{1,0:T(8,128)S(1)} %maximum_select_fusion.mine_ref, ...), custom_call_target="tpu_custom_call" | custom-call | tf_op jit(solution)/shard_map/near_pair/pallas_call | solution.py:28
  39.3 1.7 %collective-permute-start.8 = (f32[512,128]{1,0:T(8,128)S(1)}, f32[512,128]{1,0:T(8,128)S(1)}, u32[]{:S(2)}, u32[]{:S(2)}) collective-permute-start(f32[512,128]{1,0:T(8,128)S(1)} %get-tuple-element.29), channel_id=1, source_target_pairs={{0,1},{1,0},{2,3},{3,2},{4,5},{5,4},{6,7},{7,6},{8,9},{9,8},{10,11... | collective-permute-start | bytes 786440 | tf_op jit(solution)/shard_map/near_partial/ppermute | solution.py:249
  40.9 7.0 %collective-permute-done.10.x_ref = f32[256,128]{1,0:T(8,128)S(1)} collective-permute-done((f32[256,128]{1,0:T(8,128)S(1)}, f32[256,128]{1,0:T(8,128)S(1)}, u32[]{:S(2)}, u32[]{:S(2)}) %collective-permute-start.10) | collective-permute-done | bytes 131104 | tf_op jit(solution)/shard_map/across_a/ppermute | solution.py:249
  47.9 1.4 %collective-permute-done.11.far1 = f32[256,128]{1,0:T(8,128)S(1)} collective-permute-done((f32[256,128]{1,0:T(8,128)S(1)}, f32[256,128]{1,0:T(8,128)S(1)}, u32[]{:S(2)}, u32[]{:S(2)}) %collective-permute-start.11) | collective-permute-done | bytes 131104 | tf_op jit(solution)/shard_map/across_b/ppermute | solution.py:249
  49.4 1.3 %collective-permute-done.8.near = f32[512,128]{1,0:T(8,128)S(1)} collective-permute-done((f32[512,128]{1,0:T(8,128)S(1)}, f32[512,128]{1,0:T(8,128)S(1)}, u32[]{:S(2)}, u32[]{:S(2)}) %collective-permute-start.8) | collective-permute-done | bytes 262176 | tf_op jit(solution)/shard_map/near_partial/ppermute | solution.py:249
  50.7 1.3 %finish.1 = (f32[512,128]{1,0:T(8,128)}, f32[128,128]{1,0:T(8,128)S(1)}) custom-call(s32[1,4]{1,0:T(1,128)S(1)} %bitcast.4, f32[512,128]{1,0:T(8,128)S(1)} %get-tuple-element.22.masked_ref, f32[512,128]{1,0:T(8,128)S(1)} %get-tuple-element.24.own, f32[512,128]{1,0:T(8,128)S(1)} %collective-permute-done.8.near, f32[256,128]{1,0:T(8,128)S(1)} %pinned.3.far0, ...), custom_call_target="tpu_custom_call" | custom-call | tf_op jit(solution)/shard_map/finish/pallas_call | solution.py:28
  52.0 1.3 %collective-permute-done.12 = f32[128,128]{1,0:T(8,128)S(1)} collective-permute-done((f32[128,128]{1,0:T(8,128)S(1)}, f32[128,128]{1,0:T(8,128)S(1)}, u32[]{:S(2)}, u32[]{:S(2)}) %collective-permute-start.12) | collective-permute-done | bytes 65568 | tf_op jit(solution)/shard_map/swap/ppermute | solution.py:249
  53.3 1.4 %collective-permute-start.13 = (f32[128,128]{1,0:T(8,128)S(1)}, f32[128,128]{1,0:T(8,128)S(1)}, u32[]{:S(2)}, u32[]{:S(2)}) collective-permute-start(f32[128,128]{1,0:T(8,128)S(1)} %add.28), channel_id=1, source_target_pairs={{0,8},{4,12},{8,0},{12,4},{1,9},{5,13},{9,1},{13,5},{2,10},{6,14},... | collective-permute-start | bytes 196616 | tf_op jit(solution)/shard_map/swap/ppermute | solution.py:249
  54.7 2.9 %collective-permute-done.13 = f32[128,128]{1,0:T(8,128)S(1)} collective-permute-done((f32[128,128]{1,0:T(8,128)S(1)}, f32[128,128]{1,0:T(8,128)S(1)}, u32[]{:S(2)}, u32[]{:S(2)}) %collective-permute-start.13) | collective-permute-done | bytes 65568 | tf_op jit(solution)/shard_map/swap/ppermute | solution.py:249
  57.6 0.6 %add_add_fusion = f32[128,128]{1,0:T(8,128)} fusion(f32[128,128]{1,0:T(8,128)S(1)} %copy-done.3, f32[128,128]{1,0:T(8,128)S(1)} %add.28, f32[128,128]{1,0:T(8,128)S(1)} %collective-permute-done.13), kind=kLoop, calls=%fused_computation.2 | loop fusion | flops 32768 | bytes 262144 | tf_op jit(solution)/shard_map/add | solution.py:296
  (20 shorter events, 0.1 us)
Async XLA Ops:
  0.6 0.7 %copy-start.1 = (s32[4,1]{0,1:T(1,128)S(1)}, s32[4,1]{0,1:T(1,128)}, u32[]{:S(2)}) copy-start(s32[4,1]{0,1:T(1,128)} %param.6) | copy-start | bytes 52
  1.3 0.9 %copy-start = (f32[512,128]{1,0:T(8,128)S(1)}, f32[512,128]{1,0:T(8,128)}, u32[]{:S(2)}) copy-start(f32[512,128]{1,0:T(8,128)} %panel_ref.3) | copy-start | bytes 786436
  2.2 12.5 %copy-start.2 = (f32[512,512]{1,0:T(8,128)S(1)}, f32[512,512]{1,0:T(8,128)}, u32[]{:S(2)}) copy-start(f32[512,512]{1,0:T(8,128)} %a_ref) | copy-start | bytes 3145732
  2.8 8.3 %collective-permute-start = (f32[256,128]{1,0:T(8,128)S(1)}, f32[256,128]{1,0:T(8,128)S(1)}, u32[]{:S(2)}, u32[]{:S(2)}) collective-permute-start(f32[256,128]{1,0:T(8,128)S(1)} %masking.3), channel_id=1, source_target_pairs={{0,8},{1,12},{2,10},{3,11},{4,9},{5,13},{6,14},{7,15},{8,0},{9,1},... | collective-permute-start | bytes 393224 | tf_op jit(solution)/shard_map/low_crossed/ppermute | solution.py:197
  6.4 12.7 %collective-permute-start.2 = (f32[256,128]{1,0:T(8,128)S(1)}, f32[256,128]{1,0:T(8,128)S(1)}, u32[]{:S(2)}, u32[]{:S(2)}) collective-permute-start(f32[256,128]{1,0:T(8,128)S(1)} %get-tuple-element.23), channel_id=1, source_target_pairs={{0,8},{1,12},{2,0},{3,4},{4,9},{5,13},{6,1},{7,5},{8,10},{9,14},{1... | collective-permute-start | bytes 393224 | tf_op jit(solution)/shard_map/top_moved/ppermute | solution.py:197
  11.1 9.9 %collective-permute-start.5 = (f32[256,128]{1,0:T(8,128)S(1)}, f32[256,128]{1,0:T(8,128)S(1)}, u32[]{:S(2)}, u32[]{:S(2)}) collective-permute-start(f32[256,128]{1,0:T(8,128)S(1)} %broadcast_select_fusion.1), channel_id=1, source_target_pairs={{0,2},{1,6},{2,0},{3,4},{4,3},{5,7},{6,1},{7,5},{8,10},{9,14},{10,... | collective-permute-start | bytes 393224 | tf_op jit(solution)/shard_map/low_moved/ppermute | solution.py:197
  19.0 3.8 %collective-permute-start.4 = (f32[256,128]{1,0:T(8,128)S(1)}, f32[256,128]{1,0:T(8,128)S(1)}, u32[]{:S(2)}, u32[]{:S(2)}) collective-permute-start(f32[256,128]{1,0:T(8,128)S(1)} %collective-permute-done.2), channel_id=1, source_target_pairs={{0,8},{1,9},{4,12},{5,13},{10,2},{11,3},{14,6},{15,7},{16,24},{17,... | collective-permute-start | bytes 393224 | tf_op jit(solution)/shard_map/top_crossed/ppermute | solution.py:197
  20.3 4.0 %collective-permute-start.1 = (f32[512,128]{1,0:T(8,128)S(1)}, f32[512,128]{1,0:T(8,128)S(1)}, u32[]{:S(2)}, u32[]{:S(2)}) collective-permute-start(f32[512,128]{1,0:T(8,128)S(1)} %get-tuple-element.22.masked_ref), channel_id=1, source_target_pairs={{0,0},{1,4},{4,1},{5,5},{10,10},{11,14},{14,11},{15,15},{16,16},{1... | collective-permute-start | bytes 786440 | tf_op jit(solution)/shard_map/near_here/ppermute | solution.py:197
  22.9 5.4 %collective-permute-start.6 = (f32[512,128]{1,0:T(8,128)S(1)}, f32[512,128]{1,0:T(8,128)S(1)}, u32[]{:S(2)}, u32[]{:S(2)}) collective-permute-start(f32[512,128]{1,0:T(8,128)S(1)} %pad_maximum_fusion.mine_ref), channel_id=1, source_target_pairs={{0,4},{4,0},{8,12},{12,8},{1,5},{5,1},{9,13},{13,9},{2,6},{6,2},{1... | collective-permute-start | bytes 786440 | tf_op jit(solution)/shard_map/far_cores/ppermute | solution.py:249
  24.4 14.2 %collective-permute-start.3 = (f32[512,128]{1,0:T(8,128)S(1)}, f32[512,128]{1,0:T(8,128)S(1)}, u32[]{:S(2)}, u32[]{:S(2)}) collective-permute-start(f32[512,128]{1,0:T(8,128)S(1)} %maximum_select_fusion.mine_ref), channel_id=1, source_target_pairs={{0,4},{4,0},{8,12},{12,8},{1,5},{5,1},{9,13},{13,9},{2,6},{6,2},{1... | collective-permute-start | bytes 786440 | tf_op jit(solution)/shard_map/near_cores/ppermute | solution.py:249
  29.0 6.4 %collective-permute-start.9 = (f32[256,128]{1,0:T(8,128)S(1)}, f32[256,128]{1,0:T(8,128)S(1)}, u32[]{:S(2)}, u32[]{:S(2)}) collective-permute-start(f32[256,128]{1,0:T(8,128)S(1)} %get-tuple-element.31), channel_id=1, source_target_pairs={{0,1},{1,0},{2,3},{3,2},{4,5},{5,4},{6,7},{7,6},{8,9},{9,8},{10,11... | collective-permute-start | bytes 393224 | tf_op jit(solution)/shard_map/next_a/ppermute | solution.py:249
  30.7 7.0 %collective-permute-start.7 = (f32[256,128]{1,0:T(8,128)S(1)}, f32[256,128]{1,0:T(8,128)S(1)}, u32[]{:S(2)}, u32[]{:S(2)}) collective-permute-start(f32[256,128]{1,0:T(8,128)S(1)} %get-tuple-element.28), channel_id=1, source_target_pairs={{0,1},{1,0},{2,3},{3,2},{4,5},{5,4},{6,7},{7,6},{8,9},{9,8},{10,11... | collective-permute-start | bytes 393224 | tf_op jit(solution)/shard_map/next_b/ppermute | solution.py:249
  35.4 12.5 %collective-permute-start.10 = (f32[256,128]{1,0:T(8,128)S(1)}, f32[256,128]{1,0:T(8,128)S(1)}, u32[]{:S(2)}, u32[]{:S(2)}) collective-permute-start(f32[256,128]{1,0:T(8,128)S(1)} %add.27), channel_id=1, source_target_pairs={{0,2},{1,3},{2,0},{3,1},{4,6},{5,7},{6,4},{7,5},{8,10},{9,11},{10,... | collective-permute-start | bytes 393224 | tf_op jit(solution)/shard_map/across_a/ppermute | solution.py:249
  37.7 11.6 %collective-permute-start.11 = (f32[256,128]{1,0:T(8,128)S(1)}, f32[256,128]{1,0:T(8,128)S(1)}, u32[]{:S(2)}, u32[]{:S(2)}) collective-permute-start(f32[256,128]{1,0:T(8,128)S(1)} %add.26), channel_id=1, source_target_pairs={{0,2},{1,3},{2,0},{3,1},{4,6},{5,7},{6,4},{7,5},{8,10},{9,11},{10,... | collective-permute-start | bytes 393224 | tf_op jit(solution)/shard_map/across_b/ppermute | solution.py:249
  39.3 11.4 %collective-permute-start.8 = (f32[512,128]{1,0:T(8,128)S(1)}, f32[512,128]{1,0:T(8,128)S(1)}, u32[]{:S(2)}, u32[]{:S(2)}) collective-permute-start(f32[512,128]{1,0:T(8,128)S(1)} %get-tuple-element.29), channel_id=1, source_target_pairs={{0,1},{1,0},{2,3},{3,2},{4,5},{5,4},{6,7},{7,6},{8,9},{9,8},{10,11... | collective-permute-start | bytes 786440 | tf_op jit(solution)/shard_map/near_partial/ppermute | solution.py:249
  52.0 5.6 %copy-start.3 = (f32[128,128]{1,0:T(8,128)S(1)}, f32[128,128]{1,0:T(8,128)}, u32[]{:S(2)}) copy-start(f32[128,128]{1,0:T(8,128)} %param.7) | copy-start | bytes 196612
  52.0 1.3 %collective-permute-start.12 = (f32[128,128]{1,0:T(8,128)S(1)}, f32[128,128]{1,0:T(8,128)S(1)}, u32[]{:S(2)}, u32[]{:S(2)}) collective-permute-start(f32[128,128]{1,0:T(8,128)S(1)} %get-tuple-element.33), channel_id=1, source_target_pairs={{0,4},{4,0},{8,12},{12,8},{1,5},{5,1},{9,13},{13,9},{2,6},{6,2},{1... | collective-permute-start | bytes 196616 | tf_op jit(solution)/shard_map/swap/ppermute | solution.py:249
  53.3 4.3 %collective-permute-start.13 = (f32[128,128]{1,0:T(8,128)S(1)}, f32[128,128]{1,0:T(8,128)S(1)}, u32[]{:S(2)}, u32[]{:S(2)}) collective-permute-start(f32[128,128]{1,0:T(8,128)S(1)} %add.28), channel_id=1, source_target_pairs={{0,8},{4,12},{8,0},{12,4},{1,9},{5,13},{9,1},{13,5},{2,10},{6,14},... | collective-permute-start | bytes 196616 | tf_op jit(solution)/shard_map/swap/ppermute | solution.py:249

commit v7 on v6

--- a/solution.py
+++ b/solution.py
@@ -24,12 +24,13 @@
     return lax.dot_general(a, b, (dims, ((), ())), preferred_element_type=F32)
 
 
-def call(body, ins, outs, args, grant, name, flops=None):
+def call(body, ins, outs, args, grant, name, flops=None, scratch=()):
     return pl.pallas_call(
         body,
         out_shape=[jax.ShapeDtypeStruct(shape, dtype) for shape, dtype in outs],
         in_specs=ins,
         out_specs=[VMEM] * len(outs),
+        scratch_shapes=scratch,
         compiler_params=pltpu.CompilerParams(vmem_limit_bytes=grant << 20),
         cost_estimate=flops
         and pl.CostEstimate(flops=flops, bytes_accessed=0, transcendentals=0),
@@ -101,15 +102,20 @@
                 term = ref[at : at + tall, cols]
                 total = term if total is None else total + term
             g_ref[b * tall : (b + 1) * tall, cols] = total * -mask_ref[s, b].astype(F32)
-    for s in range(supers):
+    for s in range(supers if quad_ref is not None else 0):
         cols = slice(s * width, (s + 1) * width)
         mh, ml = split(masked_ref[:, cols])
         gh, gl = split(g_ref[:, cols])
         quad_ref[cols, :] = -(dot(mh, gh, ROWS) + (dot(mh, gl, ROWS) + dot(ml, gh, ROWS)))
 
 
-def finish_paired(width, mask_ref, masked_ref, own, near, far0, far1, g_ref, quad_ref):
-    finish(width, mask_ref, masked_ref, own, near, (far0, far1), g_ref, quad_ref)
+def quad_only(width, mask_ref, masked_ref, own, near, *refs):
+    *fars, g_ref, quad_ref = refs[:-2] + (refs[-1], refs[-2])
+    finish(width, mask_ref, masked_ref, own, near, tuple(fars), g_ref, quad_ref)
+
+
+def panel_only(width, mask_ref, own, near, *refs):
+    finish(width, mask_ref, None, own, near, tuple(refs[:-1]), refs[-1], None)
 
 
 def gather_any(side, masked, halves, swap):
@@ -165,33 +171,6 @@
     return ((x, l), 2 * (1 - x) + t) if x == h else ((x, l), 2 * x + t)
 
 
-def near_here(x, t, h, l):
-    if x != h:
-        return None
-    return ((x, t), 2 * h + l) if t == l else ((x, 1 - t), 2 * h + t)
-
-
-def cross_late(x, t, h, l):
-    return ((1 - x, t), 2 * h + l) if x == h else None
-
-
-def pinned(x_ref, out_ref):
-    del x_ref, out_ref
-
-
-def pin(x, flops):
-    return pl.pallas_call(
-        pinned,
-        out_shape=jax.ShapeDtypeStruct(x.shape, x.dtype),
-        in_specs=[VMEM],
-        out_specs=VMEM,
-        input_output_aliases={0: 0},
-        compiler_params=pltpu.CompilerParams(vmem_limit_bytes=4 << 20),
-        cost_estimate=pl.CostEstimate(flops=flops, bytes_accessed=1, transcendentals=0),
-        name="pinned",
-    )(x)
-
-
 def move(x, rule, name):
     with jax.named_scope(name):
         return lax.ppermute(x, GRID, route(rule))
@@ -206,38 +185,34 @@
     row, col = lax.axis_index("row"), lax.axis_index("col")
     near_side = (row // 2) == (col // 2)
     same = ((row % 2) == (col % 2)).astype(jnp.int32).reshape(1)
+    half, whole = ((rows // 2, cols), F32), ((rows, cols), F32)
 
     low_crossed = move(low, cross_early, "low_crossed")
     top_moved = move(top, far_direct, "top_moved")
     low_next = jnp.where(near_side, low_crossed, low)
-    low_moved = pin(move(low_next, far_both, "low_moved"), 100_000_000_000)
-    near = move(after(masked, low_next), near_here, "near_here")
+    low_moved = move(low_next, far_both, "low_moved")
     halves = halved(after(inverse_blocks, low_next))
-    top_next = after(top_moved, *halves)
-    top_crossed = move(top_next, cross_late, "top_crossed")
-    far = jnp.concatenate([jnp.where(near_side, top_moved, top_crossed), low_moved])
-    near = jnp.where(near_side, near, jnp.concatenate([top_moved, low_crossed]))
+    low_flip = swap(after(low_crossed, *halves), "row", 2, "low_flip")
+    top_flip = swap(top_moved, "row", 2, "top_flip")
+    near = jnp.where(
+        near_side,
+        jnp.concatenate([top_flip, low_flip]),
+        jnp.concatenate([top_moved, low_crossed]),
+    )
+    far = jnp.concatenate([jnp.where(near_side, top_moved, top_flip), low_moved])
+    near_other = swap(near, "row", 1, "near_cores")
+
     far_other = swap(far, "row", 1, "far_cores")
-    near_other = swap(near, "row", 1, "near_cores")
-
-    half = ((rows // 2, cols), F32)
-    far2a, far2b, far3a, far3b = call(
+    outs = call(
         pair, [SMEM] + [VMEM] * 4, [half] * 4, (same, *halves, far, far_other), 12, "far_pair"
     )
+    two, three = outs[:2], outs[2:]
     own, near1 = call(
-        pair,
-        [SMEM] + [VMEM] * 4,
-        [((rows, cols), F32)] * 2,
-        (same, *halves, near, near_other),
-        12,
-        "near_pair",
-    )
-    sum_a = far2a + swap(far3a, "col", 1, "next_a")
-    sum_b = far2b + swap(far3b, "col", 1, "next_b")
-    far_a = pin(swap(sum_a, "col", 2, "across_a"), 3_000_000_000)
-    far_b = swap(sum_b, "col", 2, "across_b")
-    near1 = swap(after(near1, sum_b), "col", 1, "near_partial")
-    return [own, near1, far_a, far_b]
+        pair, [SMEM] + [VMEM] * 4, [whole] * 2, (same, *halves, near, near_other), 12, "near_pair"
+    )
+    near1 = swap(near1, "col", 1, "near_partial")
+    sums = [a + swap(b, "col", 1, "next") for a, b in zip(two, three)]
+    return [own, near1, *[swap(x, "col", 2, "across") for x in sums]]
 
 
 def on_device(side, inverse_blocks, lower_panel, struct_mask, diag_inverse):
@@ -252,13 +227,13 @@
     blocks = struct_mask.shape[0]
     four = side == 4 and blocks % 2 == 0
 
-    def masked_rows(*spans):
+    def masked_rows(*spans, grant=4):
         return call(
             functools.partial(masking, spans),
             [SMEM, VMEM],
             [((rows * (last - first) // blocks, cols), F32) for first, last in spans],
             (mask, lower_panel),
-            4,
+            grant,
             "masking",
         )
 
@@ -274,21 +249,45 @@
         )
 
     if four:
-        (low,) = masked_rows((blocks // 2, blocks))
+        (low,) = masked_rows((blocks // 2, blocks), grant=60)
         masked, top = masked_rows((0, blocks), (0, blocks // 2))
-        arrived, body = gather_four(masked, top, low, inverse_blocks, halved, swap), finish_paired
+        arrived = gather_four(masked, top, low, inverse_blocks, halved, swap)
     else:
         (masked,) = masked_rows((0, blocks))
-        arrived, body = gather_any(side, masked, halved(inverse_blocks), swap), finish
-
-    g_panel, quad = call(
-        functools.partial(body, width),
-        [SMEM] + [VMEM] * (1 + len(arrived)),
-        [((rows, cols), F32), ((cols, width), F32)],
-        (mask, masked, *arrived),
-        16,
-        "finish",
-    )
+        arrived = gather_any(side, masked, halved(inverse_blocks), swap)
+
+    if four:
+        (quad,) = call(
+            functools.partial(quad_only, width),
+            [SMEM] + [VMEM] * (1 + len(arrived)),
+            [((cols, width), F32)],
+            (mask, masked, *arrived),
+            16,
+            "quad",
+            scratch=[pltpu.VMEM((rows, cols), F32)],
+        )
+        late = lax.optimization_barrier((quad, *arrived))[1:]
+        (g_panel,) = call(
+            functools.partial(panel_only, width),
+            [SMEM] + [VMEM] * len(arrived),
+            [((rows, cols), F32)],
+            (mask, *late),
+            16,
+            "panel",
+        )
+    else:
+        g_panel, quad = call(
+            functools.partial(finish, width),
+            [SMEM] + [VMEM] * (1 + len(arrived)),
+            [((rows, cols), F32), ((cols, width), F32)],
+            (mask, masked, *arrived),
+            16,
+            "finish",
+        )
+    if four:
+        for part in [swap(quad, "row", bit, "tail") for bit in range(1, side)]:
+            quad = quad + part
+        return g_panel, diag_inverse + quad
     bit = 1
     while bit < side:
         quad = quad + swap(quad, "row", bit)

time: 58.5 us -> 53.5 us (0.915)
  waiting for transfers between devices: 31 us -> 25.3 us
  Pallas kernels: 4.05 us -> 5.97 us
  starting transfers between devices: 20.1 us -> 19.2 us
    ppermute x9 -> x12, waiting for transfers between devices: 20.4 us -> 16.3 us  [swap(): return lax.ppermute(x, axis, [(i, i ^ bit) for i in range(side)])]
    ppermute x5 -> x3, starting transfers between devices: 8.67 us -> 6.54 us  [move(): return lax.ppermute(x, GRID, route(rule))]
    pallas_call x6 -> x7, Pallas kernels: 4.05 us -> 5.97 us  [call(): pl.pallas_call(body, out_shape=[jax.ShapeDtypeStruct(shape, dtype) for sh...]
    ppermute x5 -> x3, waiting for transfers between devices: 10.5 us -> 9 us  [move(): return lax.ppermute(x, GRID, route(rule))]
    ppermute x9 -> x12, starting transfers between devices: 11.4 us -> 12.7 us  [swap(): return lax.ppermute(x, axis, [(i, i ^ bit) for i in range(side)])]
    unnamed x8 -> x10, local copies, waits for them, and re-layouts: 1.61 us -> 1.24 us
  transfers between devices with their start and end apart: 14 -> 15, of which waited for: 10 -> 9; matrix products, arithmetic and copies ran while one was open for 0% -> 0% of each run, Pallas kernels for 4% -> 6%
where the time goes in v7:
time: 53.5 us; the launch traced here: 53.3 us
  waiting for transfers between devices  25.3 us (47%)
  starting transfers between devices  19.2 us (36%)
  Pallas kernels  5.97 us (11%)
  local copies, waits for them, and re-layouts  1.24 us (2%)
  between operations  0.79 us (1%)
  other arithmetic  0.77 us (1%)
    ppermute x12, waiting for transfers between devices, swap(): return lax.ppermute(x, axis, [(i, i ^ bit) for i in range(side)])  16.3 us
    ppermute x12, starting transfers between devices, swap(): return lax.ppermute(x, axis, [(i, i ^ bit) for i in range(side)])  12.7 us
    ppermute x3, waiting for transfers between devices, move(): return lax.ppermute(x, GRID, route(rule))  9 us
    ppermute x3, starting transfers between devices, move(): return lax.ppermute(x, GRID, route(rule))  6.54 us
    pallas_call x7, Pallas kernels, call(): pl.pallas_call(body, out_shape=[jax.ShapeDtypeStruct(shape, dtype) for sh...  5.97 us
    unnamed x10, local copies, waits for them, and re-layouts  1.24 us
  transfers between devices with their start and end apart: 15, of which 9 were waited for; matrix products, arithmetic and copies ran while one was open for 0% of the time, Pallas kernels for 6%

profile of v7, /device:TPU:0, one launch (start us, length us, event | category | flops | bytes accessed | tf_op | source)
XLA Modules:
  0.0 53.3 jit_solution(12168679475729302565)
XLA Ops:
  0.6 1.7 %masking.3 = f32[256,128]{1,0:T(8,128)} custom-call(s32[1,4]{1,0:T(1,128)} %bitcast.2, f32[512,128]{1,0:T(8,128)} %panel_ref.3), custom_call_target="tpu_custom_call" | custom-call | tf_op jit(solution)/shard_map/masking/pallas_call | solution.py:28
  2.3 2.9 %collective-permute-start = (f32[256,128]{1,0:T(8,128)}, f32[256,128]{1,0:T(8,128)S(1)}, u32[]{:S(2)}, u32[]{:S(2)}) collective-permute-start(f32[256,128]{1,0:T(8,128)} %masking.3), channel_id=1, source_target_pairs={{0,8},{1,12},{2,10},{3,11},{4,9},{5,13},{6,14},{7,15},{8,0},{9,1},... | collective-permute-start | bytes 393224 | tf_op jit(solution)/shard_map/low_crossed/ppermute | solution.py:176
  5.3 0.6 %masking.2 = (f32[512,128]{1,0:T(8,128)S(1)}, f32[256,128]{1,0:T(8,128)S(1)}) custom-call(s32[1,4]{1,0:T(1,128)S(1)} %bitcast.3, f32[512,128]{1,0:T(8,128)S(1)} %copy-done), custom_call_target="tpu_custom_call" | custom-call | tf_op jit(solution)/shard_map/masking/pallas_call | solution.py:28
  5.9 0.1 collective-permute-start.1
  5.9 4.9 %collective-permute-done = f32[256,128]{1,0:T(8,128)S(1)} collective-permute-done((f32[256,128]{1,0:T(8,128)}, f32[256,128]{1,0:T(8,128)S(1)}, u32[]{:S(2)}, u32[]{:S(2)}) %collective-permute-start) | collective-permute-done | bytes 131104 | tf_op jit(solution)/shard_map/low_crossed/ppermute | solution.py:176
  10.9 3.5 %collective-permute-start.6 = (f32[256,128]{1,0:T(8,128)S(1)}, f32[256,128]{1,0:T(8,128)S(1)}, u32[]{:S(2)}, u32[]{:S(2)}) collective-permute-start(f32[256,128]{1,0:T(8,128)S(1)} %broadcast_select_fusion.1), channel_id=1, source_target_pairs={{0,2},{1,6},{2,0},{3,4},{4,3},{5,7},{6,1},{7,5},{8,10},{9,14},{10,... | collective-permute-start | bytes 393224 | tf_op jit(solution)/shard_map/low_moved/ppermute | solution.py:176
  14.4 4.1 %collective-permute-done.1 = f32[256,128]{1,0:T(8,128)S(1)} collective-permute-done((f32[256,128]{1,0:T(8,128)S(1)}, f32[256,128]{1,0:T(8,128)S(1)}, u32[]{:S(2)}, u32[]{:S(2)}) %collective-permute-start.1) | collective-permute-done | bytes 131104 | tf_op jit(solution)/shard_map/top_moved/ppermute | solution.py:176
  18.5 1.2 %copy-done.2 = f32[512,512]{1,0:T(8,128)S(1)} copy-done((f32[512,512]{1,0:T(8,128)S(1)}, f32[512,512]{1,0:T(8,128)}, u32[]{:S(2)}) %copy-start.2) | copy-done | bytes 1048600
  19.7 0.1 splitting.1
  19.9 2.1 %collective-permute-start.3 = (f32[256,128]{1,0:T(8,128)S(1)}, f32[256,128]{1,0:T(8,128)S(1)}, u32[]{:S(2)}, u32[]{:S(2)}) collective-permute-start(f32[256,128]{1,0:T(8,128)S(1)} %collective-permute-done), channel_id=1, source_target_pairs={{0,8},{4,12},{8,0},{12,4},{1,9},{5,13},{9,1},{13,5},{2,10},{6,14},... | collective-permute-start | bytes 393224 | tf_op jit(solution)/shard_map/low_flip/ppermute | solution.py:224
  22.0 1.5 %collective-permute-done.2 = f32[256,128]{1,0:T(8,128)S(1)} collective-permute-done((f32[256,128]{1,0:T(8,128)S(1)}, f32[256,128]{1,0:T(8,128)S(1)}, u32[]{:S(2)}, u32[]{:S(2)}) %collective-permute-start.2) | collective-permute-done | bytes 131104 | tf_op jit(solution)/shard_map/top_flip/ppermute | solution.py:224
  23.5 0.1 collective-permute-start.7
  23.6 1.3 %collective-permute-done.3 = f32[256,128]{1,0:T(8,128)S(1)} collective-permute-done((f32[256,128]{1,0:T(8,128)S(1)}, f32[256,128]{1,0:T(8,128)S(1)}, u32[]{:S(2)}, u32[]{:S(2)}) %collective-permute-start.3) | collective-permute-done | bytes 131104 | tf_op jit(solution)/shard_map/low_flip/ppermute | solution.py:224
  25.0 0.1 collective-permute-start.4
  25.1 0.1 collective-permute-done.7.other_ref
  25.1 0.7 %far_pair.1 = (f32[256,128]{1,0:T(8,128)S(1)}, f32[256,128]{1,0:T(8,128)S(1)}, f32[256,128]{1,0:T(8,128)S(1)}, f32[256,128]{1,0:T(8,128)S(1)}) custom-call(s32[1]{0:T(128)} %bitcast.1.same_ref, bf16[512,512]{1,0:T(8,128)(2,1)S(1)} %get-tuple-element.20.high_ref, bf16[512,512]{1,0:T(8,128)(2,1)S(1)} %get-tuple-element.21.low_ref, ...), custom_call_target="tpu_custom_call" | custom-call | tf_op jit(solution)/shard_map/far_pair/pallas_call | solution.py:28
  25.9 1.2 %collective-permute-start.8 = (f32[256,128]{1,0:T(8,128)S(1)}, f32[256,128]{1,0:T(8,128)S(1)}, u32[]{:S(2)}, u32[]{:S(2)}) collective-permute-start(f32[256,128]{1,0:T(8,128)S(1)} %get-tuple-element.27), channel_id=1, source_target_pairs={{0,1},{1,0},{2,3},{3,2},{4,5},{5,4},{6,7},{7,6},{8,9},{9,8},{10,11... | collective-permute-start | bytes 393224 | tf_op jit(solution)/shard_map/next/ppermute | solution.py:224
  27.1 0.9 %collective-permute-start.10 = (f32[256,128]{1,0:T(8,128)S(1)}, f32[256,128]{1,0:T(8,128)S(1)}, u32[]{:S(2)}, u32[]{:S(2)}) collective-permute-start(f32[256,128]{1,0:T(8,128)S(1)} %get-tuple-element.29), channel_id=1, source_target_pairs={{0,1},{1,0},{2,3},{3,2},{4,5},{5,4},{6,7},{7,6},{8,9},{9,8},{10,11... | collective-permute-start | bytes 393224 | tf_op jit(solution)/shard_map/next/ppermute | solution.py:224
  28.0 0.7 %near_pair.1 = (f32[512,128]{1,0:T(8,128)S(1)}, f32[512,128]{1,0:T(8,128)S(1)}) custom-call(s32[1]{0:T(128)} %bitcast.1.same_ref, bf16[512,512]{1,0:T(8,128)(2,1)S(1)} %get-tuple-element.20.high_ref, bf16[512,512]{1,0:T(8,128)(2,1)S(1)} %get-tuple-element.21.low_ref, f32[512,128]{1,0:T(8,128)S(1)} %maximum_select_fusion.mine_ref, ...), custom_call_target="tpu_custom_call" | custom-call | tf_op jit(solution)/shard_map/near_pair/pallas_call | solution.py:28
  28.7 1.2 %collective-permute-start.5 = (f32[512,128]{1,0:T(8,128)S(1)}, f32[512,128]{1,0:T(8,128)S(1)}, u32[]{:S(2)}, u32[]{:S(2)}) collective-permute-start(f32[512,128]{1,0:T(8,128)S(1)} %get-tuple-element.25), channel_id=1, source_target_pairs={{0,1},{1,0},{2,3},{3,2},{4,5},{5,4},{6,7},{7,6},{8,9},{9,8},{10,11... | collective-permute-start | bytes 786440 | tf_op jit(solution)/shard_map/near_partial/ppermute | solution.py:224
  29.9 2.4 %collective-permute-done.8 = f32[256,128]{1,0:T(8,128)S(1)} collective-permute-done((f32[256,128]{1,0:T(8,128)S(1)}, f32[256,128]{1,0:T(8,128)S(1)}, u32[]{:S(2)}, u32[]{:S(2)}) %collective-permute-start.8) | collective-permute-done | bytes 131104 | tf_op jit(solution)/shard_map/next/ppermute | solution.py:224
  32.2 2.1 %collective-permute-start.9 = (f32[256,128]{1,0:T(8,128)S(1)}, f32[256,128]{1,0:T(8,128)S(1)}, u32[]{:S(2)}, u32[]{:S(2)}) collective-permute-start(f32[256,128]{1,0:T(8,128)S(1)} %add.29), channel_id=1, source_target_pairs={{0,2},{1,3},{2,0},{3,1},{4,6},{5,7},{6,4},{7,5},{8,10},{9,11},{10,... | collective-permute-start | bytes 393224 | tf_op jit(solution)/shard_map/across/ppermute | solution.py:224
  34.4 0.7 %collective-permute-done.10 = f32[256,128]{1,0:T(8,128)S(1)} collective-permute-done((f32[256,128]{1,0:T(8,128)S(1)}, f32[256,128]{1,0:T(8,128)S(1)}, u32[]{:S(2)}, u32[]{:S(2)}) %collective-permute-start.10) | collective-permute-done | bytes 131104 | tf_op jit(solution)/shard_map/next/ppermute | solution.py:224
  35.1 2.1 %collective-permute-start.11 = (f32[256,128]{1,0:T(8,128)S(1)}, f32[256,128]{1,0:T(8,128)S(1)}, u32[]{:S(2)}, u32[]{:S(2)}) collective-permute-start(f32[256,128]{1,0:T(8,128)S(1)} %add.30), channel_id=1, source_target_pairs={{0,2},{1,3},{2,0},{3,1},{4,6},{5,7},{6,4},{7,5},{8,10},{9,11},{10,... | collective-permute-start | bytes 393224 | tf_op jit(solution)/shard_map/across/ppermute | solution.py:224
  37.2 8.6 %collective-permute-done.5.near = f32[512,128]{1,0:T(8,128)S(1)} collective-permute-done((f32[512,128]{1,0:T(8,128)S(1)}, f32[512,128]{1,0:T(8,128)S(1)}, u32[]{:S(2)}, u32[]{:S(2)}) %collective-permute-start.5) | collective-permute-done | bytes 262176 | tf_op jit(solution)/shard_map/near_partial/ppermute | solution.py:224
  45.8 0.8 %quad.1 = f32[128,128]{1,0:T(8,128)S(1)} custom-call(s32[1,4]{1,0:T(1,128)S(1)} %bitcast.4, f32[512,128]{1,0:T(8,128)S(1)} %get-tuple-element.18.masked_ref, f32[512,128]{1,0:T(8,128)S(1)} %get-tuple-element.30.own, f32[512,128]{1,0:T(8,128)S(1)} %collective-permute-done.5.near, f32[256,128]{1,0:T(8,128)S(1)} %collective-permute-done.9.refs_0_, ...), custom_call_target="tpu_custom_call" | custom-call | tf_op jit(solution)/shard_map/quad/pallas_call | solution.py:28
  46.7 1.2 %collective-permute-start.14 = (f32[128,128]{1,0:T(8,128)S(1)}, f32[128,128]{1,0:T(8,128)S(1)}, u32[]{:S(2)}, u32[]{:S(2)}) collective-permute-start(f32[128,128]{1,0:T(8,128)S(1)} %quad.1), channel_id=1, source_target_pairs={{0,12},{4,8},{8,4},{12,0},{1,13},{5,9},{9,5},{13,1},{2,14},{6,10},... | collective-permute-start | bytes 196616 | tf_op jit(solution)/shard_map/tail/ppermute | solution.py:224
  47.9 1.7 %collective-permute-start.13 = (f32[128,128]{1,0:T(8,128)S(1)}, f32[128,128]{1,0:T(8,128)S(1)}, u32[]{:S(2)}, u32[]{:S(2)}) collective-permute-start(f32[128,128]{1,0:T(8,128)S(1)} %quad.1), channel_id=1, source_target_pairs={{0,8},{4,12},{8,0},{12,4},{1,9},{5,13},{9,1},{13,5},{2,10},{6,14},... | collective-permute-start | bytes 196616 | tf_op jit(solution)/shard_map/tail/ppermute | solution.py:224
  49.6 0.0 collective-permute-start.12
  49.6 1.3 %panel.1 = f32[512,128]{1,0:T(8,128)} custom-call(s32[1,4]{1,0:T(1,128)S(1)} %bitcast.5, f32[512,128]{1,0:T(8,128)S(1)} %get-tuple-element.30.own, f32[512,128]{1,0:T(8,128)S(1)} %collective-permute-done.5.near, f32[256,128]{1,0:T(8,128)S(1)} %collective-permute-done.9.refs_0_, f32[256,128]{1,0:T(8,128)S(1)} %collective-permute-done.11.refs_1_), custom_call_target="tpu_custom_call" | custom-call | tf_op jit(solution)/shard_map/panel/pallas_call | solution.py:28
  50.9 1.8 %collective-permute-done.13 = f32[128,128]{1,0:T(8,128)S(1)} collective-permute-done((f32[128,128]{1,0:T(8,128)S(1)}, f32[128,128]{1,0:T(8,128)S(1)}, u32[]{:S(2)}, u32[]{:S(2)}) %collective-permute-start.13) | collective-permute-done | bytes 65568 | tf_op jit(solution)/shard_map/tail/ppermute | solution.py:224
  52.7 0.6 %add_add_fusion = f32[128,128]{1,0:T(8,128)} fusion(f32[128,128]{1,0:T(8,128)S(1)} %copy-done.4, f32[128,128]{1,0:T(8,128)S(1)} %collective-permute-done.14, f32[128,128]{1,0:T(8,128)S(1)} %collective-permute-done.13, f32[128,128]{1,0:T(8,128)S(1)} %quad.1, f32[128,128]{1,0:T(8,128)S(1)} %collective-permute-done.12), kind=kLoop, calls=%fused_computation.2 | loop fusion | flops 65536 | bytes 393216 | tf_op jit(solution)/shard_map/add | solution.py:290
  (22 shorter events, 0.2 us)
Async XLA Ops:
  0.6 4.6 %copy-start = (f32[512,128]{1,0:T(8,128)S(1)}, f32[512,128]{1,0:T(8,128)}, u32[]{:S(2)}) copy-start(f32[512,128]{1,0:T(8,128)} %panel_ref.3) | copy-start | bytes 786436
  0.6 4.6 %copy-start.1 = (s32[4,1]{0,1:T(1,128)S(1)}, s32[4,1]{0,1:T(1,128)}, u32[]{:S(2)}) copy-start(s32[4,1]{0,1:T(1,128)} %param.6) | copy-start | bytes 52
  2.3 8.6 %copy-start.3 = (f32[256,128]{1,0:T(8,128)S(1)}, f32[256,128]{1,0:T(8,128)}, u32[]{:S(2)}) copy-start(f32[256,128]{1,0:T(8,128)} %masking.3) | copy-start | bytes 393220
  2.3 8.6 %collective-permute-start = (f32[256,128]{1,0:T(8,128)}, f32[256,128]{1,0:T(8,128)S(1)}, u32[]{:S(2)}, u32[]{:S(2)}) collective-permute-start(f32[256,128]{1,0:T(8,128)} %masking.3), channel_id=1, source_target_pairs={{0,8},{1,12},{2,10},{3,11},{4,9},{5,13},{6,14},{7,15},{8,0},{9,1},... | collective-permute-start | bytes 393224 | tf_op jit(solution)/shard_map/low_crossed/ppermute | solution.py:176
  5.9 12.7 %collective-permute-start.1 = (f32[256,128]{1,0:T(8,128)S(1)}, f32[256,128]{1,0:T(8,128)S(1)}, u32[]{:S(2)}, u32[]{:S(2)}) collective-permute-start(f32[256,128]{1,0:T(8,128)S(1)} %get-tuple-element.22), channel_id=1, source_target_pairs={{0,8},{1,12},{2,0},{3,4},{4,9},{5,13},{6,1},{7,5},{8,10},{9,14},{1... | collective-permute-start | bytes 393224 | tf_op jit(solution)/shard_map/top_moved/ppermute | solution.py:176
  10.9 12.6 %collective-permute-start.6 = (f32[256,128]{1,0:T(8,128)S(1)}, f32[256,128]{1,0:T(8,128)S(1)}, u32[]{:S(2)}, u32[]{:S(2)}) collective-permute-start(f32[256,128]{1,0:T(8,128)S(1)} %broadcast_select_fusion.1), channel_id=1, source_target_pairs={{0,2},{1,6},{2,0},{3,4},{4,3},{5,7},{6,1},{7,5},{8,10},{9,14},{10,... | collective-permute-start | bytes 393224 | tf_op jit(solution)/shard_map/low_moved/ppermute | solution.py:176
  18.5 5.0 %collective-permute-start.2 = (f32[256,128]{1,0:T(8,128)S(1)}, f32[256,128]{1,0:T(8,128)S(1)}, u32[]{:S(2)}, u32[]{:S(2)}) collective-permute-start(f32[256,128]{1,0:T(8,128)S(1)} %collective-permute-done.1), channel_id=1, source_target_pairs={{0,8},{4,12},{8,0},{12,4},{1,9},{5,13},{9,1},{13,5},{2,10},{6,14},... | collective-permute-start | bytes 393224 | tf_op jit(solution)/shard_map/top_flip/ppermute | solution.py:224
  18.5 1.2 %copy-start.2 = (f32[512,512]{1,0:T(8,128)S(1)}, f32[512,512]{1,0:T(8,128)}, u32[]{:S(2)}) copy-start(f32[512,512]{1,0:T(8,128)} %a_ref) | copy-start | bytes 3145732
  19.9 5.0 %collective-permute-start.3 = (f32[256,128]{1,0:T(8,128)S(1)}, f32[256,128]{1,0:T(8,128)S(1)}, u32[]{:S(2)}, u32[]{:S(2)}) collective-permute-start(f32[256,128]{1,0:T(8,128)S(1)} %collective-permute-done), channel_id=1, source_target_pairs={{0,8},{4,12},{8,0},{12,4},{1,9},{5,13},{9,1},{13,5},{2,10},{6,14},... | collective-permute-start | bytes 393224 | tf_op jit(solution)/shard_map/low_flip/ppermute | solution.py:224
  23.5 1.6 %collective-permute-start.7 = (f32[512,128]{1,0:T(8,128)S(1)}, f32[512,128]{1,0:T(8,128)S(1)}, u32[]{:S(2)}, u32[]{:S(2)}) collective-permute-start(f32[512,128]{1,0:T(8,128)S(1)} %pad_maximum_fusion.mine_ref), channel_id=1, source_target_pairs={{0,4},{4,0},{8,12},{12,8},{1,5},{5,1},{9,13},{13,9},{2,6},{6,2},{1... | collective-permute-start | bytes 786440 | tf_op jit(solution)/shard_map/far_cores/ppermute | solution.py:224
  25.0 3.0 %collective-permute-start.4 = (f32[512,128]{1,0:T(8,128)S(1)}, f32[512,128]{1,0:T(8,128)S(1)}, u32[]{:S(2)}, u32[]{:S(2)}) collective-permute-start(f32[512,128]{1,0:T(8,128)S(1)} %maximum_select_fusion.mine_ref), channel_id=1, source_target_pairs={{0,4},{4,0},{8,12},{12,8},{1,5},{5,1},{9,13},{13,9},{2,6},{6,2},{1... | collective-permute-start | bytes 786440 | tf_op jit(solution)/shard_map/near_cores/ppermute | solution.py:224
  25.9 6.4 %collective-permute-start.8 = (f32[256,128]{1,0:T(8,128)S(1)}, f32[256,128]{1,0:T(8,128)S(1)}, u32[]{:S(2)}, u32[]{:S(2)}) collective-permute-start(f32[256,128]{1,0:T(8,128)S(1)} %get-tuple-element.27), channel_id=1, source_target_pairs={{0,1},{1,0},{2,3},{3,2},{4,5},{5,4},{6,7},{7,6},{8,9},{9,8},{10,11... | collective-permute-start | bytes 393224 | tf_op jit(solution)/shard_map/next/ppermute | solution.py:224
  27.1 8.0 %collective-permute-start.10 = (f32[256,128]{1,0:T(8,128)S(1)}, f32[256,128]{1,0:T(8,128)S(1)}, u32[]{:S(2)}, u32[]{:S(2)}) collective-permute-start(f32[256,128]{1,0:T(8,128)S(1)} %get-tuple-element.29), channel_id=1, source_target_pairs={{0,1},{1,0},{2,3},{3,2},{4,5},{5,4},{6,7},{7,6},{8,9},{9,8},{10,11... | collective-permute-start | bytes 393224 | tf_op jit(solution)/shard_map/next/ppermute | solution.py:224
  28.7 17.1 %collective-permute-start.5 = (f32[512,128]{1,0:T(8,128)S(1)}, f32[512,128]{1,0:T(8,128)S(1)}, u32[]{:S(2)}, u32[]{:S(2)}) collective-permute-start(f32[512,128]{1,0:T(8,128)S(1)} %get-tuple-element.25), channel_id=1, source_target_pairs={{0,1},{1,0},{2,3},{3,2},{4,5},{5,4},{6,7},{7,6},{8,9},{9,8},{10,11... | collective-permute-start | bytes 786440 | tf_op jit(solution)/shard_map/near_partial/ppermute | solution.py:224
  32.2 13.6 %collective-permute-start.9 = (f32[256,128]{1,0:T(8,128)S(1)}, f32[256,128]{1,0:T(8,128)S(1)}, u32[]{:S(2)}, u32[]{:S(2)}) collective-permute-start(f32[256,128]{1,0:T(8,128)S(1)} %add.29), channel_id=1, source_target_pairs={{0,2},{1,3},{2,0},{3,1},{4,6},{5,7},{6,4},{7,5},{8,10},{9,11},{10,... | collective-permute-start | bytes 393224 | tf_op jit(solution)/shard_map/across/ppermute | solution.py:224
  35.1 10.7 %collective-permute-start.11 = (f32[256,128]{1,0:T(8,128)S(1)}, f32[256,128]{1,0:T(8,128)S(1)}, u32[]{:S(2)}, u32[]{:S(2)}) collective-permute-start(f32[256,128]{1,0:T(8,128)S(1)} %add.30), channel_id=1, source_target_pairs={{0,2},{1,3},{2,0},{3,1},{4,6},{5,7},{6,4},{7,5},{8,10},{9,11},{10,... | collective-permute-start | bytes 393224 | tf_op jit(solution)/shard_map/across/ppermute | solution.py:224
  46.7 6.0 %copy-start.4 = (f32[128,128]{1,0:T(8,128)S(1)}, f32[128,128]{1,0:T(8,128)}, u32[]{:S(2)}) copy-start(f32[128,128]{1,0:T(8,128)} %param.7) | copy-start | bytes 196612
  46.7 4.2 %collective-permute-start.14 = (f32[128,128]{1,0:T(8,128)S(1)}, f32[128,128]{1,0:T(8,128)S(1)}, u32[]{:S(2)}, u32[]{:S(2)}) collective-permute-start(f32[128,128]{1,0:T(8,128)S(1)} %quad.1), channel_id=1, source_target_pairs={{0,12},{4,8},{8,4},{12,0},{1,13},{5,9},{9,5},{13,1},{2,14},{6,10},... | collective-permute-start | bytes 196616 | tf_op jit(solution)/shard_map/tail/ppermute | solution.py:224
  47.9 4.8 %collective-permute-start.13 = (f32[128,128]{1,0:T(8,128)S(1)}, f32[128,128]{1,0:T(8,128)S(1)}, u32[]{:S(2)}, u32[]{:S(2)}) collective-permute-start(f32[128,128]{1,0:T(8,128)S(1)} %quad.1), channel_id=1, source_target_pairs={{0,8},{4,12},{8,0},{12,4},{1,9},{5,13},{9,1},{13,5},{2,10},{6,14},... | collective-permute-start | bytes 196616 | tf_op jit(solution)/shard_map/tail/ppermute | solution.py:224
  49.6 3.1 %collective-permute-start.12 = (f32[128,128]{1,0:T(8,128)S(1)}, f32[128,128]{1,0:T(8,128)S(1)}, u32[]{:S(2)}, u32[]{:S(2)}) collective-permute-start(f32[128,128]{1,0:T(8,128)S(1)} %quad.1), channel_id=1, source_target_pairs={{0,4},{4,0},{8,12},{12,8},{1,5},{5,1},{9,13},{13,9},{2,6},{6,2},{1... | collective-permute-start | bytes 196616 | tf_op jit(solution)/shard_map/tail/ppermute | solution.py:224

commit v8 on v7

--- a/solution.py
+++ b/solution.py
@@ -189,11 +189,11 @@
 
     low_crossed = move(low, cross_early, "low_crossed")
     top_moved = move(top, far_direct, "top_moved")
-    low_next = jnp.where(near_side, low_crossed, low)
+    halves = halved(after(inverse_blocks, top))
+    low_next = jnp.where(near_side, after(low_crossed, *halves), low)
     low_moved = move(low_next, far_both, "low_moved")
-    halves = halved(after(inverse_blocks, low_next))
-    low_flip = swap(after(low_crossed, *halves), "row", 2, "low_flip")
     top_flip = swap(top_moved, "row", 2, "top_flip")
+    low_flip = swap(after(low_crossed, low_moved), "row", 2, "low_flip")
     near = jnp.where(
         near_side,
         jnp.concatenate([top_flip, low_flip]),

time: 53.5 us -> 53.6 us (level)
  waiting for transfers between devices: 25.3 us -> 29.9 us
  starting transfers between devices: 19.2 us -> 14.7 us
    ppermute x12, starting transfers between devices: 12.7 us -> 8.16 us  [swap(): return lax.ppermute(x, axis, [(i, i ^ bit) for i in range(side)])]
    ppermute x12, waiting for transfers between devices: 16.3 us -> 20.3 us  [swap(): return lax.ppermute(x, axis, [(i, i ^ bit) for i in range(side)])]
    ppermute x3, waiting for transfers between devices: 9 us -> 9.57 us  [move(): return lax.ppermute(x, GRID, route(rule))]
  transfers between devices with their start and end apart: 15 -> 15, of which waited for: 9 -> 12; matrix products, arithmetic and copies ran while one was open for 0% -> 0% of each run, Pallas kernels for 6% -> 6%
where the time goes in v8:
time: 53.6 us; the launch traced here: 53.4 us
  waiting for transfers between devices  29.9 us (56%)
  starting transfers between devices  14.7 us (27%)
  Pallas kernels  5.97 us (11%)
  local copies, waits for them, and re-layouts  1.24 us (2%)
  between operations  0.81 us (2%)
  other arithmetic  0.77 us (1%)
    ppermute x12, waiting for transfers between devices, swap(): return lax.ppermute(x, axis, [(i, i ^ bit) for i in range(side)])  20.3 us
    ppermute x3, waiting for transfers between devices, move(): return lax.ppermute(x, GRID, route(rule))  9.57 us
    ppermute x12, starting transfers between devices, swap(): return lax.ppermute(x, axis, [(i, i ^ bit) for i in range(side)])  8.16 us
    ppermute x3, starting transfers between devices, move(): return lax.ppermute(x, GRID, route(rule))  6.54 us
    pallas_call x7, Pallas kernels, call(): pl.pallas_call(body, out_shape=[jax.ShapeDtypeStruct(shape, dtype) for sh...  5.97 us
    unnamed x10, local copies, waits for them, and re-layouts  1.24 us
  transfers between devices with their start and end apart: 15, of which 12 were waited for; matrix products, arithmetic and copies ran while one was open for 0% of the time, Pallas kernels for 6%

profile of v8, /device:TPU:0, one launch (start us, length us, event | category | flops | bytes accessed | tf_op | source)
XLA Modules:
  0.0 53.4 jit_solution(2006801154517136425)
XLA Ops:
  0.6 1.7 %masking.3 = f32[256,128]{1,0:T(8,128)} custom-call(s32[1,4]{1,0:T(1,128)} %bitcast.2, f32[512,128]{1,0:T(8,128)} %panel_ref.3), custom_call_target="tpu_custom_call" | custom-call | tf_op jit(solution)/shard_map/masking/pallas_call | solution.py:28
  2.3 2.9 %collective-permute-start.2 = (f32[256,128]{1,0:T(8,128)}, f32[256,128]{1,0:T(8,128)S(1)}, u32[]{:S(2)}, u32[]{:S(2)}) collective-permute-start(f32[256,128]{1,0:T(8,128)} %masking.3), channel_id=1, source_target_pairs={{0,8},{1,12},{2,10},{3,11},{4,9},{5,13},{6,14},{7,15},{8,0},{9,1},... | collective-permute-start | bytes 393224 | tf_op jit(solution)/shard_map/low_crossed/ppermute | solution.py:176
  5.3 0.6 %masking.2 = (f32[512,128]{1,0:T(8,128)S(1)}, f32[256,128]{1,0:T(8,128)S(1)}) custom-call(s32[1,4]{1,0:T(1,128)S(1)} %bitcast.3, f32[512,128]{1,0:T(8,128)S(1)} %copy-done), custom_call_target="tpu_custom_call" | custom-call | tf_op jit(solution)/shard_map/masking/pallas_call | solution.py:28
  5.9 1.2 %copy-done.2 = f32[512,512]{1,0:T(8,128)S(1)} copy-done((f32[512,512]{1,0:T(8,128)S(1)}, f32[512,512]{1,0:T(8,128)}, u32[]{:S(2)}) %copy-start.2) | copy-done | bytes 1048600
  7.2 0.1 splitting.1
  7.3 3.6 %collective-permute-done.2 = f32[256,128]{1,0:T(8,128)S(1)} collective-permute-done((f32[256,128]{1,0:T(8,128)}, f32[256,128]{1,0:T(8,128)S(1)}, u32[]{:S(2)}, u32[]{:S(2)}) %collective-permute-start.2) | collective-permute-done | bytes 131104 | tf_op jit(solution)/shard_map/low_crossed/ppermute | solution.py:176
  10.9 3.5 %collective-permute-start.3 = (f32[256,128]{1,0:T(8,128)S(1)}, f32[256,128]{1,0:T(8,128)S(1)}, u32[]{:S(2)}, u32[]{:S(2)}) collective-permute-start(f32[256,128]{1,0:T(8,128)S(1)} %broadcast_select_fusion.1), channel_id=1, source_target_pairs={{0,2},{1,6},{2,0},{3,4},{4,3},{5,7},{6,1},{7,5},{8,10},{9,14},{10,... | collective-permute-start | bytes 393224 | tf_op jit(solution)/shard_map/low_moved/ppermute | solution.py:176
  14.4 4.1 %collective-permute-done = f32[256,128]{1,0:T(8,128)S(1)} collective-permute-done((f32[256,128]{1,0:T(8,128)S(1)}, f32[256,128]{1,0:T(8,128)S(1)}, u32[]{:S(2)}, u32[]{:S(2)}) %collective-permute-start) | collective-permute-done | bytes 131104 | tf_op jit(solution)/shard_map/top_moved/ppermute | solution.py:176
  18.5 2.0 %collective-permute-done.3 = f32[256,128]{1,0:T(8,128)S(1)} collective-permute-done((f32[256,128]{1,0:T(8,128)S(1)}, f32[256,128]{1,0:T(8,128)S(1)}, u32[]{:S(2)}, u32[]{:S(2)}) %collective-permute-start.3) | collective-permute-done | bytes 131104 | tf_op jit(solution)/shard_map/low_moved/ppermute | solution.py:176
  20.5 0.1 collective-permute-start.4
  20.6 2.9 %collective-permute-done.1 = f32[256,128]{1,0:T(8,128)S(1)} collective-permute-done((f32[256,128]{1,0:T(8,128)S(1)}, f32[256,128]{1,0:T(8,128)S(1)}, u32[]{:S(2)}, u32[]{:S(2)}) %collective-permute-start.1) | collective-permute-done | bytes 131104 | tf_op jit(solution)/shard_map/top_flip/ppermute | solution.py:224
  23.5 0.1 collective-permute-start.7
  23.6 1.8 %collective-permute-done.4 = f32[256,128]{1,0:T(8,128)S(1)} collective-permute-done((f32[256,128]{1,0:T(8,128)S(1)}, f32[256,128]{1,0:T(8,128)S(1)}, u32[]{:S(2)}, u32[]{:S(2)}) %collective-permute-start.4) | collective-permute-done | bytes 131104 | tf_op jit(solution)/shard_map/low_flip/ppermute | solution.py:224
  25.6 0.7 %far_pair.1 = (f32[256,128]{1,0:T(8,128)S(1)}, f32[256,128]{1,0:T(8,128)S(1)}, f32[256,128]{1,0:T(8,128)S(1)}, f32[256,128]{1,0:T(8,128)S(1)}) custom-call(s32[1]{0:T(128)} %bitcast.1.same_ref, bf16[512,512]{1,0:T(8,128)(2,1)S(1)} %get-tuple-element.22.high_ref, bf16[512,512]{1,0:T(8,128)(2,1)S(1)} %get-tuple-element.23.low_ref, ...), custom_call_target="tpu_custom_call" | custom-call | tf_op jit(solution)/shard_map/far_pair/pallas_call | solution.py:28
  26.3 0.1 collective-permute-start.8
  26.4 2.0 %collective-permute-start.10 = (f32[256,128]{1,0:T(8,128)S(1)}, f32[256,128]{1,0:T(8,128)S(1)}, u32[]{:S(2)}, u32[]{:S(2)}) collective-permute-start(f32[256,128]{1,0:T(8,128)S(1)} %get-tuple-element.31), channel_id=1, source_target_pairs={{0,1},{1,0},{2,3},{3,2},{4,5},{5,4},{6,7},{7,6},{8,9},{9,8},{10,11... | collective-permute-start | bytes 393224 | tf_op jit(solution)/shard_map/next/ppermute | solution.py:224
  28.4 0.7 %near_pair.1 = (f32[512,128]{1,0:T(8,128)S(1)}, f32[512,128]{1,0:T(8,128)S(1)}) custom-call(s32[1]{0:T(128)} %bitcast.1.same_ref, bf16[512,512]{1,0:T(8,128)(2,1)S(1)} %get-tuple-element.22.high_ref, bf16[512,512]{1,0:T(8,128)(2,1)S(1)} %get-tuple-element.23.low_ref, f32[512,128]{1,0:T(8,128)S(1)} %maximum_select_fusion.mine_ref, ...), custom_call_target="tpu_custom_call" | custom-call | tf_op jit(solution)/shard_map/near_pair/pallas_call | solution.py:28
  29.1 0.2 collective-permute-start.6
  29.3 3.4 %collective-permute-done.8 = f32[256,128]{1,0:T(8,128)S(1)} collective-permute-done((f32[256,128]{1,0:T(8,128)S(1)}, f32[256,128]{1,0:T(8,128)S(1)}, u32[]{:S(2)}, u32[]{:S(2)}) %collective-permute-start.8) | collective-permute-done | bytes 131104 | tf_op jit(solution)/shard_map/next/ppermute | solution.py:224
  32.7 1.9 %collective-permute-start.9 = (f32[256,128]{1,0:T(8,128)S(1)}, f32[256,128]{1,0:T(8,128)S(1)}, u32[]{:S(2)}, u32[]{:S(2)}) collective-permute-start(f32[256,128]{1,0:T(8,128)S(1)} %add.29), channel_id=1, source_target_pairs={{0,2},{1,3},{2,0},{3,1},{4,6},{5,7},{6,4},{7,5},{8,10},{9,11},{10,... | collective-permute-start | bytes 393224 | tf_op jit(solution)/shard_map/across/ppermute | solution.py:224
  34.5 0.9 %collective-permute-done.10 = f32[256,128]{1,0:T(8,128)S(1)} collective-permute-done((f32[256,128]{1,0:T(8,128)S(1)}, f32[256,128]{1,0:T(8,128)S(1)}, u32[]{:S(2)}, u32[]{:S(2)}) %collective-permute-start.10) | collective-permute-done | bytes 131104 | tf_op jit(solution)/shard_map/next/ppermute | solution.py:224
  35.5 1.9 %collective-permute-start.11 = (f32[256,128]{1,0:T(8,128)S(1)}, f32[256,128]{1,0:T(8,128)S(1)}, u32[]{:S(2)}, u32[]{:S(2)}) collective-permute-start(f32[256,128]{1,0:T(8,128)S(1)} %add.30), channel_id=1, source_target_pairs={{0,2},{1,3},{2,0},{3,1},{4,6},{5,7},{6,4},{7,5},{8,10},{9,11},{10,... | collective-permute-start | bytes 393224 | tf_op jit(solution)/shard_map/across/ppermute | solution.py:224
  37.4 4.2 %collective-permute-done.9.refs_0_ = f32[256,128]{1,0:T(8,128)S(1)} collective-permute-done((f32[256,128]{1,0:T(8,128)S(1)}, f32[256,128]{1,0:T(8,128)S(1)}, u32[]{:S(2)}, u32[]{:S(2)}) %collective-permute-start.9) | collective-permute-done | bytes 131104 | tf_op jit(solution)/shard_map/across/ppermute | solution.py:224
  41.5 2.6 %collective-permute-done.11.refs_1_ = f32[256,128]{1,0:T(8,128)S(1)} collective-permute-done((f32[256,128]{1,0:T(8,128)S(1)}, f32[256,128]{1,0:T(8,128)S(1)}, u32[]{:S(2)}, u32[]{:S(2)}) %collective-permute-start.11) | collective-permute-done | bytes 131104 | tf_op jit(solution)/shard_map/across/ppermute | solution.py:224
  44.1 2.2 %collective-permute-done.6.near = f32[512,128]{1,0:T(8,128)S(1)} collective-permute-done((f32[512,128]{1,0:T(8,128)S(1)}, f32[512,128]{1,0:T(8,128)S(1)}, u32[]{:S(2)}, u32[]{:S(2)}) %collective-permute-start.6) | collective-permute-done | bytes 262176 | tf_op jit(solution)/shard_map/near_partial/ppermute | solution.py:224
  46.3 0.8 %quad.1 = f32[128,128]{1,0:T(8,128)S(1)} custom-call(s32[1,4]{1,0:T(1,128)S(1)} %bitcast.4, f32[512,128]{1,0:T(8,128)S(1)} %get-tuple-element.19.masked_ref, f32[512,128]{1,0:T(8,128)S(1)} %get-tuple-element.32.own, f32[512,128]{1,0:T(8,128)S(1)} %collective-permute-done.6.near, f32[256,128]{1,0:T(8,128)S(1)} %collective-permute-done.9.refs_0_, ...), custom_call_target="tpu_custom_call" | custom-call | tf_op jit(solution)/shard_map/quad/pallas_call | solution.py:28
  47.2 1.3 %collective-permute-start.13 = (f32[128,128]{1,0:T(8,128)S(1)}, f32[128,128]{1,0:T(8,128)S(1)}, u32[]{:S(2)}, u32[]{:S(2)}) collective-permute-start(f32[128,128]{1,0:T(8,128)S(1)} %quad.1), channel_id=1, source_target_pairs={{0,8},{4,12},{8,0},{12,4},{1,9},{5,13},{9,1},{13,5},{2,10},{6,14},... | collective-permute-start | bytes 196616 | tf_op jit(solution)/shard_map/tail/ppermute | solution.py:224
  48.5 0.5 %collective-permute-start.12 = (f32[128,128]{1,0:T(8,128)S(1)}, f32[128,128]{1,0:T(8,128)S(1)}, u32[]{:S(2)}, u32[]{:S(2)}) collective-permute-start(f32[128,128]{1,0:T(8,128)S(1)} %quad.1), channel_id=1, source_target_pairs={{0,4},{4,0},{8,12},{12,8},{1,5},{5,1},{9,13},{13,9},{2,6},{6,2},{1... | collective-permute-start | bytes 196616 | tf_op jit(solution)/shard_map/tail/ppermute | solution.py:224
  49.1 1.3 %panel.1 = f32[512,128]{1,0:T(8,128)} custom-call(s32[1,4]{1,0:T(1,128)S(1)} %bitcast.5, f32[512,128]{1,0:T(8,128)S(1)} %get-tuple-element.32.own, f32[512,128]{1,0:T(8,128)S(1)} %collective-permute-done.6.near, f32[256,128]{1,0:T(8,128)S(1)} %collective-permute-done.9.refs_0_, f32[256,128]{1,0:T(8,128)S(1)} %collective-permute-done.11.refs_1_), custom_call_target="tpu_custom_call" | custom-call | tf_op jit(solution)/shard_map/panel/pallas_call | solution.py:28
  50.4 1.2 %collective-permute-done.14 = f32[128,128]{1,0:T(8,128)S(1)} collective-permute-done((f32[128,128]{1,0:T(8,128)S(1)}, f32[128,128]{1,0:T(8,128)S(1)}, u32[]{:S(2)}, u32[]{:S(2)}) %collective-permute-start.14) | collective-permute-done | bytes 65568 | tf_op jit(solution)/shard_map/tail/ppermute | solution.py:224
  51.6 1.1 %collective-permute-done.13 = f32[128,128]{1,0:T(8,128)S(1)} collective-permute-done((f32[128,128]{1,0:T(8,128)S(1)}, f32[128,128]{1,0:T(8,128)S(1)}, u32[]{:S(2)}, u32[]{:S(2)}) %collective-permute-start.13) | collective-permute-done | bytes 65568 | tf_op jit(solution)/shard_map/tail/ppermute | solution.py:224
  52.7 0.6 %add_add_fusion = f32[128,128]{1,0:T(8,128)} fusion(f32[128,128]{1,0:T(8,128)S(1)} %copy-done.4, f32[128,128]{1,0:T(8,128)S(1)} %collective-permute-done.14, f32[128,128]{1,0:T(8,128)S(1)} %collective-permute-done.13, f32[128,128]{1,0:T(8,128)S(1)} %quad.1, f32[128,128]{1,0:T(8,128)S(1)} %collective-permute-done.12), kind=kLoop, calls=%fused_computation.2 | loop fusion | flops 65536 | bytes 393216 | tf_op jit(solution)/shard_map/add | solution.py:290
  (22 shorter events, 0.4 us)
Async XLA Ops:
  0.6 4.6 %copy-start = (f32[512,128]{1,0:T(8,128)S(1)}, f32[512,128]{1,0:T(8,128)}, u32[]{:S(2)}) copy-start(f32[512,128]{1,0:T(8,128)} %panel_ref.3) | copy-start | bytes 786436
  0.6 4.6 %copy-start.1 = (s32[4,1]{0,1:T(1,128)S(1)}, s32[4,1]{0,1:T(1,128)}, u32[]{:S(2)}) copy-start(s32[4,1]{0,1:T(1,128)} %param.6) | copy-start | bytes 52
  2.3 8.6 %collective-permute-start.2 = (f32[256,128]{1,0:T(8,128)}, f32[256,128]{1,0:T(8,128)S(1)}, u32[]{:S(2)}, u32[]{:S(2)}) collective-permute-start(f32[256,128]{1,0:T(8,128)} %masking.3), channel_id=1, source_target_pairs={{0,8},{1,12},{2,10},{3,11},{4,9},{5,13},{6,14},{7,15},{8,0},{9,1},... | collective-permute-start | bytes 393224 | tf_op jit(solution)/shard_map/low_crossed/ppermute | solution.py:176
  5.9 12.7 %collective-permute-start = (f32[256,128]{1,0:T(8,128)S(1)}, f32[256,128]{1,0:T(8,128)S(1)}, u32[]{:S(2)}, u32[]{:S(2)}) collective-permute-start(f32[256,128]{1,0:T(8,128)S(1)} %get-tuple-element.20), channel_id=1, source_target_pairs={{0,8},{1,12},{2,0},{3,4},{4,9},{5,13},{6,1},{7,5},{8,10},{9,14},{1... | collective-permute-start | bytes 393224 | tf_op jit(solution)/shard_map/top_moved/ppermute | solution.py:176
  5.9 1.2 %copy-start.2 = (f32[512,512]{1,0:T(8,128)S(1)}, f32[512,512]{1,0:T(8,128)}, u32[]{:S(2)}) copy-start(f32[512,512]{1,0:T(8,128)} %a_ref) | copy-start | bytes 3145732
  7.1 3.7 %copy-start.3 = (f32[256,128]{1,0:T(8,128)S(1)}, f32[256,128]{1,0:T(8,128)}, u32[]{:S(2)}) copy-start(f32[256,128]{1,0:T(8,128)} %masking.3) | copy-start | bytes 393220
  10.9 9.6 %collective-permute-start.3 = (f32[256,128]{1,0:T(8,128)S(1)}, f32[256,128]{1,0:T(8,128)S(1)}, u32[]{:S(2)}, u32[]{:S(2)}) collective-permute-start(f32[256,128]{1,0:T(8,128)S(1)} %broadcast_select_fusion.1), channel_id=1, source_target_pairs={{0,2},{1,6},{2,0},{3,4},{4,3},{5,7},{6,1},{7,5},{8,10},{9,14},{10,... | collective-permute-start | bytes 393224 | tf_op jit(solution)/shard_map/low_moved/ppermute | solution.py:176
  18.5 5.0 %collective-permute-start.1 = (f32[256,128]{1,0:T(8,128)S(1)}, f32[256,128]{1,0:T(8,128)S(1)}, u32[]{:S(2)}, u32[]{:S(2)}) collective-permute-start(f32[256,128]{1,0:T(8,128)S(1)} %collective-permute-done), channel_id=1, source_target_pairs={{0,8},{4,12},{8,0},{12,4},{1,9},{5,13},{9,1},{13,5},{2,10},{6,14},... | collective-permute-start | bytes 393224 | tf_op jit(solution)/shard_map/top_flip/ppermute | solution.py:224
  20.5 5.0 %collective-permute-start.4 = (f32[256,128]{1,0:T(8,128)S(1)}, f32[256,128]{1,0:T(8,128)S(1)}, u32[]{:S(2)}, u32[]{:S(2)}) collective-permute-start(f32[256,128]{1,0:T(8,128)S(1)} %collective-permute-done.2), channel_id=1, source_target_pairs={{0,8},{4,12},{8,0},{12,4},{1,9},{5,13},{9,1},{13,5},{2,10},{6,14},... | collective-permute-start | bytes 393224 | tf_op jit(solution)/shard_map/low_flip/ppermute | solution.py:224
  23.5 2.0 %collective-permute-start.7 = (f32[512,128]{1,0:T(8,128)S(1)}, f32[512,128]{1,0:T(8,128)S(1)}, u32[]{:S(2)}, u32[]{:S(2)}) collective-permute-start(f32[512,128]{1,0:T(8,128)S(1)} %pad_maximum_fusion.mine_ref), channel_id=1, source_target_pairs={{0,4},{4,0},{8,12},{12,8},{1,5},{5,1},{9,13},{13,9},{2,6},{6,2},{1... | collective-permute-start | bytes 786440 | tf_op jit(solution)/shard_map/far_cores/ppermute | solution.py:224
  25.5 2.9 %collective-permute-start.5 = (f32[512,128]{1,0:T(8,128)S(1)}, f32[512,128]{1,0:T(8,128)S(1)}, u32[]{:S(2)}, u32[]{:S(2)}) collective-permute-start(f32[512,128]{1,0:T(8,128)S(1)} %maximum_select_fusion.mine_ref), channel_id=1, source_target_pairs={{0,4},{4,0},{8,12},{12,8},{1,5},{5,1},{9,13},{13,9},{2,6},{6,2},{1... | collective-permute-start | bytes 786440 | tf_op jit(solution)/shard_map/near_cores/ppermute | solution.py:224
  26.3 6.4 %collective-permute-start.8 = (f32[256,128]{1,0:T(8,128)S(1)}, f32[256,128]{1,0:T(8,128)S(1)}, u32[]{:S(2)}, u32[]{:S(2)}) collective-permute-start(f32[256,128]{1,0:T(8,128)S(1)} %get-tuple-element.29), channel_id=1, source_target_pairs={{0,1},{1,0},{2,3},{3,2},{4,5},{5,4},{6,7},{7,6},{8,9},{9,8},{10,11... | collective-permute-start | bytes 393224 | tf_op jit(solution)/shard_map/next/ppermute | solution.py:224
  26.4 9.1 %collective-permute-start.10 = (f32[256,128]{1,0:T(8,128)S(1)}, f32[256,128]{1,0:T(8,128)S(1)}, u32[]{:S(2)}, u32[]{:S(2)}) collective-permute-start(f32[256,128]{1,0:T(8,128)S(1)} %get-tuple-element.31), channel_id=1, source_target_pairs={{0,1},{1,0},{2,3},{3,2},{4,5},{5,4},{6,7},{7,6},{8,9},{9,8},{10,11... | collective-permute-start | bytes 393224 | tf_op jit(solution)/shard_map/next/ppermute | solution.py:224
  29.1 17.2 %collective-permute-start.6 = (f32[512,128]{1,0:T(8,128)S(1)}, f32[512,128]{1,0:T(8,128)S(1)}, u32[]{:S(2)}, u32[]{:S(2)}) collective-permute-start(f32[512,128]{1,0:T(8,128)S(1)} %get-tuple-element.27), channel_id=1, source_target_pairs={{0,1},{1,0},{2,3},{3,2},{4,5},{5,4},{6,7},{7,6},{8,9},{9,8},{10,11... | collective-permute-start | bytes 786440 | tf_op jit(solution)/shard_map/near_partial/ppermute | solution.py:224
  32.7 8.8 %collective-permute-start.9 = (f32[256,128]{1,0:T(8,128)S(1)}, f32[256,128]{1,0:T(8,128)S(1)}, u32[]{:S(2)}, u32[]{:S(2)}) collective-permute-start(f32[256,128]{1,0:T(8,128)S(1)} %add.29), channel_id=1, source_target_pairs={{0,2},{1,3},{2,0},{3,1},{4,6},{5,7},{6,4},{7,5},{8,10},{9,11},{10,... | collective-permute-start | bytes 393224 | tf_op jit(solution)/shard_map/across/ppermute | solution.py:224
  35.5 8.6 %collective-permute-start.11 = (f32[256,128]{1,0:T(8,128)S(1)}, f32[256,128]{1,0:T(8,128)S(1)}, u32[]{:S(2)}, u32[]{:S(2)}) collective-permute-start(f32[256,128]{1,0:T(8,128)S(1)} %add.30), channel_id=1, source_target_pairs={{0,2},{1,3},{2,0},{3,1},{4,6},{5,7},{6,4},{7,5},{8,10},{9,11},{10,... | collective-permute-start | bytes 393224 | tf_op jit(solution)/shard_map/across/ppermute | solution.py:224
  47.1 5.6 %copy-start.4 = (f32[128,128]{1,0:T(8,128)S(1)}, f32[128,128]{1,0:T(8,128)}, u32[]{:S(2)}) copy-start(f32[128,128]{1,0:T(8,128)} %param.7) | copy-start | bytes 196612
  47.1 4.5 %collective-permute-start.14 = (f32[128,128]{1,0:T(8,128)S(1)}, f32[128,128]{1,0:T(8,128)S(1)}, u32[]{:S(2)}, u32[]{:S(2)}) collective-permute-start(f32[128,128]{1,0:T(8,128)S(1)} %quad.1), channel_id=1, source_target_pairs={{0,12},{4,8},{8,4},{12,0},{1,13},{5,9},{9,5},{13,1},{2,14},{6,10},... | collective-permute-start | bytes 196616 | tf_op jit(solution)/shard_map/tail/ppermute | solution.py:224
  47.2 5.5 %collective-permute-start.13 = (f32[128,128]{1,0:T(8,128)S(1)}, f32[128,128]{1,0:T(8,128)S(1)}, u32[]{:S(2)}, u32[]{:S(2)}) collective-permute-start(f32[128,128]{1,0:T(8,128)S(1)} %quad.1), channel_id=1, source_target_pairs={{0,8},{4,12},{8,0},{12,4},{1,9},{5,13},{9,1},{13,5},{2,10},{6,14},... | collective-permute-start | bytes 196616 | tf_op jit(solution)/shard_map/tail/ppermute | solution.py:224
  48.5 4.2 %collective-permute-start.12 = (f32[128,128]{1,0:T(8,128)S(1)}, f32[128,128]{1,0:T(8,128)S(1)}, u32[]{:S(2)}, u32[]{:S(2)}) collective-permute-start(f32[128,128]{1,0:T(8,128)S(1)} %quad.1), channel_id=1, source_target_pairs={{0,4},{4,0},{8,12},{12,8},{1,5},{5,1},{9,13},{13,9},{2,6},{6,2},{1... | collective-permute-start | bytes 196616 | tf_op jit(solution)/shard_map/tail/ppermute | solution.py:224

commit v9 on v8

--- a/solution.py
+++ b/solution.py
@@ -73,17 +73,20 @@
 
 
 def pair(same_ref, high_ref, low_ref, mine_ref, other_ref, *outs):
-    ah, al = high_ref[...], low_ref[...]
     same = same_ref[0] == 1
     mine, other = mine_ref[...], other_ref[...]
-    for m, refs in (
-        (jnp.where(same, mine, other), outs[: len(outs) // 2]),
-        (jnp.where(same, other, mine), outs[len(outs) // 2 :]),
-    ):
-        out = product(ah, al, m)
-        tall = out.shape[0] // len(refs)
-        for i, ref in enumerate(refs):
-            ref[...] = out[i * tall : (i + 1) * tall, :]
+    width = mine.shape[1]
+    first, second = jnp.where(same, mine, other), jnp.where(same, other, mine)
+    (h0, l0), (h1, l1) = split(first), split(second)
+    ah = high_ref[...]
+    low = dot(low_ref[...], jnp.concatenate([h0, h1], axis=1), INNER)
+    n = len(outs) // 2
+    for i, (h, l) in enumerate(((h0, l0), (h1, l1))):
+        both = dot(ah, jnp.concatenate([h, l], axis=1), INNER)
+        out = both[:, :width] + (both[:, width:] + low[:, i * width : (i + 1) * width])
+        tall = out.shape[0] // n
+        for j, ref in enumerate(outs[i * n : (i + 1) * n]):
+            ref[...] = out[j * tall : (j + 1) * tall, :]
 
 
 def finish(width, mask_ref, masked_ref, *refs):

time: 53.6 us -> 53.4 us (level)
  no operation moved by 1% of the time
where the time goes in v9:
time: 53.4 us; the launch traced here: 53.3 us
  waiting for transfers between devices  30 us (56%)
  starting transfers between devices  14.7 us (28%)
  Pallas kernels  5.73 us (11%)
  local copies, waits for them, and re-layouts  1.24 us (2%)
  between operations  0.81 us (2%)
  other arithmetic  0.77 us (1%)
    ppermute x12, waiting for transfers between devices, swap(): return lax.ppermute(x, axis, [(i, i ^ bit) for i in range(side)])  20.4 us
    ppermute x3, waiting for transfers between devices, move(): return lax.ppermute(x, GRID, route(rule))  9.57 us
    ppermute x12, starting transfers between devices, swap(): return lax.ppermute(x, axis, [(i, i ^ bit) for i in range(side)])  8.15 us
    ppermute x3, starting transfers between devices, move(): return lax.ppermute(x, GRID, route(rule))  6.54 us
    pallas_call x7, Pallas kernels, call(): pl.pallas_call(body, out_shape=[jax.ShapeDtypeStruct(shape, dtype) for sh...  5.73 us
    unnamed x10, local copies, waits for them, and re-layouts  1.24 us
  transfers between devices with their start and end apart: 15, of which 12 were waited for; matrix products, arithmetic and copies ran while one was open for 0% of the time, Pallas kernels for 6%

profile of v9, /device:TPU:0, one launch (start us, length us, event | category | flops | bytes accessed | tf_op | source)
XLA Modules:
  0.0 53.3 jit_solution(8638984988222223077)
XLA Ops:
  0.6 1.7 %masking.3 = f32[256,128]{1,0:T(8,128)} custom-call(s32[1,4]{1,0:T(1,128)} %bitcast.2, f32[512,128]{1,0:T(8,128)} %panel_ref.3), custom_call_target="tpu_custom_call" | custom-call | tf_op jit(solution)/shard_map/masking/pallas_call | solution.py:28
  2.3 2.9 %collective-permute-start.2 = (f32[256,128]{1,0:T(8,128)}, f32[256,128]{1,0:T(8,128)S(1)}, u32[]{:S(2)}, u32[]{:S(2)}) collective-permute-start(f32[256,128]{1,0:T(8,128)} %masking.3), channel_id=1, source_target_pairs={{0,8},{1,12},{2,10},{3,11},{4,9},{5,13},{6,14},{7,15},{8,0},{9,1},... | collective-permute-start | bytes 393224 | tf_op jit(solution)/shard_map/low_crossed/ppermute | solution.py:179
  5.3 0.6 %masking.2 = (f32[512,128]{1,0:T(8,128)S(1)}, f32[256,128]{1,0:T(8,128)S(1)}) custom-call(s32[1,4]{1,0:T(1,128)S(1)} %bitcast.3, f32[512,128]{1,0:T(8,128)S(1)} %copy-done), custom_call_target="tpu_custom_call" | custom-call | tf_op jit(solution)/shard_map/masking/pallas_call | solution.py:28
  5.9 1.2 %copy-done.2 = f32[512,512]{1,0:T(8,128)S(1)} copy-done((f32[512,512]{1,0:T(8,128)S(1)}, f32[512,512]{1,0:T(8,128)}, u32[]{:S(2)}) %copy-start.2) | copy-done | bytes 1048600
  7.2 0.1 splitting.1
  7.3 3.6 %collective-permute-done.2 = f32[256,128]{1,0:T(8,128)S(1)} collective-permute-done((f32[256,128]{1,0:T(8,128)}, f32[256,128]{1,0:T(8,128)S(1)}, u32[]{:S(2)}, u32[]{:S(2)}) %collective-permute-start.2) | collective-permute-done | bytes 131104 | tf_op jit(solution)/shard_map/low_crossed/ppermute | solution.py:179
  10.9 3.5 %collective-permute-start.3 = (f32[256,128]{1,0:T(8,128)S(1)}, f32[256,128]{1,0:T(8,128)S(1)}, u32[]{:S(2)}, u32[]{:S(2)}) collective-permute-start(f32[256,128]{1,0:T(8,128)S(1)} %broadcast_select_fusion.1), channel_id=1, source_target_pairs={{0,2},{1,6},{2,0},{3,4},{4,3},{5,7},{6,1},{7,5},{8,10},{9,14},{10,... | collective-permute-start | bytes 393224 | tf_op jit(solution)/shard_map/low_moved/ppermute | solution.py:179
  14.4 4.1 %collective-permute-done = f32[256,128]{1,0:T(8,128)S(1)} collective-permute-done((f32[256,128]{1,0:T(8,128)S(1)}, f32[256,128]{1,0:T(8,128)S(1)}, u32[]{:S(2)}, u32[]{:S(2)}) %collective-permute-start) | collective-permute-done | bytes 131104 | tf_op jit(solution)/shard_map/top_moved/ppermute | solution.py:179
  18.5 2.0 %collective-permute-done.3 = f32[256,128]{1,0:T(8,128)S(1)} collective-permute-done((f32[256,128]{1,0:T(8,128)S(1)}, f32[256,128]{1,0:T(8,128)S(1)}, u32[]{:S(2)}, u32[]{:S(2)}) %collective-permute-start.3) | collective-permute-done | bytes 131104 | tf_op jit(solution)/shard_map/low_moved/ppermute | solution.py:179
  20.5 0.1 collective-permute-start.4
  20.6 2.9 %collective-permute-done.1 = f32[256,128]{1,0:T(8,128)S(1)} collective-permute-done((f32[256,128]{1,0:T(8,128)S(1)}, f32[256,128]{1,0:T(8,128)S(1)}, u32[]{:S(2)}, u32[]{:S(2)}) %collective-permute-start.1) | collective-permute-done | bytes 131104 | tf_op jit(solution)/shard_map/top_flip/ppermute | solution.py:227
  23.6 1.8 %collective-permute-done.4 = f32[256,128]{1,0:T(8,128)S(1)} collective-permute-done((f32[256,128]{1,0:T(8,128)S(1)}, f32[256,128]{1,0:T(8,128)S(1)}, u32[]{:S(2)}, u32[]{:S(2)}) %collective-permute-start.4) | collective-permute-done | bytes 131104 | tf_op jit(solution)/shard_map/low_flip/ppermute | solution.py:227
  25.6 0.6 %far_pair.1 = (f32[256,128]{1,0:T(8,128)S(1)}, f32[256,128]{1,0:T(8,128)S(1)}, f32[256,128]{1,0:T(8,128)S(1)}, f32[256,128]{1,0:T(8,128)S(1)}) custom-call(s32[1]{0:T(128)} %bitcast.1.same_ref, bf16[512,512]{1,0:T(8,128)(2,1)S(1)} %get-tuple-element.22.high_ref, bf16[512,512]{1,0:T(8,128)(2,1)S(1)} %get-tuple-element.23.low_ref, ...), custom_call_target="tpu_custom_call" | custom-call | tf_op jit(solution)/shard_map/far_pair/pallas_call | solution.py:28
  26.2 0.1 collective-permute-start.8
  26.3 2.0 %collective-permute-start.10 = (f32[256,128]{1,0:T(8,128)S(1)}, f32[256,128]{1,0:T(8,128)S(1)}, u32[]{:S(2)}, u32[]{:S(2)}) collective-permute-start(f32[256,128]{1,0:T(8,128)S(1)} %get-tuple-element.31), channel_id=1, source_target_pairs={{0,1},{1,0},{2,3},{3,2},{4,5},{5,4},{6,7},{7,6},{8,9},{9,8},{10,11... | collective-permute-start | bytes 393224 | tf_op jit(solution)/shard_map/next/ppermute | solution.py:227
  28.3 0.6 %near_pair.1 = (f32[512,128]{1,0:T(8,128)S(1)}, f32[512,128]{1,0:T(8,128)S(1)}) custom-call(s32[1]{0:T(128)} %bitcast.1.same_ref, bf16[512,512]{1,0:T(8,128)(2,1)S(1)} %get-tuple-element.22.high_ref, bf16[512,512]{1,0:T(8,128)(2,1)S(1)} %get-tuple-element.23.low_ref, f32[512,128]{1,0:T(8,128)S(1)} %maximum_select_fusion.mine_ref, ...), custom_call_target="tpu_custom_call" | custom-call | tf_op jit(solution)/shard_map/near_pair/pallas_call | solution.py:28
  28.9 0.2 collective-permute-start.6
  29.1 3.5 %collective-permute-done.8 = f32[256,128]{1,0:T(8,128)S(1)} collective-permute-done((f32[256,128]{1,0:T(8,128)S(1)}, f32[256,128]{1,0:T(8,128)S(1)}, u32[]{:S(2)}, u32[]{:S(2)}) %collective-permute-start.8) | collective-permute-done | bytes 131104 | tf_op jit(solution)/shard_map/next/ppermute | solution.py:227
  32.6 1.9 %collective-permute-start.9 = (f32[256,128]{1,0:T(8,128)S(1)}, f32[256,128]{1,0:T(8,128)S(1)}, u32[]{:S(2)}, u32[]{:S(2)}) collective-permute-start(f32[256,128]{1,0:T(8,128)S(1)} %add.29), channel_id=1, source_target_pairs={{0,2},{1,3},{2,0},{3,1},{4,6},{5,7},{6,4},{7,5},{8,10},{9,11},{10,... | collective-permute-start | bytes 393224 | tf_op jit(solution)/shard_map/across/ppermute | solution.py:227
  34.4 0.9 %collective-permute-done.10 = f32[256,128]{1,0:T(8,128)S(1)} collective-permute-done((f32[256,128]{1,0:T(8,128)S(1)}, f32[256,128]{1,0:T(8,128)S(1)}, u32[]{:S(2)}, u32[]{:S(2)}) %collective-permute-start.10) | collective-permute-done | bytes 131104 | tf_op jit(solution)/shard_map/next/ppermute | solution.py:227
  35.4 1.9 %collective-permute-start.11 = (f32[256,128]{1,0:T(8,128)S(1)}, f32[256,128]{1,0:T(8,128)S(1)}, u32[]{:S(2)}, u32[]{:S(2)}) collective-permute-start(f32[256,128]{1,0:T(8,128)S(1)} %add.30), channel_id=1, source_target_pairs={{0,2},{1,3},{2,0},{3,1},{4,6},{5,7},{6,4},{7,5},{8,10},{9,11},{10,... | collective-permute-start | bytes 393224 | tf_op jit(solution)/shard_map/across/ppermute | solution.py:227
  37.2 4.2 %collective-permute-done.9.refs_0_ = f32[256,128]{1,0:T(8,128)S(1)} collective-permute-done((f32[256,128]{1,0:T(8,128)S(1)}, f32[256,128]{1,0:T(8,128)S(1)}, u32[]{:S(2)}, u32[]{:S(2)}) %collective-permute-start.9) | collective-permute-done | bytes 131104 | tf_op jit(solution)/shard_map/across/ppermute | solution.py:227
  41.4 2.6 %collective-permute-done.11.refs_1_ = f32[256,128]{1,0:T(8,128)S(1)} collective-permute-done((f32[256,128]{1,0:T(8,128)S(1)}, f32[256,128]{1,0:T(8,128)S(1)}, u32[]{:S(2)}, u32[]{:S(2)}) %collective-permute-start.11) | collective-permute-done | bytes 131104 | tf_op jit(solution)/shard_map/across/ppermute | solution.py:227
  44.0 2.2 %collective-permute-done.6.near = f32[512,128]{1,0:T(8,128)S(1)} collective-permute-done((f32[512,128]{1,0:T(8,128)S(1)}, f32[512,128]{1,0:T(8,128)S(1)}, u32[]{:S(2)}, u32[]{:S(2)}) %collective-permute-start.6) | collective-permute-done | bytes 262176 | tf_op jit(solution)/shard_map/near_partial/ppermute | solution.py:227
  46.2 0.8 %quad.1 = f32[128,128]{1,0:T(8,128)S(1)} custom-call(s32[1,4]{1,0:T(1,128)S(1)} %bitcast.4, f32[512,128]{1,0:T(8,128)S(1)} %get-tuple-element.19.masked_ref, f32[512,128]{1,0:T(8,128)S(1)} %get-tuple-element.32.own, f32[512,128]{1,0:T(8,128)S(1)} %collective-permute-done.6.near, f32[256,128]{1,0:T(8,128)S(1)} %collective-permute-done.9.refs_0_, ...), custom_call_target="tpu_custom_call" | custom-call | tf_op jit(solution)/shard_map/quad/pallas_call | solution.py:28
  47.0 0.1 collective-permute-start.14
  47.1 1.3 %collective-permute-start.13 = (f32[128,128]{1,0:T(8,128)S(1)}, f32[128,128]{1,0:T(8,128)S(1)}, u32[]{:S(2)}, u32[]{:S(2)}) collective-permute-start(f32[128,128]{1,0:T(8,128)S(1)} %quad.1), channel_id=1, source_target_pairs={{0,8},{4,12},{8,0},{12,4},{1,9},{5,13},{9,1},{13,5},{2,10},{6,14},... | collective-permute-start | bytes 196616 | tf_op jit(solution)/shard_map/tail/ppermute | solution.py:227
  48.4 0.6 %collective-permute-start.12 = (f32[128,128]{1,0:T(8,128)S(1)}, f32[128,128]{1,0:T(8,128)S(1)}, u32[]{:S(2)}, u32[]{:S(2)}) collective-permute-start(f32[128,128]{1,0:T(8,128)S(1)} %quad.1), channel_id=1, source_target_pairs={{0,4},{4,0},{8,12},{12,8},{1,5},{5,1},{9,13},{13,9},{2,6},{6,2},{1... | collective-permute-start | bytes 196616 | tf_op jit(solution)/shard_map/tail/ppermute | solution.py:227
  49.0 1.3 %panel.1 = f32[512,128]{1,0:T(8,128)} custom-call(s32[1,4]{1,0:T(1,128)S(1)} %bitcast.5, f32[512,128]{1,0:T(8,128)S(1)} %get-tuple-element.32.own, f32[512,128]{1,0:T(8,128)S(1)} %collective-permute-done.6.near, f32[256,128]{1,0:T(8,128)S(1)} %collective-permute-done.9.refs_0_, f32[256,128]{1,0:T(8,128)S(1)} %collective-permute-done.11.refs_1_), custom_call_target="tpu_custom_call" | custom-call | tf_op jit(solution)/shard_map/panel/pallas_call | solution.py:28
  50.2 1.2 %collective-permute-done.14 = f32[128,128]{1,0:T(8,128)S(1)} collective-permute-done((f32[128,128]{1,0:T(8,128)S(1)}, f32[128,128]{1,0:T(8,128)S(1)}, u32[]{:S(2)}, u32[]{:S(2)}) %collective-permute-start.14) | collective-permute-done | bytes 65568 | tf_op jit(solution)/shard_map/tail/ppermute | solution.py:227
  51.5 1.1 %collective-permute-done.13 = f32[128,128]{1,0:T(8,128)S(1)} collective-permute-done((f32[128,128]{1,0:T(8,128)S(1)}, f32[128,128]{1,0:T(8,128)S(1)}, u32[]{:S(2)}, u32[]{:S(2)}) %collective-permute-start.13) | collective-permute-done | bytes 65568 | tf_op jit(solution)/shard_map/tail/ppermute | solution.py:227
  52.6 0.6 %add_add_fusion = f32[128,128]{1,0:T(8,128)} fusion(f32[128,128]{1,0:T(8,128)S(1)} %copy-done.4, f32[128,128]{1,0:T(8,128)S(1)} %collective-permute-done.14, f32[128,128]{1,0:T(8,128)S(1)} %collective-permute-done.13, f32[128,128]{1,0:T(8,128)S(1)} %quad.1, f32[128,128]{1,0:T(8,128)S(1)} %collective-permute-done.12), kind=kLoop, calls=%fused_computation.2 | loop fusion | flops 65536 | bytes 393216 | tf_op jit(solution)/shard_map/add | solution.py:293
  (22 shorter events, 0.4 us)
Async XLA Ops:
  0.6 4.6 %copy-start = (f32[512,128]{1,0:T(8,128)S(1)}, f32[512,128]{1,0:T(8,128)}, u32[]{:S(2)}) copy-start(f32[512,128]{1,0:T(8,128)} %panel_ref.3) | copy-start | bytes 786436
  0.6 4.6 %copy-start.1 = (s32[4,1]{0,1:T(1,128)S(1)}, s32[4,1]{0,1:T(1,128)}, u32[]{:S(2)}) copy-start(s32[4,1]{0,1:T(1,128)} %param.6) | copy-start | bytes 52
  2.3 8.6 %collective-permute-start.2 = (f32[256,128]{1,0:T(8,128)}, f32[256,128]{1,0:T(8,128)S(1)}, u32[]{:S(2)}, u32[]{:S(2)}) collective-permute-start(f32[256,128]{1,0:T(8,128)} %masking.3), channel_id=1, source_target_pairs={{0,8},{1,12},{2,10},{3,11},{4,9},{5,13},{6,14},{7,15},{8,0},{9,1},... | collective-permute-start | bytes 393224 | tf_op jit(solution)/shard_map/low_crossed/ppermute | solution.py:179
  5.9 12.7 %collective-permute-start = (f32[256,128]{1,0:T(8,128)S(1)}, f32[256,128]{1,0:T(8,128)S(1)}, u32[]{:S(2)}, u32[]{:S(2)}) collective-permute-start(f32[256,128]{1,0:T(8,128)S(1)} %get-tuple-element.20), channel_id=1, source_target_pairs={{0,8},{1,12},{2,0},{3,4},{4,9},{5,13},{6,1},{7,5},{8,10},{9,14},{1... | collective-permute-start | bytes 393224 | tf_op jit(solution)/shard_map/top_moved/ppermute | solution.py:179
  5.9 1.2 %copy-start.2 = (f32[512,512]{1,0:T(8,128)S(1)}, f32[512,512]{1,0:T(8,128)}, u32[]{:S(2)}) copy-start(f32[512,512]{1,0:T(8,128)} %a_ref) | copy-start | bytes 3145732
  7.1 3.7 %copy-start.3 = (f32[256,128]{1,0:T(8,128)S(1)}, f32[256,128]{1,0:T(8,128)}, u32[]{:S(2)}) copy-start(f32[256,128]{1,0:T(8,128)} %masking.3) | copy-start | bytes 393220
  10.9 9.6 %collective-permute-start.3 = (f32[256,128]{1,0:T(8,128)S(1)}, f32[256,128]{1,0:T(8,128)S(1)}, u32[]{:S(2)}, u32[]{:S(2)}) collective-permute-start(f32[256,128]{1,0:T(8,128)S(1)} %broadcast_select_fusion.1), channel_id=1, source_target_pairs={{0,2},{1,6},{2,0},{3,4},{4,3},{5,7},{6,1},{7,5},{8,10},{9,14},{10,... | collective-permute-start | bytes 393224 | tf_op jit(solution)/shard_map/low_moved/ppermute | solution.py:179
  18.5 5.0 %collective-permute-start.1 = (f32[256,128]{1,0:T(8,128)S(1)}, f32[256,128]{1,0:T(8,128)S(1)}, u32[]{:S(2)}, u32[]{:S(2)}) collective-permute-start(f32[256,128]{1,0:T(8,128)S(1)} %collective-permute-done), channel_id=1, source_target_pairs={{0,8},{4,12},{8,0},{12,4},{1,9},{5,13},{9,1},{13,5},{2,10},{6,14},... | collective-permute-start | bytes 393224 | tf_op jit(solution)/shard_map/top_flip/ppermute | solution.py:227
  20.5 5.0 %collective-permute-start.4 = (f32[256,128]{1,0:T(8,128)S(1)}, f32[256,128]{1,0:T(8,128)S(1)}, u32[]{:S(2)}, u32[]{:S(2)}) collective-permute-start(f32[256,128]{1,0:T(8,128)S(1)} %collective-permute-done.2), channel_id=1, source_target_pairs={{0,8},{4,12},{8,0},{12,4},{1,9},{5,13},{9,1},{13,5},{2,10},{6,14},... | collective-permute-start | bytes 393224 | tf_op jit(solution)/shard_map/low_flip/ppermute | solution.py:227
  23.5 2.0 %collective-permute-start.7 = (f32[512,128]{1,0:T(8,128)S(1)}, f32[512,128]{1,0:T(8,128)S(1)}, u32[]{:S(2)}, u32[]{:S(2)}) collective-permute-start(f32[512,128]{1,0:T(8,128)S(1)} %pad_maximum_fusion.mine_ref), channel_id=1, source_target_pairs={{0,4},{4,0},{8,12},{12,8},{1,5},{5,1},{9,13},{13,9},{2,6},{6,2},{1... | collective-permute-start | bytes 786440 | tf_op jit(solution)/shard_map/far_cores/ppermute | solution.py:227
  25.5 2.8 %collective-permute-start.5 = (f32[512,128]{1,0:T(8,128)S(1)}, f32[512,128]{1,0:T(8,128)S(1)}, u32[]{:S(2)}, u32[]{:S(2)}) collective-permute-start(f32[512,128]{1,0:T(8,128)S(1)} %maximum_select_fusion.mine_ref), channel_id=1, source_target_pairs={{0,4},{4,0},{8,12},{12,8},{1,5},{5,1},{9,13},{13,9},{2,6},{6,2},{1... | collective-permute-start | bytes 786440 | tf_op jit(solution)/shard_map/near_cores/ppermute | solution.py:227
  26.2 6.4 %collective-permute-start.8 = (f32[256,128]{1,0:T(8,128)S(1)}, f32[256,128]{1,0:T(8,128)S(1)}, u32[]{:S(2)}, u32[]{:S(2)}) collective-permute-start(f32[256,128]{1,0:T(8,128)S(1)} %get-tuple-element.29), channel_id=1, source_target_pairs={{0,1},{1,0},{2,3},{3,2},{4,5},{5,4},{6,7},{7,6},{8,9},{9,8},{10,11... | collective-permute-start | bytes 393224 | tf_op jit(solution)/shard_map/next/ppermute | solution.py:227
  26.3 9.1 %collective-permute-start.10 = (f32[256,128]{1,0:T(8,128)S(1)}, f32[256,128]{1,0:T(8,128)S(1)}, u32[]{:S(2)}, u32[]{:S(2)}) collective-permute-start(f32[256,128]{1,0:T(8,128)S(1)} %get-tuple-element.31), channel_id=1, source_target_pairs={{0,1},{1,0},{2,3},{3,2},{4,5},{5,4},{6,7},{7,6},{8,9},{9,8},{10,11... | collective-permute-start | bytes 393224 | tf_op jit(solution)/shard_map/next/ppermute | solution.py:227
  28.9 17.3 %collective-permute-start.6 = (f32[512,128]{1,0:T(8,128)S(1)}, f32[512,128]{1,0:T(8,128)S(1)}, u32[]{:S(2)}, u32[]{:S(2)}) collective-permute-start(f32[512,128]{1,0:T(8,128)S(1)} %get-tuple-element.27), channel_id=1, source_target_pairs={{0,1},{1,0},{2,3},{3,2},{4,5},{5,4},{6,7},{7,6},{8,9},{9,8},{10,11... | collective-permute-start | bytes 786440 | tf_op jit(solution)/shard_map/near_partial/ppermute | solution.py:227
  32.6 8.8 %collective-permute-start.9 = (f32[256,128]{1,0:T(8,128)S(1)}, f32[256,128]{1,0:T(8,128)S(1)}, u32[]{:S(2)}, u32[]{:S(2)}) collective-permute-start(f32[256,128]{1,0:T(8,128)S(1)} %add.29), channel_id=1, source_target_pairs={{0,2},{1,3},{2,0},{3,1},{4,6},{5,7},{6,4},{7,5},{8,10},{9,11},{10,... | collective-permute-start | bytes 393224 | tf_op jit(solution)/shard_map/across/ppermute | solution.py:227
  35.4 8.6 %collective-permute-start.11 = (f32[256,128]{1,0:T(8,128)S(1)}, f32[256,128]{1,0:T(8,128)S(1)}, u32[]{:S(2)}, u32[]{:S(2)}) collective-permute-start(f32[256,128]{1,0:T(8,128)S(1)} %add.30), channel_id=1, source_target_pairs={{0,2},{1,3},{2,0},{3,1},{4,6},{5,7},{6,4},{7,5},{8,10},{9,11},{10,... | collective-permute-start | bytes 393224 | tf_op jit(solution)/shard_map/across/ppermute | solution.py:227
  47.0 5.6 %copy-start.4 = (f32[128,128]{1,0:T(8,128)S(1)}, f32[128,128]{1,0:T(8,128)}, u32[]{:S(2)}) copy-start(f32[128,128]{1,0:T(8,128)} %param.7) | copy-start | bytes 196612
  47.0 4.5 %collective-permute-start.14 = (f32[128,128]{1,0:T(8,128)S(1)}, f32[128,128]{1,0:T(8,128)S(1)}, u32[]{:S(2)}, u32[]{:S(2)}) collective-permute-start(f32[128,128]{1,0:T(8,128)S(1)} %quad.1), channel_id=1, source_target_pairs={{0,12},{4,8},{8,4},{12,0},{1,13},{5,9},{9,5},{13,1},{2,14},{6,10},... | collective-permute-start | bytes 196616 | tf_op jit(solution)/shard_map/tail/ppermute | solution.py:227
  47.1 5.5 %collective-permute-start.13 = (f32[128,128]{1,0:T(8,128)S(1)}, f32[128,128]{1,0:T(8,128)S(1)}, u32[]{:S(2)}, u32[]{:S(2)}) collective-permute-start(f32[128,128]{1,0:T(8,128)S(1)} %quad.1), channel_id=1, source_target_pairs={{0,8},{4,12},{8,0},{12,4},{1,9},{5,13},{9,1},{13,5},{2,10},{6,14},... | collective-permute-start | bytes 196616 | tf_op jit(solution)/shard_map/tail/ppermute | solution.py:227
  48.4 4.2 %collective-permute-start.12 = (f32[128,128]{1,0:T(8,128)S(1)}, f32[128,128]{1,0:T(8,128)S(1)}, u32[]{:S(2)}, u32[]{:S(2)}) collective-permute-start(f32[128,128]{1,0:T(8,128)S(1)} %quad.1), channel_id=1, source_target_pairs={{0,4},{4,0},{8,12},{12,8},{1,5},{5,1},{9,13},{13,9},{2,6},{6,2},{1... | collective-permute-start | bytes 196616 | tf_op jit(solution)/shard_map/tail/ppermute | solution.py:227

commit v10 on v9

--- a/solution.py
+++ b/solution.py
@@ -109,7 +109,8 @@
         cols = slice(s * width, (s + 1) * width)
         mh, ml = split(masked_ref[:, cols])
         gh, gl = split(g_ref[:, cols])
-        quad_ref[cols, :] = -(dot(mh, gh, ROWS) + (dot(mh, gl, ROWS) + dot(ml, gh, ROWS)))
+        both = dot(mh, jnp.concatenate([gh, gl], axis=1), ROWS)
+        quad_ref[cols, :] = -(both[:, :width] + (both[:, width:] + dot(ml, gh, ROWS)))
 
 
 def quad_only(width, mask_ref, masked_ref, own, near, *refs):

time: 53.4 us -> 53.4 us (level)
  no operation moved by 1% of the time
where the time goes in v10:
time: 53.4 us; the launch traced here: 53.2 us
  waiting for transfers between devices  30 us (56%)
  starting transfers between devices  14.7 us (28%)
  Pallas kernels  5.69 us (11%)
  local copies, waits for them, and re-layouts  1.24 us (2%)
  between operations  0.81 us (2%)
  other arithmetic  0.77 us (1%)
    ppermute x12, waiting for transfers between devices, swap(): return lax.ppermute(x, axis, [(i, i ^ bit) for i in range(side)])  20.4 us
    ppermute x3, waiting for transfers between devices, move(): return lax.ppermute(x, GRID, route(rule))  9.57 us
    ppermute x12, starting transfers between devices, swap(): return lax.ppermute(x, axis, [(i, i ^ bit) for i in range(side)])  8.15 us
    ppermute x3, starting transfers between devices, move(): return lax.ppermute(x, GRID, route(rule))  6.54 us
    pallas_call x7, Pallas kernels, call(): pl.pallas_call(body, out_shape=[jax.ShapeDtypeStruct(shape, dtype) for sh...  5.69 us
    unnamed x10, local copies, waits for them, and re-layouts  1.24 us
  transfers between devices with their start and end apart: 15, of which 12 were waited for; matrix products, arithmetic and copies ran while one was open for 0% of the time, Pallas kernels for 6%

profile of v10, /device:TPU:0, one launch (start us, length us, event | category | flops | bytes accessed | tf_op | source)
XLA Modules:
  0.0 53.2 jit_solution(17960499767124329154)
XLA Ops:
  0.6 1.7 %masking.3 = f32[256,128]{1,0:T(8,128)} custom-call(s32[1,4]{1,0:T(1,128)} %bitcast.2, f32[512,128]{1,0:T(8,128)} %panel_ref.3), custom_call_target="tpu_custom_call" | custom-call | tf_op jit(solution)/shard_map/masking/pallas_call | solution.py:28
  2.3 2.9 %collective-permute-start.2 = (f32[256,128]{1,0:T(8,128)}, f32[256,128]{1,0:T(8,128)S(1)}, u32[]{:S(2)}, u32[]{:S(2)}) collective-permute-start(f32[256,128]{1,0:T(8,128)} %masking.3), channel_id=1, source_target_pairs={{0,8},{1,12},{2,10},{3,11},{4,9},{5,13},{6,14},{7,15},{8,0},{9,1},... | collective-permute-start | bytes 393224 | tf_op jit(solution)/shard_map/low_crossed/ppermute | solution.py:180
  5.3 0.6 %masking.2 = (f32[512,128]{1,0:T(8,128)S(1)}, f32[256,128]{1,0:T(8,128)S(1)}) custom-call(s32[1,4]{1,0:T(1,128)S(1)} %bitcast.3, f32[512,128]{1,0:T(8,128)S(1)} %copy-done), custom_call_target="tpu_custom_call" | custom-call | tf_op jit(solution)/shard_map/masking/pallas_call | solution.py:28
  5.9 1.2 %copy-done.2 = f32[512,512]{1,0:T(8,128)S(1)} copy-done((f32[512,512]{1,0:T(8,128)S(1)}, f32[512,512]{1,0:T(8,128)}, u32[]{:S(2)}) %copy-start.2) | copy-done | bytes 1048600
  7.2 0.1 splitting.1
  7.3 3.6 %collective-permute-done.2 = f32[256,128]{1,0:T(8,128)S(1)} collective-permute-done((f32[256,128]{1,0:T(8,128)}, f32[256,128]{1,0:T(8,128)S(1)}, u32[]{:S(2)}, u32[]{:S(2)}) %collective-permute-start.2) | collective-permute-done | bytes 131104 | tf_op jit(solution)/shard_map/low_crossed/ppermute | solution.py:180
  10.9 3.5 %collective-permute-start.3 = (f32[256,128]{1,0:T(8,128)S(1)}, f32[256,128]{1,0:T(8,128)S(1)}, u32[]{:S(2)}, u32[]{:S(2)}) collective-permute-start(f32[256,128]{1,0:T(8,128)S(1)} %broadcast_select_fusion.1), channel_id=1, source_target_pairs={{0,2},{1,6},{2,0},{3,4},{4,3},{5,7},{6,1},{7,5},{8,10},{9,14},{10,... | collective-permute-start | bytes 393224 | tf_op jit(solution)/shard_map/low_moved/ppermute | solution.py:180
  14.4 4.1 %collective-permute-done = f32[256,128]{1,0:T(8,128)S(1)} collective-permute-done((f32[256,128]{1,0:T(8,128)S(1)}, f32[256,128]{1,0:T(8,128)S(1)}, u32[]{:S(2)}, u32[]{:S(2)}) %collective-permute-start) | collective-permute-done | bytes 131104 | tf_op jit(solution)/shard_map/top_moved/ppermute | solution.py:180
  18.5 2.0 %collective-permute-done.3 = f32[256,128]{1,0:T(8,128)S(1)} collective-permute-done((f32[256,128]{1,0:T(8,128)S(1)}, f32[256,128]{1,0:T(8,128)S(1)}, u32[]{:S(2)}, u32[]{:S(2)}) %collective-permute-start.3) | collective-permute-done | bytes 131104 | tf_op jit(solution)/shard_map/low_moved/ppermute | solution.py:180
  20.5 0.1 collective-permute-start.4
  20.6 2.9 %collective-permute-done.1 = f32[256,128]{1,0:T(8,128)S(1)} collective-permute-done((f32[256,128]{1,0:T(8,128)S(1)}, f32[256,128]{1,0:T(8,128)S(1)}, u32[]{:S(2)}, u32[]{:S(2)}) %collective-permute-start.1) | collective-permute-done | bytes 131104 | tf_op jit(solution)/shard_map/top_flip/ppermute | solution.py:228
  23.6 1.8 %collective-permute-done.4 = f32[256,128]{1,0:T(8,128)S(1)} collective-permute-done((f32[256,128]{1,0:T(8,128)S(1)}, f32[256,128]{1,0:T(8,128)S(1)}, u32[]{:S(2)}, u32[]{:S(2)}) %collective-permute-start.4) | collective-permute-done | bytes 131104 | tf_op jit(solution)/shard_map/low_flip/ppermute | solution.py:228
  25.6 0.6 %far_pair.1 = (f32[256,128]{1,0:T(8,128)S(1)}, f32[256,128]{1,0:T(8,128)S(1)}, f32[256,128]{1,0:T(8,128)S(1)}, f32[256,128]{1,0:T(8,128)S(1)}) custom-call(s32[1]{0:T(128)} %bitcast.1.same_ref, bf16[512,512]{1,0:T(8,128)(2,1)S(1)} %get-tuple-element.22.high_ref, bf16[512,512]{1,0:T(8,128)(2,1)S(1)} %get-tuple-element.23.low_ref, ...), custom_call_target="tpu_custom_call" | custom-call | tf_op jit(solution)/shard_map/far_pair/pallas_call | solution.py:28
  26.2 0.1 collective-permute-start.8
  26.3 2.0 %collective-permute-start.10 = (f32[256,128]{1,0:T(8,128)S(1)}, f32[256,128]{1,0:T(8,128)S(1)}, u32[]{:S(2)}, u32[]{:S(2)}) collective-permute-start(f32[256,128]{1,0:T(8,128)S(1)} %get-tuple-element.31), channel_id=1, source_target_pairs={{0,1},{1,0},{2,3},{3,2},{4,5},{5,4},{6,7},{7,6},{8,9},{9,8},{10,11... | collective-permute-start | bytes 393224 | tf_op jit(solution)/shard_map/next/ppermute | solution.py:228
  28.3 0.6 %near_pair.1 = (f32[512,128]{1,0:T(8,128)S(1)}, f32[512,128]{1,0:T(8,128)S(1)}) custom-call(s32[1]{0:T(128)} %bitcast.1.same_ref, bf16[512,512]{1,0:T(8,128)(2,1)S(1)} %get-tuple-element.22.high_ref, bf16[512,512]{1,0:T(8,128)(2,1)S(1)} %get-tuple-element.23.low_ref, f32[512,128]{1,0:T(8,128)S(1)} %maximum_select_fusion.mine_ref, ...), custom_call_target="tpu_custom_call" | custom-call | tf_op jit(solution)/shard_map/near_pair/pallas_call | solution.py:28
  28.9 0.2 collective-permute-start.6
  29.1 3.5 %collective-permute-done.8 = f32[256,128]{1,0:T(8,128)S(1)} collective-permute-done((f32[256,128]{1,0:T(8,128)S(1)}, f32[256,128]{1,0:T(8,128)S(1)}, u32[]{:S(2)}, u32[]{:S(2)}) %collective-permute-start.8) | collective-permute-done | bytes 131104 | tf_op jit(solution)/shard_map/next/ppermute | solution.py:228
  32.6 1.9 %collective-permute-start.9 = (f32[256,128]{1,0:T(8,128)S(1)}, f32[256,128]{1,0:T(8,128)S(1)}, u32[]{:S(2)}, u32[]{:S(2)}) collective-permute-start(f32[256,128]{1,0:T(8,128)S(1)} %add.29), channel_id=1, source_target_pairs={{0,2},{1,3},{2,0},{3,1},{4,6},{5,7},{6,4},{7,5},{8,10},{9,11},{10,... | collective-permute-start | bytes 393224 | tf_op jit(solution)/shard_map/across/ppermute | solution.py:228
  34.4 0.9 %collective-permute-done.10 = f32[256,128]{1,0:T(8,128)S(1)} collective-permute-done((f32[256,128]{1,0:T(8,128)S(1)}, f32[256,128]{1,0:T(8,128)S(1)}, u32[]{:S(2)}, u32[]{:S(2)}) %collective-permute-start.10) | collective-permute-done | bytes 131104 | tf_op jit(solution)/shard_map/next/ppermute | solution.py:228
  35.4 1.9 %collective-permute-start.11 = (f32[256,128]{1,0:T(8,128)S(1)}, f32[256,128]{1,0:T(8,128)S(1)}, u32[]{:S(2)}, u32[]{:S(2)}) collective-permute-start(f32[256,128]{1,0:T(8,128)S(1)} %add.30), channel_id=1, source_target_pairs={{0,2},{1,3},{2,0},{3,1},{4,6},{5,7},{6,4},{7,5},{8,10},{9,11},{10,... | collective-permute-start | bytes 393224 | tf_op jit(solution)/shard_map/across/ppermute | solution.py:228
  37.2 4.2 %collective-permute-done.9.refs_0_ = f32[256,128]{1,0:T(8,128)S(1)} collective-permute-done((f32[256,128]{1,0:T(8,128)S(1)}, f32[256,128]{1,0:T(8,128)S(1)}, u32[]{:S(2)}, u32[]{:S(2)}) %collective-permute-start.9) | collective-permute-done | bytes 131104 | tf_op jit(solution)/shard_map/across/ppermute | solution.py:228
  41.4 2.6 %collective-permute-done.11.refs_1_ = f32[256,128]{1,0:T(8,128)S(1)} collective-permute-done((f32[256,128]{1,0:T(8,128)S(1)}, f32[256,128]{1,0:T(8,128)S(1)}, u32[]{:S(2)}, u32[]{:S(2)}) %collective-permute-start.11) | collective-permute-done | bytes 131104 | tf_op jit(solution)/shard_map/across/ppermute | solution.py:228
  44.0 2.2 %collective-permute-done.6.near = f32[512,128]{1,0:T(8,128)S(1)} collective-permute-done((f32[512,128]{1,0:T(8,128)S(1)}, f32[512,128]{1,0:T(8,128)S(1)}, u32[]{:S(2)}, u32[]{:S(2)}) %collective-permute-start.6) | collective-permute-done | bytes 262176 | tf_op jit(solution)/shard_map/near_partial/ppermute | solution.py:228
  46.2 0.8 %quad.1 = f32[128,128]{1,0:T(8,128)S(1)} custom-call(s32[1,4]{1,0:T(1,128)S(1)} %bitcast.4, f32[512,128]{1,0:T(8,128)S(1)} %get-tuple-element.19.masked_ref, f32[512,128]{1,0:T(8,128)S(1)} %get-tuple-element.32.own, f32[512,128]{1,0:T(8,128)S(1)} %collective-permute-done.6.near, f32[256,128]{1,0:T(8,128)S(1)} %collective-permute-done.9.refs_0_, ...), custom_call_target="tpu_custom_call" | custom-call | tf_op jit(solution)/shard_map/quad/pallas_call | solution.py:28
  47.0 0.1 collective-permute-start.14
  47.1 1.3 %collective-permute-start.13 = (f32[128,128]{1,0:T(8,128)S(1)}, f32[128,128]{1,0:T(8,128)S(1)}, u32[]{:S(2)}, u32[]{:S(2)}) collective-permute-start(f32[128,128]{1,0:T(8,128)S(1)} %quad.1), channel_id=1, source_target_pairs={{0,8},{4,12},{8,0},{12,4},{1,9},{5,13},{9,1},{13,5},{2,10},{6,14},... | collective-permute-start | bytes 196616 | tf_op jit(solution)/shard_map/tail/ppermute | solution.py:228
  48.4 0.6 %collective-permute-start.12 = (f32[128,128]{1,0:T(8,128)S(1)}, f32[128,128]{1,0:T(8,128)S(1)}, u32[]{:S(2)}, u32[]{:S(2)}) collective-permute-start(f32[128,128]{1,0:T(8,128)S(1)} %quad.1), channel_id=1, source_target_pairs={{0,4},{4,0},{8,12},{12,8},{1,5},{5,1},{9,13},{13,9},{2,6},{6,2},{1... | collective-permute-start | bytes 196616 | tf_op jit(solution)/shard_map/tail/ppermute | solution.py:228
  48.9 1.3 %panel.1 = f32[512,128]{1,0:T(8,128)} custom-call(s32[1,4]{1,0:T(1,128)S(1)} %bitcast.5, f32[512,128]{1,0:T(8,128)S(1)} %get-tuple-element.32.own, f32[512,128]{1,0:T(8,128)S(1)} %collective-permute-done.6.near, f32[256,128]{1,0:T(8,128)S(1)} %collective-permute-done.9.refs_0_, f32[256,128]{1,0:T(8,128)S(1)} %collective-permute-done.11.refs_1_), custom_call_target="tpu_custom_call" | custom-call | tf_op jit(solution)/shard_map/panel/pallas_call | solution.py:28
  50.2 1.2 %collective-permute-done.14 = f32[128,128]{1,0:T(8,128)S(1)} collective-permute-done((f32[128,128]{1,0:T(8,128)S(1)}, f32[128,128]{1,0:T(8,128)S(1)}, u32[]{:S(2)}, u32[]{:S(2)}) %collective-permute-start.14) | collective-permute-done | bytes 65568 | tf_op jit(solution)/shard_map/tail/ppermute | solution.py:228
  51.4 1.1 %collective-permute-done.13 = f32[128,128]{1,0:T(8,128)S(1)} collective-permute-done((f32[128,128]{1,0:T(8,128)S(1)}, f32[128,128]{1,0:T(8,128)S(1)}, u32[]{:S(2)}, u32[]{:S(2)}) %collective-permute-start.13) | collective-permute-done | bytes 65568 | tf_op jit(solution)/shard_map/tail/ppermute | solution.py:228
  52.6 0.6 %add_add_fusion = f32[128,128]{1,0:T(8,128)} fusion(f32[128,128]{1,0:T(8,128)S(1)} %copy-done.4, f32[128,128]{1,0:T(8,128)S(1)} %collective-permute-done.14, f32[128,128]{1,0:T(8,128)S(1)} %collective-permute-done.13, f32[128,128]{1,0:T(8,128)S(1)} %quad.1, f32[128,128]{1,0:T(8,128)S(1)} %collective-permute-done.12), kind=kLoop, calls=%fused_computation.2 | loop fusion | flops 65536 | bytes 393216 | tf_op jit(solution)/shard_map/add | solution.py:294
  (22 shorter events, 0.4 us)
Async XLA Ops:
  0.6 4.6 %copy-start = (f32[512,128]{1,0:T(8,128)S(1)}, f32[512,128]{1,0:T(8,128)}, u32[]{:S(2)}) copy-start(f32[512,128]{1,0:T(8,128)} %panel_ref.3) | copy-start | bytes 786436
  0.6 4.6 %copy-start.1 = (s32[4,1]{0,1:T(1,128)S(1)}, s32[4,1]{0,1:T(1,128)}, u32[]{:S(2)}) copy-start(s32[4,1]{0,1:T(1,128)} %param.6) | copy-start | bytes 52
  2.3 8.6 %collective-permute-start.2 = (f32[256,128]{1,0:T(8,128)}, f32[256,128]{1,0:T(8,128)S(1)}, u32[]{:S(2)}, u32[]{:S(2)}) collective-permute-start(f32[256,128]{1,0:T(8,128)} %masking.3), channel_id=1, source_target_pairs={{0,8},{1,12},{2,10},{3,11},{4,9},{5,13},{6,14},{7,15},{8,0},{9,1},... | collective-permute-start | bytes 393224 | tf_op jit(solution)/shard_map/low_crossed/ppermute | solution.py:180
  5.9 12.7 %collective-permute-start = (f32[256,128]{1,0:T(8,128)S(1)}, f32[256,128]{1,0:T(8,128)S(1)}, u32[]{:S(2)}, u32[]{:S(2)}) collective-permute-start(f32[256,128]{1,0:T(8,128)S(1)} %get-tuple-element.20), channel_id=1, source_target_pairs={{0,8},{1,12},{2,0},{3,4},{4,9},{5,13},{6,1},{7,5},{8,10},{9,14},{1... | collective-permute-start | bytes 393224 | tf_op jit(solution)/shard_map/top_moved/ppermute | solution.py:180
  5.9 1.2 %copy-start.2 = (f32[512,512]{1,0:T(8,128)S(1)}, f32[512,512]{1,0:T(8,128)}, u32[]{:S(2)}) copy-start(f32[512,512]{1,0:T(8,128)} %a_ref) | copy-start | bytes 3145732
  7.1 3.7 %copy-start.3 = (f32[256,128]{1,0:T(8,128)S(1)}, f32[256,128]{1,0:T(8,128)}, u32[]{:S(2)}) copy-start(f32[256,128]{1,0:T(8,128)} %masking.3) | copy-start | bytes 393220
  10.9 9.6 %collective-permute-start.3 = (f32[256,128]{1,0:T(8,128)S(1)}, f32[256,128]{1,0:T(8,128)S(1)}, u32[]{:S(2)}, u32[]{:S(2)}) collective-permute-start(f32[256,128]{1,0:T(8,128)S(1)} %broadcast_select_fusion.1), channel_id=1, source_target_pairs={{0,2},{1,6},{2,0},{3,4},{4,3},{5,7},{6,1},{7,5},{8,10},{9,14},{10,... | collective-permute-start | bytes 393224 | tf_op jit(solution)/shard_map/low_moved/ppermute | solution.py:180
  18.5 5.0 %collective-permute-start.1 = (f32[256,128]{1,0:T(8,128)S(1)}, f32[256,128]{1,0:T(8,128)S(1)}, u32[]{:S(2)}, u32[]{:S(2)}) collective-permute-start(f32[256,128]{1,0:T(8,128)S(1)} %collective-permute-done), channel_id=1, source_target_pairs={{0,8},{4,12},{8,0},{12,4},{1,9},{5,13},{9,1},{13,5},{2,10},{6,14},... | collective-permute-start | bytes 393224 | tf_op jit(solution)/shard_map/top_flip/ppermute | solution.py:228
  20.5 5.0 %collective-permute-start.4 = (f32[256,128]{1,0:T(8,128)S(1)}, f32[256,128]{1,0:T(8,128)S(1)}, u32[]{:S(2)}, u32[]{:S(2)}) collective-permute-start(f32[256,128]{1,0:T(8,128)S(1)} %collective-permute-done.2), channel_id=1, source_target_pairs={{0,8},{4,12},{8,0},{12,4},{1,9},{5,13},{9,1},{13,5},{2,10},{6,14},... | collective-permute-start | bytes 393224 | tf_op jit(solution)/shard_map/low_flip/ppermute | solution.py:228
  23.5 2.0 %collective-permute-start.7 = (f32[512,128]{1,0:T(8,128)S(1)}, f32[512,128]{1,0:T(8,128)S(1)}, u32[]{:S(2)}, u32[]{:S(2)}) collective-permute-start(f32[512,128]{1,0:T(8,128)S(1)} %pad_maximum_fusion.mine_ref), channel_id=1, source_target_pairs={{0,4},{4,0},{8,12},{12,8},{1,5},{5,1},{9,13},{13,9},{2,6},{6,2},{1... | collective-permute-start | bytes 786440 | tf_op jit(solution)/shard_map/far_cores/ppermute | solution.py:228
  25.5 2.8 %collective-permute-start.5 = (f32[512,128]{1,0:T(8,128)S(1)}, f32[512,128]{1,0:T(8,128)S(1)}, u32[]{:S(2)}, u32[]{:S(2)}) collective-permute-start(f32[512,128]{1,0:T(8,128)S(1)} %maximum_select_fusion.mine_ref), channel_id=1, source_target_pairs={{0,4},{4,0},{8,12},{12,8},{1,5},{5,1},{9,13},{13,9},{2,6},{6,2},{1... | collective-permute-start | bytes 786440 | tf_op jit(solution)/shard_map/near_cores/ppermute | solution.py:228
  26.2 6.4 %collective-permute-start.8 = (f32[256,128]{1,0:T(8,128)S(1)}, f32[256,128]{1,0:T(8,128)S(1)}, u32[]{:S(2)}, u32[]{:S(2)}) collective-permute-start(f32[256,128]{1,0:T(8,128)S(1)} %get-tuple-element.29), channel_id=1, source_target_pairs={{0,1},{1,0},{2,3},{3,2},{4,5},{5,4},{6,7},{7,6},{8,9},{9,8},{10,11... | collective-permute-start | bytes 393224 | tf_op jit(solution)/shard_map/next/ppermute | solution.py:228
  26.3 9.1 %collective-permute-start.10 = (f32[256,128]{1,0:T(8,128)S(1)}, f32[256,128]{1,0:T(8,128)S(1)}, u32[]{:S(2)}, u32[]{:S(2)}) collective-permute-start(f32[256,128]{1,0:T(8,128)S(1)} %get-tuple-element.31), channel_id=1, source_target_pairs={{0,1},{1,0},{2,3},{3,2},{4,5},{5,4},{6,7},{7,6},{8,9},{9,8},{10,11... | collective-permute-start | bytes 393224 | tf_op jit(solution)/shard_map/next/ppermute | solution.py:228
  28.9 17.3 %collective-permute-start.6 = (f32[512,128]{1,0:T(8,128)S(1)}, f32[512,128]{1,0:T(8,128)S(1)}, u32[]{:S(2)}, u32[]{:S(2)}) collective-permute-start(f32[512,128]{1,0:T(8,128)S(1)} %get-tuple-element.27), channel_id=1, source_target_pairs={{0,1},{1,0},{2,3},{3,2},{4,5},{5,4},{6,7},{7,6},{8,9},{9,8},{10,11... | collective-permute-start | bytes 786440 | tf_op jit(solution)/shard_map/near_partial/ppermute | solution.py:228
  32.6 8.8 %collective-permute-start.9 = (f32[256,128]{1,0:T(8,128)S(1)}, f32[256,128]{1,0:T(8,128)S(1)}, u32[]{:S(2)}, u32[]{:S(2)}) collective-permute-start(f32[256,128]{1,0:T(8,128)S(1)} %add.29), channel_id=1, source_target_pairs={{0,2},{1,3},{2,0},{3,1},{4,6},{5,7},{6,4},{7,5},{8,10},{9,11},{10,... | collective-permute-start | bytes 393224 | tf_op jit(solution)/shard_map/across/ppermute | solution.py:228
  35.4 8.6 %collective-permute-start.11 = (f32[256,128]{1,0:T(8,128)S(1)}, f32[256,128]{1,0:T(8,128)S(1)}, u32[]{:S(2)}, u32[]{:S(2)}) collective-permute-start(f32[256,128]{1,0:T(8,128)S(1)} %add.30), channel_id=1, source_target_pairs={{0,2},{1,3},{2,0},{3,1},{4,6},{5,7},{6,4},{7,5},{8,10},{9,11},{10,... | collective-permute-start | bytes 393224 | tf_op jit(solution)/shard_map/across/ppermute | solution.py:228
  47.0 5.6 %copy-start.4 = (f32[128,128]{1,0:T(8,128)S(1)}, f32[128,128]{1,0:T(8,128)}, u32[]{:S(2)}) copy-start(f32[128,128]{1,0:T(8,128)} %param.7) | copy-start | bytes 196612
  47.0 4.5 %collective-permute-start.14 = (f32[128,128]{1,0:T(8,128)S(1)}, f32[128,128]{1,0:T(8,128)S(1)}, u32[]{:S(2)}, u32[]{:S(2)}) collective-permute-start(f32[128,128]{1,0:T(8,128)S(1)} %quad.1), channel_id=1, source_target_pairs={{0,12},{4,8},{8,4},{12,0},{1,13},{5,9},{9,5},{13,1},{2,14},{6,10},... | collective-permute-start | bytes 196616 | tf_op jit(solution)/shard_map/tail/ppermute | solution.py:228
  47.1 5.5 %collective-permute-start.13 = (f32[128,128]{1,0:T(8,128)S(1)}, f32[128,128]{1,0:T(8,128)S(1)}, u32[]{:S(2)}, u32[]{:S(2)}) collective-permute-start(f32[128,128]{1,0:T(8,128)S(1)} %quad.1), channel_id=1, source_target_pairs={{0,8},{4,12},{8,0},{12,4},{1,9},{5,13},{9,1},{13,5},{2,10},{6,14},... | collective-permute-start | bytes 196616 | tf_op jit(solution)/shard_map/tail/ppermute | solution.py:228
  48.4 4.2 %collective-permute-start.12 = (f32[128,128]{1,0:T(8,128)S(1)}, f32[128,128]{1,0:T(8,128)S(1)}, u32[]{:S(2)}, u32[]{:S(2)}) collective-permute-start(f32[128,128]{1,0:T(8,128)S(1)} %quad.1), channel_id=1, source_target_pairs={{0,4},{4,0},{8,12},{12,8},{1,5},{5,1},{9,13},{13,9},{2,6},{6,2},{1... | collective-permute-start | bytes 196616 | tf_op jit(solution)/shard_map/tail/ppermute | solution.py:228

commit v11 on v9

--- a/solution.py
+++ b/solution.py
@@ -192,11 +192,11 @@
 
     low_crossed = move(low, cross_early, "low_crossed")
     top_moved = move(top, far_direct, "top_moved")
-    halves = halved(after(inverse_blocks, top))
-    low_next = jnp.where(near_side, after(low_crossed, *halves), low)
+    low_next = jnp.where(near_side, low_crossed, low)
     low_moved = move(low_next, far_both, "low_moved")
+    halves = halved(after(inverse_blocks, low_next))
+    low_flip = swap(after(low_crossed, *halves), "row", 2, "low_flip")
     top_flip = swap(top_moved, "row", 2, "top_flip")
-    low_flip = swap(after(low_crossed, low_moved), "row", 2, "low_flip")
     near = jnp.where(
         near_side,
         jnp.concatenate([top_flip, low_flip]),

time: 53.4 us -> 53.4 us (level)
  waiting for transfers between devices: 30 us -> 25.4 us
  starting transfers between devices: 14.7 us -> 19.2 us
    ppermute x12, starting transfers between devices: 8.15 us -> 12.7 us  [swap(): return lax.ppermute(x, axis, [(i, i ^ bit) for i in range(side)])]
    ppermute x12, waiting for transfers between devices: 20.4 us -> 16.4 us  [swap(): return lax.ppermute(x, axis, [(i, i ^ bit) for i in range(side)])]
    ppermute x3, waiting for transfers between devices: 9.57 us -> 9 us  [move(): return lax.ppermute(x, GRID, route(rule))]
  transfers between devices with their start and end apart: 15 -> 15, of which waited for: 12 -> 9; matrix products, arithmetic and copies ran while one was open for 0% -> 0% of each run, Pallas kernels for 6% -> 6%
where the time goes in v11:
time: 53.4 us; the launch traced here: 53.2 us
  waiting for transfers between devices  25.4 us (48%)
  starting transfers between devices  19.2 us (36%)
  Pallas kernels  5.72 us (11%)
  local copies, waits for them, and re-layouts  1.24 us (2%)
  between operations  0.79 us (1%)
  other arithmetic  0.77 us (1%)
    ppermute x12, waiting for transfers between devices, swap(): return lax.ppermute(x, axis, [(i, i ^ bit) for i in range(side)])  16.4 us
    ppermute x12, starting transfers between devices, swap(): return lax.ppermute(x, axis, [(i, i ^ bit) for i in range(side)])  12.7 us
    ppermute x3, waiting for transfers between devices, move(): return lax.ppermute(x, GRID, route(rule))  9 us
    ppermute x3, starting transfers between devices, move(): return lax.ppermute(x, GRID, route(rule))  6.54 us
    pallas_call x7, Pallas kernels, call(): pl.pallas_call(body, out_shape=[jax.ShapeDtypeStruct(shape, dtype) for sh...  5.72 us
    unnamed x10, local copies, waits for them, and re-layouts  1.24 us
  transfers between devices with their start and end apart: 15, of which 9 were waited for; matrix products, arithmetic and copies ran while one was open for 0% of the time, Pallas kernels for 6%

profile of v11, /device:TPU:0, one launch (start us, length us, event | category | flops | bytes accessed | tf_op | source)
XLA Modules:
  0.0 53.2 jit_solution(9379044954992108604)
XLA Ops:
  0.6 1.7 %masking.3 = f32[256,128]{1,0:T(8,128)} custom-call(s32[1,4]{1,0:T(1,128)} %bitcast.2, f32[512,128]{1,0:T(8,128)} %panel_ref.3), custom_call_target="tpu_custom_call" | custom-call | tf_op jit(solution)/shard_map/masking/pallas_call | solution.py:28
  2.3 2.9 %collective-permute-start = (f32[256,128]{1,0:T(8,128)}, f32[256,128]{1,0:T(8,128)S(1)}, u32[]{:S(2)}, u32[]{:S(2)}) collective-permute-start(f32[256,128]{1,0:T(8,128)} %masking.3), channel_id=1, source_target_pairs={{0,8},{1,12},{2,10},{3,11},{4,9},{5,13},{6,14},{7,15},{8,0},{9,1},... | collective-permute-start | bytes 393224 | tf_op jit(solution)/shard_map/low_crossed/ppermute | solution.py:179
  5.3 0.6 %masking.2 = (f32[512,128]{1,0:T(8,128)S(1)}, f32[256,128]{1,0:T(8,128)S(1)}) custom-call(s32[1,4]{1,0:T(1,128)S(1)} %bitcast.3, f32[512,128]{1,0:T(8,128)S(1)} %copy-done), custom_call_target="tpu_custom_call" | custom-call | tf_op jit(solution)/shard_map/masking/pallas_call | solution.py:28
  5.9 0.1 collective-permute-start.1
  5.9 4.9 %collective-permute-done = f32[256,128]{1,0:T(8,128)S(1)} collective-permute-done((f32[256,128]{1,0:T(8,128)}, f32[256,128]{1,0:T(8,128)S(1)}, u32[]{:S(2)}, u32[]{:S(2)}) %collective-permute-start) | collective-permute-done | bytes 131104 | tf_op jit(solution)/shard_map/low_crossed/ppermute | solution.py:179
  10.9 3.5 %collective-permute-start.6 = (f32[256,128]{1,0:T(8,128)S(1)}, f32[256,128]{1,0:T(8,128)S(1)}, u32[]{:S(2)}, u32[]{:S(2)}) collective-permute-start(f32[256,128]{1,0:T(8,128)S(1)} %broadcast_select_fusion.1), channel_id=1, source_target_pairs={{0,2},{1,6},{2,0},{3,4},{4,3},{5,7},{6,1},{7,5},{8,10},{9,14},{10,... | collective-permute-start | bytes 393224 | tf_op jit(solution)/shard_map/low_moved/ppermute | solution.py:179
  14.4 4.1 %collective-permute-done.1 = f32[256,128]{1,0:T(8,128)S(1)} collective-permute-done((f32[256,128]{1,0:T(8,128)S(1)}, f32[256,128]{1,0:T(8,128)S(1)}, u32[]{:S(2)}, u32[]{:S(2)}) %collective-permute-start.1) | collective-permute-done | bytes 131104 | tf_op jit(solution)/shard_map/top_moved/ppermute | solution.py:179
  18.5 1.2 %copy-done.2 = f32[512,512]{1,0:T(8,128)S(1)} copy-done((f32[512,512]{1,0:T(8,128)S(1)}, f32[512,512]{1,0:T(8,128)}, u32[]{:S(2)}) %copy-start.2) | copy-done | bytes 1048600
  19.7 0.1 splitting.1
  19.9 2.1 %collective-permute-start.3 = (f32[256,128]{1,0:T(8,128)S(1)}, f32[256,128]{1,0:T(8,128)S(1)}, u32[]{:S(2)}, u32[]{:S(2)}) collective-permute-start(f32[256,128]{1,0:T(8,128)S(1)} %collective-permute-done), channel_id=1, source_target_pairs={{0,8},{4,12},{8,0},{12,4},{1,9},{5,13},{9,1},{13,5},{2,10},{6,14},... | collective-permute-start | bytes 393224 | tf_op jit(solution)/shard_map/low_flip/ppermute | solution.py:227
  22.0 1.5 %collective-permute-done.2 = f32[256,128]{1,0:T(8,128)S(1)} collective-permute-done((f32[256,128]{1,0:T(8,128)S(1)}, f32[256,128]{1,0:T(8,128)S(1)}, u32[]{:S(2)}, u32[]{:S(2)}) %collective-permute-start.2) | collective-permute-done | bytes 131104 | tf_op jit(solution)/shard_map/top_flip/ppermute | solution.py:227
  23.5 0.1 collective-permute-start.7
  23.6 1.3 %collective-permute-done.3 = f32[256,128]{1,0:T(8,128)S(1)} collective-permute-done((f32[256,128]{1,0:T(8,128)S(1)}, f32[256,128]{1,0:T(8,128)S(1)}, u32[]{:S(2)}, u32[]{:S(2)}) %collective-permute-start.3) | collective-permute-done | bytes 131104 | tf_op jit(solution)/shard_map/low_flip/ppermute | solution.py:227
  25.0 0.1 collective-permute-start.4
  25.1 0.1 collective-permute-done.7.other_ref
  25.1 0.6 %far_pair.1 = (f32[256,128]{1,0:T(8,128)S(1)}, f32[256,128]{1,0:T(8,128)S(1)}, f32[256,128]{1,0:T(8,128)S(1)}, f32[256,128]{1,0:T(8,128)S(1)}) custom-call(s32[1]{0:T(128)} %bitcast.1.same_ref, bf16[512,512]{1,0:T(8,128)(2,1)S(1)} %get-tuple-element.20.high_ref, bf16[512,512]{1,0:T(8,128)(2,1)S(1)} %get-tuple-element.21.low_ref, ...), custom_call_target="tpu_custom_call" | custom-call | tf_op jit(solution)/shard_map/far_pair/pallas_call | solution.py:28
  25.7 1.2 %collective-permute-start.8 = (f32[256,128]{1,0:T(8,128)S(1)}, f32[256,128]{1,0:T(8,128)S(1)}, u32[]{:S(2)}, u32[]{:S(2)}) collective-permute-start(f32[256,128]{1,0:T(8,128)S(1)} %get-tuple-element.27), channel_id=1, source_target_pairs={{0,1},{1,0},{2,3},{3,2},{4,5},{5,4},{6,7},{7,6},{8,9},{9,8},{10,11... | collective-permute-start | bytes 393224 | tf_op jit(solution)/shard_map/next/ppermute | solution.py:227
  26.9 0.9 %collective-permute-start.10 = (f32[256,128]{1,0:T(8,128)S(1)}, f32[256,128]{1,0:T(8,128)S(1)}, u32[]{:S(2)}, u32[]{:S(2)}) collective-permute-start(f32[256,128]{1,0:T(8,128)S(1)} %get-tuple-element.29), channel_id=1, source_target_pairs={{0,1},{1,0},{2,3},{3,2},{4,5},{5,4},{6,7},{7,6},{8,9},{9,8},{10,11... | collective-permute-start | bytes 393224 | tf_op jit(solution)/shard_map/next/ppermute | solution.py:227
  27.8 0.6 %near_pair.1 = (f32[512,128]{1,0:T(8,128)S(1)}, f32[512,128]{1,0:T(8,128)S(1)}) custom-call(s32[1]{0:T(128)} %bitcast.1.same_ref, bf16[512,512]{1,0:T(8,128)(2,1)S(1)} %get-tuple-element.20.high_ref, bf16[512,512]{1,0:T(8,128)(2,1)S(1)} %get-tuple-element.21.low_ref, f32[512,128]{1,0:T(8,128)S(1)} %maximum_select_fusion.mine_ref, ...), custom_call_target="tpu_custom_call" | custom-call | tf_op jit(solution)/shard_map/near_pair/pallas_call | solution.py:28
  28.4 1.2 %collective-permute-start.5 = (f32[512,128]{1,0:T(8,128)S(1)}, f32[512,128]{1,0:T(8,128)S(1)}, u32[]{:S(2)}, u32[]{:S(2)}) collective-permute-start(f32[512,128]{1,0:T(8,128)S(1)} %get-tuple-element.25), channel_id=1, source_target_pairs={{0,1},{1,0},{2,3},{3,2},{4,5},{5,4},{6,7},{7,6},{8,9},{9,8},{10,11... | collective-permute-start | bytes 786440 | tf_op jit(solution)/shard_map/near_partial/ppermute | solution.py:227
  29.6 2.5 %collective-permute-done.8 = f32[256,128]{1,0:T(8,128)S(1)} collective-permute-done((f32[256,128]{1,0:T(8,128)S(1)}, f32[256,128]{1,0:T(8,128)S(1)}, u32[]{:S(2)}, u32[]{:S(2)}) %collective-permute-start.8) | collective-permute-done | bytes 131104 | tf_op jit(solution)/shard_map/next/ppermute | solution.py:227
  32.1 2.1 %collective-permute-start.9 = (f32[256,128]{1,0:T(8,128)S(1)}, f32[256,128]{1,0:T(8,128)S(1)}, u32[]{:S(2)}, u32[]{:S(2)}) collective-permute-start(f32[256,128]{1,0:T(8,128)S(1)} %add.29), channel_id=1, source_target_pairs={{0,2},{1,3},{2,0},{3,1},{4,6},{5,7},{6,4},{7,5},{8,10},{9,11},{10,... | collective-permute-start | bytes 393224 | tf_op jit(solution)/shard_map/across/ppermute | solution.py:227
  34.3 0.7 %collective-permute-done.10 = f32[256,128]{1,0:T(8,128)S(1)} collective-permute-done((f32[256,128]{1,0:T(8,128)S(1)}, f32[256,128]{1,0:T(8,128)S(1)}, u32[]{:S(2)}, u32[]{:S(2)}) %collective-permute-start.10) | collective-permute-done | bytes 131104 | tf_op jit(solution)/shard_map/next/ppermute | solution.py:227
  34.9 2.1 %collective-permute-start.11 = (f32[256,128]{1,0:T(8,128)S(1)}, f32[256,128]{1,0:T(8,128)S(1)}, u32[]{:S(2)}, u32[]{:S(2)}) collective-permute-start(f32[256,128]{1,0:T(8,128)S(1)} %add.30), channel_id=1, source_target_pairs={{0,2},{1,3},{2,0},{3,1},{4,6},{5,7},{6,4},{7,5},{8,10},{9,11},{10,... | collective-permute-start | bytes 393224 | tf_op jit(solution)/shard_map/across/ppermute | solution.py:227
  37.1 8.6 %collective-permute-done.5.near = f32[512,128]{1,0:T(8,128)S(1)} collective-permute-done((f32[512,128]{1,0:T(8,128)S(1)}, f32[512,128]{1,0:T(8,128)S(1)}, u32[]{:S(2)}, u32[]{:S(2)}) %collective-permute-start.5) | collective-permute-done | bytes 262176 | tf_op jit(solution)/shard_map/near_partial/ppermute | solution.py:227
  45.7 0.8 %quad.1 = f32[128,128]{1,0:T(8,128)S(1)} custom-call(s32[1,4]{1,0:T(1,128)S(1)} %bitcast.4, f32[512,128]{1,0:T(8,128)S(1)} %get-tuple-element.18.masked_ref, f32[512,128]{1,0:T(8,128)S(1)} %get-tuple-element.30.own, f32[512,128]{1,0:T(8,128)S(1)} %collective-permute-done.5.near, f32[256,128]{1,0:T(8,128)S(1)} %collective-permute-done.9.refs_0_, ...), custom_call_target="tpu_custom_call" | custom-call | tf_op jit(solution)/shard_map/quad/pallas_call | solution.py:28
  46.6 1.2 %collective-permute-start.14 = (f32[128,128]{1,0:T(8,128)S(1)}, f32[128,128]{1,0:T(8,128)S(1)}, u32[]{:S(2)}, u32[]{:S(2)}) collective-permute-start(f32[128,128]{1,0:T(8,128)S(1)} %quad.1), channel_id=1, source_target_pairs={{0,12},{4,8},{8,4},{12,0},{1,13},{5,9},{9,5},{13,1},{2,14},{6,10},... | collective-permute-start | bytes 196616 | tf_op jit(solution)/shard_map/tail/ppermute | solution.py:227
  47.8 1.7 %collective-permute-start.13 = (f32[128,128]{1,0:T(8,128)S(1)}, f32[128,128]{1,0:T(8,128)S(1)}, u32[]{:S(2)}, u32[]{:S(2)}) collective-permute-start(f32[128,128]{1,0:T(8,128)S(1)} %quad.1), channel_id=1, source_target_pairs={{0,8},{4,12},{8,0},{12,4},{1,9},{5,13},{9,1},{13,5},{2,10},{6,14},... | collective-permute-start | bytes 196616 | tf_op jit(solution)/shard_map/tail/ppermute | solution.py:227
  49.4 0.0 collective-permute-start.12
  49.5 1.3 %panel.1 = f32[512,128]{1,0:T(8,128)} custom-call(s32[1,4]{1,0:T(1,128)S(1)} %bitcast.5, f32[512,128]{1,0:T(8,128)S(1)} %get-tuple-element.30.own, f32[512,128]{1,0:T(8,128)S(1)} %collective-permute-done.5.near, f32[256,128]{1,0:T(8,128)S(1)} %collective-permute-done.9.refs_0_, f32[256,128]{1,0:T(8,128)S(1)} %collective-permute-done.11.refs_1_), custom_call_target="tpu_custom_call" | custom-call | tf_op jit(solution)/shard_map/panel/pallas_call | solution.py:28
  50.8 1.8 %collective-permute-done.13 = f32[128,128]{1,0:T(8,128)S(1)} collective-permute-done((f32[128,128]{1,0:T(8,128)S(1)}, f32[128,128]{1,0:T(8,128)S(1)}, u32[]{:S(2)}, u32[]{:S(2)}) %collective-permute-start.13) | collective-permute-done | bytes 65568 | tf_op jit(solution)/shard_map/tail/ppermute | solution.py:227
  52.5 0.6 %add_add_fusion = f32[128,128]{1,0:T(8,128)} fusion(f32[128,128]{1,0:T(8,128)S(1)} %copy-done.4, f32[128,128]{1,0:T(8,128)S(1)} %collective-permute-done.14, f32[128,128]{1,0:T(8,128)S(1)} %collective-permute-done.13, f32[128,128]{1,0:T(8,128)S(1)} %quad.1, f32[128,128]{1,0:T(8,128)S(1)} %collective-permute-done.12), kind=kLoop, calls=%fused_computation.2 | loop fusion | flops 65536 | bytes 393216 | tf_op jit(solution)/shard_map/add | solution.py:293
  (22 shorter events, 0.2 us)
Async XLA Ops:
  0.6 4.6 %copy-start = (f32[512,128]{1,0:T(8,128)S(1)}, f32[512,128]{1,0:T(8,128)}, u32[]{:S(2)}) copy-start(f32[512,128]{1,0:T(8,128)} %panel_ref.3) | copy-start | bytes 786436
  0.6 4.6 %copy-start.1 = (s32[4,1]{0,1:T(1,128)S(1)}, s32[4,1]{0,1:T(1,128)}, u32[]{:S(2)}) copy-start(s32[4,1]{0,1:T(1,128)} %param.6) | copy-start | bytes 52
  2.3 8.6 %copy-start.3 = (f32[256,128]{1,0:T(8,128)S(1)}, f32[256,128]{1,0:T(8,128)}, u32[]{:S(2)}) copy-start(f32[256,128]{1,0:T(8,128)} %masking.3) | copy-start | bytes 393220
  2.3 8.6 %collective-permute-start = (f32[256,128]{1,0:T(8,128)}, f32[256,128]{1,0:T(8,128)S(1)}, u32[]{:S(2)}, u32[]{:S(2)}) collective-permute-start(f32[256,128]{1,0:T(8,128)} %masking.3), channel_id=1, source_target_pairs={{0,8},{1,12},{2,10},{3,11},{4,9},{5,13},{6,14},{7,15},{8,0},{9,1},... | collective-permute-start | bytes 393224 | tf_op jit(solution)/shard_map/low_crossed/ppermute | solution.py:179
  5.9 12.7 %collective-permute-start.1 = (f32[256,128]{1,0:T(8,128)S(1)}, f32[256,128]{1,0:T(8,128)S(1)}, u32[]{:S(2)}, u32[]{:S(2)}) collective-permute-start(f32[256,128]{1,0:T(8,128)S(1)} %get-tuple-element.22), channel_id=1, source_target_pairs={{0,8},{1,12},{2,0},{3,4},{4,9},{5,13},{6,1},{7,5},{8,10},{9,14},{1... | collective-permute-start | bytes 393224 | tf_op jit(solution)/shard_map/top_moved/ppermute | solution.py:179
  10.9 12.6 %collective-permute-start.6 = (f32[256,128]{1,0:T(8,128)S(1)}, f32[256,128]{1,0:T(8,128)S(1)}, u32[]{:S(2)}, u32[]{:S(2)}) collective-permute-start(f32[256,128]{1,0:T(8,128)S(1)} %broadcast_select_fusion.1), channel_id=1, source_target_pairs={{0,2},{1,6},{2,0},{3,4},{4,3},{5,7},{6,1},{7,5},{8,10},{9,14},{10,... | collective-permute-start | bytes 393224 | tf_op jit(solution)/shard_map/low_moved/ppermute | solution.py:179
  18.5 5.0 %collective-permute-start.2 = (f32[256,128]{1,0:T(8,128)S(1)}, f32[256,128]{1,0:T(8,128)S(1)}, u32[]{:S(2)}, u32[]{:S(2)}) collective-permute-start(f32[256,128]{1,0:T(8,128)S(1)} %collective-permute-done.1), channel_id=1, source_target_pairs={{0,8},{4,12},{8,0},{12,4},{1,9},{5,13},{9,1},{13,5},{2,10},{6,14},... | collective-permute-start | bytes 393224 | tf_op jit(solution)/shard_map/top_flip/ppermute | solution.py:227
  18.5 1.2 %copy-start.2 = (f32[512,512]{1,0:T(8,128)S(1)}, f32[512,512]{1,0:T(8,128)}, u32[]{:S(2)}) copy-start(f32[512,512]{1,0:T(8,128)} %a_ref) | copy-start | bytes 3145732
  19.9 5.0 %collective-permute-start.3 = (f32[256,128]{1,0:T(8,128)S(1)}, f32[256,128]{1,0:T(8,128)S(1)}, u32[]{:S(2)}, u32[]{:S(2)}) collective-permute-start(f32[256,128]{1,0:T(8,128)S(1)} %collective-permute-done), channel_id=1, source_target_pairs={{0,8},{4,12},{8,0},{12,4},{1,9},{5,13},{9,1},{13,5},{2,10},{6,14},... | collective-permute-start | bytes 393224 | tf_op jit(solution)/shard_map/low_flip/ppermute | solution.py:227
  23.5 1.6 %collective-permute-start.7 = (f32[512,128]{1,0:T(8,128)S(1)}, f32[512,128]{1,0:T(8,128)S(1)}, u32[]{:S(2)}, u32[]{:S(2)}) collective-permute-start(f32[512,128]{1,0:T(8,128)S(1)} %pad_maximum_fusion.mine_ref), channel_id=1, source_target_pairs={{0,4},{4,0},{8,12},{12,8},{1,5},{5,1},{9,13},{13,9},{2,6},{6,2},{1... | collective-permute-start | bytes 786440 | tf_op jit(solution)/shard_map/far_cores/ppermute | solution.py:227
  25.0 2.9 %collective-permute-start.4 = (f32[512,128]{1,0:T(8,128)S(1)}, f32[512,128]{1,0:T(8,128)S(1)}, u32[]{:S(2)}, u32[]{:S(2)}) collective-permute-start(f32[512,128]{1,0:T(8,128)S(1)} %maximum_select_fusion.mine_ref), channel_id=1, source_target_pairs={{0,4},{4,0},{8,12},{12,8},{1,5},{5,1},{9,13},{13,9},{2,6},{6,2},{1... | collective-permute-start | bytes 786440 | tf_op jit(solution)/shard_map/near_cores/ppermute | solution.py:227
  25.7 6.4 %collective-permute-start.8 = (f32[256,128]{1,0:T(8,128)S(1)}, f32[256,128]{1,0:T(8,128)S(1)}, u32[]{:S(2)}, u32[]{:S(2)}) collective-permute-start(f32[256,128]{1,0:T(8,128)S(1)} %get-tuple-element.27), channel_id=1, source_target_pairs={{0,1},{1,0},{2,3},{3,2},{4,5},{5,4},{6,7},{7,6},{8,9},{9,8},{10,11... | collective-permute-start | bytes 393224 | tf_op jit(solution)/shard_map/next/ppermute | solution.py:227
  26.9 8.0 %collective-permute-start.10 = (f32[256,128]{1,0:T(8,128)S(1)}, f32[256,128]{1,0:T(8,128)S(1)}, u32[]{:S(2)}, u32[]{:S(2)}) collective-permute-start(f32[256,128]{1,0:T(8,128)S(1)} %get-tuple-element.29), channel_id=1, source_target_pairs={{0,1},{1,0},{2,3},{3,2},{4,5},{5,4},{6,7},{7,6},{8,9},{9,8},{10,11... | collective-permute-start | bytes 393224 | tf_op jit(solution)/shard_map/next/ppermute | solution.py:227
  28.4 17.2 %collective-permute-start.5 = (f32[512,128]{1,0:T(8,128)S(1)}, f32[512,128]{1,0:T(8,128)S(1)}, u32[]{:S(2)}, u32[]{:S(2)}) collective-permute-start(f32[512,128]{1,0:T(8,128)S(1)} %get-tuple-element.25), channel_id=1, source_target_pairs={{0,1},{1,0},{2,3},{3,2},{4,5},{5,4},{6,7},{7,6},{8,9},{9,8},{10,11... | collective-permute-start | bytes 786440 | tf_op jit(solution)/shard_map/near_partial/ppermute | solution.py:227
  32.1 13.6 %collective-permute-start.9 = (f32[256,128]{1,0:T(8,128)S(1)}, f32[256,128]{1,0:T(8,128)S(1)}, u32[]{:S(2)}, u32[]{:S(2)}) collective-permute-start(f32[256,128]{1,0:T(8,128)S(1)} %add.29), channel_id=1, source_target_pairs={{0,2},{1,3},{2,0},{3,1},{4,6},{5,7},{6,4},{7,5},{8,10},{9,11},{10,... | collective-permute-start | bytes 393224 | tf_op jit(solution)/shard_map/across/ppermute | solution.py:227
  34.9 10.7 %collective-permute-start.11 = (f32[256,128]{1,0:T(8,128)S(1)}, f32[256,128]{1,0:T(8,128)S(1)}, u32[]{:S(2)}, u32[]{:S(2)}) collective-permute-start(f32[256,128]{1,0:T(8,128)S(1)} %add.30), channel_id=1, source_target_pairs={{0,2},{1,3},{2,0},{3,1},{4,6},{5,7},{6,4},{7,5},{8,10},{9,11},{10,... | collective-permute-start | bytes 393224 | tf_op jit(solution)/shard_map/across/ppermute | solution.py:227
  46.5 6.0 %copy-start.4 = (f32[128,128]{1,0:T(8,128)S(1)}, f32[128,128]{1,0:T(8,128)}, u32[]{:S(2)}) copy-start(f32[128,128]{1,0:T(8,128)} %param.7) | copy-start | bytes 196612
  46.6 4.2 %collective-permute-start.14 = (f32[128,128]{1,0:T(8,128)S(1)}, f32[128,128]{1,0:T(8,128)S(1)}, u32[]{:S(2)}, u32[]{:S(2)}) collective-permute-start(f32[128,128]{1,0:T(8,128)S(1)} %quad.1), channel_id=1, source_target_pairs={{0,12},{4,8},{8,4},{12,0},{1,13},{5,9},{9,5},{13,1},{2,14},{6,10},... | collective-permute-start | bytes 196616 | tf_op jit(solution)/shard_map/tail/ppermute | solution.py:227
  47.8 4.7 %collective-permute-start.13 = (f32[128,128]{1,0:T(8,128)S(1)}, f32[128,128]{1,0:T(8,128)S(1)}, u32[]{:S(2)}, u32[]{:S(2)}) collective-permute-start(f32[128,128]{1,0:T(8,128)S(1)} %quad.1), channel_id=1, source_target_pairs={{0,8},{4,12},{8,0},{12,4},{1,9},{5,13},{9,1},{13,5},{2,10},{6,14},... | collective-permute-start | bytes 196616 | tf_op jit(solution)/shard_map/tail/ppermute | solution.py:227
  49.4 3.1 %collective-permute-start.12 = (f32[128,128]{1,0:T(8,128)S(1)}, f32[128,128]{1,0:T(8,128)S(1)}, u32[]{:S(2)}, u32[]{:S(2)}) collective-permute-start(f32[128,128]{1,0:T(8,128)S(1)} %quad.1), channel_id=1, source_target_pairs={{0,4},{4,0},{8,12},{12,8},{1,5},{5,1},{9,13},{13,9},{2,6},{6,2},{1... | collective-permute-start | bytes 196616 | tf_op jit(solution)/shard_map/tail/ppermute | solution.py:227
